TPU v7x, 128 devices: a whole 4x4x4 slice. The times are simulated.
128 devices in a mesh: tiles: 16 (over y, z), nests: 8 (over x, core).
Axes of the slice: x: 4, y: 4, z: 4, core: 2. Of those that a mesh axis runs over, the one named last changes fastest.
Arguments:
- parent: float32 [1024, 2048, 128], P('tiles', 'nests'), may hold values from -6 to 6
- nest_state: float32 [8, 64, 128, 128], P('nests', 'tiles'), may hold values from -6 to 6
- parent_mix: float32 [128, 128], replicated, may hold values from -0.24 to 0.24
- nest_mix: float32 [128, 128], replicated, may hold values from -0.24 to 0.24
- courant: float32 [2, 128], replicated, may hold values from 0.05 to 0.45
- nest_pos: int32 [8, 2], P('nests'), may hold values from 0 to 5954, as said below
Outputs:
- parent_out: float32 [1024, 2048, 128], P('tiles', 'nests')
- nest_out: float32 [8, 64, 128, 128], P('nests', 'tiles')
Inputs may be any that keep to these rules, and one draw needn't show every extreme that they name: nest_pos[n] = (3 i + a, 3 q + c) with a, c in 0..2, i <= 1001, and n * 256 <= q <= (n + 1) * 256 - 64: nest n reads and feeds only parent columns of the n-th group of 256 columns.
All inputs are finite; a program needn't handle non-finite values.
Results may differ from a plain program's by a relative error of at most 0.0003.
Values sent between devices are 32-bit elements; how exact they have to be, the bound alone decides.
No kernel may reach another device: no remote copies, remote signals or barrier semaphores. Data moves between devices by JAX's collectives and lax.ppermute only.
A program may use at most 128 MiB of HBM per device.

v0:
```python
import jax
import jax.numpy as jnp
from jax import lax
from jax.sharding import PartitionSpec as P

BLK = 64
STEPS = 3


KAPPA = 0.125
HIGH = lax.Precision.HIGHEST


def with_halo(block, sides, width):
    for axis, dim in sides:
        count = lax.axis_size(axis)
        forward = [(i, i + 1) for i in range(count - 1)]
        backward = [(target, source) for source, target in forward]
        low = lax.ppermute(
            lax.slice_in_dim(block, block.shape[dim] - width, None, axis=dim), axis, forward
        )
        high = lax.ppermute(lax.slice_in_dim(block, 0, width, axis=dim), axis, backward)
        block = jnp.concatenate([low, block, high], axis=dim)
    return block


def passed_along(block, axis, distance):
    devices = range(lax.axis_size(axis))
    route = [(i - distance, i) for i in devices if i - distance in devices]
    return lax.ppermute(block, axis, route)


def nest_advance(current, upper, edge, courant, nest_mix):
    left = jnp.concatenate([edge, current[:, :-1]], axis=1)
    mixed = jnp.einsum("xyc,cd->xyd", current, nest_mix, precision=HIGH)
    return current + courant[0] * (upper - current) + courant[1] * (left - current) + mixed


def bilinear(data, anchor, rows, columns_count, block_len):
    cols = jnp.arange(columns_count, dtype=jnp.int32)
    spot = anchor[1] + cols
    near = spot // 3 - anchor[1] // 3
    frac_y = (spot % 3).astype(jnp.float32) / 3.0
    places = jnp.arange(block_len, dtype=jnp.int32)[None, :]
    zero = jnp.zeros((columns_count, block_len), jnp.float32)
    table = jnp.where(places == near[:, None], (1.0 - frac_y)[:, None] + zero, zero)
    table = table + jnp.where(places == near[:, None] + 1, frac_y[:, None] + zero, zero)
    frac_x = ((anchor[0] + rows) % 3).astype(jnp.float32) / 3.0
    upper_part = jnp.einsum("nb,xbc->xnc", table, data[:, 0], precision=HIGH)
    lower_part = jnp.einsum("nb,xbc->xnc", table, data[:, 1], precision=HIGH)
    return (1.0 - frac_x)[:, None, None] * upper_part + frac_x[:, None, None] * lower_part


def shards(parent, nest_state, parent_mix, nest_mix, courant, nest_pos):
    tile_rows, tile_cols, width = parent.shape
    nest_rows = nest_state.shape[1]
    nest_cols = nest_state.shape[2]
    tiles_count = lax.axis_size("tiles")
    slots = (nest_rows + 1) // 3 + 2
    tile_index = lax.axis_index("tiles")
    column_index = lax.axis_index("nests")
    anchor = nest_pos[0]
    corner = anchor[1] // 3
    base = tile_index * nest_rows
    lowest = (anchor[0] + base) // 3
    strip = lax.dynamic_slice_in_dim(parent, corner - column_index * tile_cols, BLK, 1)
    receivers = jnp.arange(tiles_count, dtype=jnp.int32)
    wanted = ((anchor[0] + receivers * nest_rows) // 3)[:, None] + jnp.arange(
        slots, dtype=jnp.int32
    )[None, :]
    local = wanted - tile_index * tile_rows
    inside = (local >= 0) & (local < tile_rows)
    taken = strip[jnp.clip(local, 0, tile_rows - 1)]
    local_rows = lax.psum_scatter(
        jnp.where(inside[..., None, None], taken, 0.0), "tiles", scatter_dimension=0, tiled=True
    ).reshape(slots, BLK, width)
    padded = with_halo(parent, (("tiles", 0), ("nests", 1)), 1)
    beside_all = padded[2:, 1:-1] + padded[:-2, 1:-1] + padded[1:-1, 2:] + padded[1:-1, :-2]
    mixed = jnp.einsum("xyc,cd->xyd", parent, parent_mix, precision=HIGH)
    parent_new = parent + KAPPA * (beside_all - 4.0 * parent) + mixed
    rows = base + jnp.arange(nest_rows, dtype=jnp.int32)
    near_row = (anchor[0] + rows) // 3 - lowest
    data = jnp.stack([local_rows[near_row], local_rows[near_row + 1]], axis=1)
    interp = bilinear(data, anchor, rows, nest_cols, BLK)
    start = 0.5 * (nest_state[0] + interp)
    first = tile_index == 0
    edge = start[:, :1]
    current = start
    for step in range(STEPS):
        above = passed_along(current[-1:], "tiles", 1)
        above = jnp.where(first, start[:1], above)
        upper = jnp.concatenate([above, current[:-1]], axis=0)
        current = nest_advance(current, upper, edge, courant, nest_mix)
    fb_rows = (nest_rows + 2) // 3
    fb_cols = (nest_cols + 2) // 3
    counter = jnp.arange(fb_rows, dtype=jnp.int32)
    ys = -anchor[1] % 3 + 3 * jnp.arange(fb_cols, dtype=jnp.int32)
    col_live = ys < nest_cols
    xs = base + -(anchor[0] + base) % 3 + 3 * counter
    row_live = xs < base + nest_rows
    own_values = current[jnp.clip(xs - base, 0, nest_rows - 1)][:, jnp.clip(ys, 0, nest_cols - 1)]
    own_values = jnp.where((row_live[:, None] & col_live[None, :])[..., None], own_values, 0.0)
    pcol = (anchor[1] + ys) // 3 - column_index * tile_cols
    col_ok = col_live & (pcol >= 0) & (pcol < tile_cols)
    piece = lax.all_gather(own_values, "tiles", axis=0, tiled=True)
    slot_index = jnp.arange(piece.shape[0], dtype=jnp.int32)
    sender = slot_index // fb_rows
    sender_base = sender * nest_rows
    sender_x = sender_base + -(anchor[0] + sender_base) % 3 + 3 * (slot_index % fb_rows)
    prow = (anchor[0] + sender_x) // 3 - tile_index * tile_rows
    row_ok = (sender_x < sender_base + nest_rows) & (prow >= 0) & (prow < tile_rows)
    valid = row_ok[:, None] & col_ok[None, :]
    old = parent_new[
        jnp.clip(prow, 0, tile_rows - 1)[:, None], jnp.clip(pcol, 0, tile_cols - 1)[None, :]
    ]
    diff = jnp.where(valid[..., None], 0.5 * (piece - old), 0.0)
    row_index = jnp.where(valid, prow[:, None], tile_rows)
    col_index = jnp.broadcast_to(jnp.clip(pcol, 0, tile_cols - 1)[None, :], valid.shape)
    parent_out = parent_new.at[row_index, col_index].add(diff, mode="drop")
    return (parent_out, current[None])


def solution(mesh):
    placed = (
        P("tiles", "nests", None),
        P("nests", "tiles", None, None),
        P(),
        P(),
        P(),
        P("nests", None),
    )
    return jax.shard_map(
        shards,
        mesh=mesh,
        in_specs=placed,
        out_specs=(P("tiles", "nests", None), P("nests", "tiles", None, None)),
        check_vma=False,
    )
```

profile of v0, /device:TPU:1, one launch (start us, length us, event | category | flops | bytes accessed | tf_op | source)
XLA Modules:
  0.0 214.0 jit_solution(3485163505775321891)
XLA Ops:
  7.2 0.0 copy-start
  7.2 0.0 copy-start.6
  7.2 0.0 copy-start.5
  7.2 0.0 reduce-scatter.4.cloned.1.call-start
  7.3 1.0 fusion.71
  8.3 4.4 %collective-permute-start.1 = (f32[1,256,128]{2,1,0:T(8,128)S(1)}, f32[1,256,128]{2,1,0:T(8,128)S(1)}, u32[]{:S(2)}, u32[]{:S(2)}) collective-permute-start(f32[1,256,128]{2,1,0:T(8,128)S(1)} %get-tuple-element.13), channel_id=1, source_target_pairs={{0,8},{8,16},{16,24},{24,32},{32,40},{40,48},{48,56},{56,64},{64,7... | collective-permute-start | bytes 393224 | tf_op jit(solution)/shard_map/ppermute | solution.py:19
  12.6 1.3 collective-permute-start
  13.9 1.3 fusion.72
  17.9 0.7 and_select_fusion.3
  18.5 0.1 compare_select_fusion.1
  18.6 0.1 fusion.44
  18.7 2.0 constant_dynamic-slice_fusion
  20.7 0.1 reshape.533
  20.8 1.8 gather_fusion
  22.6 2.7 %broadcast_select_fusion = f32[16,3,64,128]{3,2,1,0:T(8,128)} fusion(f32[16,3,64,128]{3,2,1,0:T(8,128)} %bitcast.60, pred[16,3]{1,0:T(8,128)(4,1)S(1)} %fusion.44), kind=kLoop, calls=%fused_computation.28 | loop fusion | flops 393216 | bytes 3145776 | tf_op jit(solution)/shard_map/jit(_where)/select_n | solution.py:75
  25.3 0.0 reduce-scatter.4.cloned.1.call-update
  25.3 0.7 clamp_shift-left_fusion
  26.0 0.7 fusion.58
  26.7 0.7 compare_and_fusion
  28.0 0.7 broadcast_subtract_fusion.1
  28.7 0.7 fusion.52
  29.3 0.6 broadcast_add_fusion
  30.0 0.7 fusion.53
  30.8 0.7 compare_and_fusion.1
  31.5 0.1 compare_select_fusion
  31.5 0.1 multiply_reduce_fusion
  31.6 0.1 and_reduce_fusion
  31.7 0.1 broadcast_and_fusion.1
  31.8 0.1 broadcast_and_fusion
  31.9 0.1 broadcast_or_fusion
  32.0 0.1 reshape.577
  32.1 0.1 reshape.571
  32.2 0.7 constant_dynamic-update-slice_fusion.2
  32.9 7.7 %constant_dynamic-update-slice_fusion.1 = f32[66,256,128]{2,1,0:T(8,128)} fusion(f32[66,256,128]{2,1,0:T(8,128)} %constant_dynamic-update-slice_fusion.2, f32[64,256,128]{2,1,0:T(8,128)} %param.6), kind=kLoop, calls=%fused_computation.88 | loop fusion | bytes 16777216
  40.5 60.6 %reduce-scatter.4.cloned.1.call-done = f32[1,3,64,128]{3,2,1,0:T(8,128)} async-done(((f32[16,3,64,128]{3,2,1,0:T(8,128)}), f32[1,3,64,128]{3,2,1,0:T(8,128)}) %reduce-scatter.4.cloned.1.call-update) | async-done | bytes 98320
  101.1 1.4 gather_fusion.1
  102.5 1.4 gather_fusion.2
  104.0 0.4 convolution_multiply_fusion.1
  104.4 0.5 fusion.10
  104.9 2.4 %collective-permute-start.4 = (f32[1,128,128]{2,1,0:T(8,128)S(1)}, f32[1,128,128]{2,1,0:T(8,128)S(1)}, u32[]{:S(2)}, u32[]{:S(2)}) collective-permute-start(f32[1,128,128]{2,1,0:T(8,128)S(1)} %slice.129), channel_id=1, source_target_pairs={{0,8},{8,16},{16,24},{24,32},{32,40},{40,48},{48,56},{56,64},{64,7... | collective-permute-start | bytes 196616 | tf_op jit(solution)/shard_map/ppermute | solution.py:30
  107.3 0.0 collective-permute-done
  107.3 0.7 constant_dynamic-update-slice_fusion
  108.0 0.6 collective-permute-done.4
  108.6 0.4 convolution_add_fusion.2
  109.0 3.7 %collective-permute-start.5 = (f32[1,128,128]{2,1,0:T(8,128)S(1)}, f32[1,128,128]{2,1,0:T(8,128)S(1)}, u32[]{:S(2)}, u32[]{:S(2)}) collective-permute-start(f32[1,128,128]{2,1,0:T(8,128)S(1)} %slice.133), channel_id=1, source_target_pairs={{0,8},{8,16},{16,24},{24,32},{32,40},{40,48},{48,56},{56,64},{64,7... | collective-permute-start | bytes 196616 | tf_op jit(solution)/shard_map/ppermute | solution.py:30
  112.7 1.1 fusion.70
  113.8 7.1 %collective-permute-start.3 = (f32[66,1,128]{2,1,0:T(1,128)S(1)}, f32[66,1,128]{2,1,0:T(1,128)S(1)}, u32[]{:S(2)}, u32[]{:S(2)}) collective-permute-start(f32[66,1,128]{2,1,0:T(1,128)S(1)} %get-tuple-element.11), channel_id=1, source_target_pairs={{0,1},{1,2},{2,3},{3,4},{4,5},{5,6},{6,7},{8,9},{9,10},{10,11},{11... | collective-permute-start | bytes 101384 | tf_op jit(solution)/shard_map/ppermute | solution.py:19
  120.9 1.9 collective-permute-start.2
  122.9 0.0 collective-permute-done.5
  122.9 0.4 convolution_add_fusion.1
  123.3 3.0 %collective-permute-start.6 = (f32[1,128,128]{2,1,0:T(8,128)S(1)}, f32[1,128,128]{2,1,0:T(8,128)S(1)}, u32[]{:S(2)}, u32[]{:S(2)}) collective-permute-start(f32[1,128,128]{2,1,0:T(8,128)S(1)} %slice.136), channel_id=1, source_target_pairs={{0,8},{8,16},{16,24},{24,32},{32,40},{40,48},{48,56},{56,64},{64,7... | collective-permute-start | bytes 196616 | tf_op jit(solution)/shard_map/ppermute | solution.py:30
  126.3 27.0 %fusion.4 = f32[64,256,128]{2,1,0:T(8,128)} fusion(f32[64,256,128]{2,1,0:T(8,128)} %param.6, f32[66,256,128]{2,1,0:T(8,128)} %constant_dynamic-update-slice_fusion, f32[66,1,128]{2,1,0:T(1,128)S(1)} %collective-permute-done.3, f32[66,1,128]{2,1,0:T(1,128)S(1)} %collective-permute-done.2, f32[1,256,128]{2,1,0:T(8,128)S(1)} %collective-permute-done.1, ...), kind=kOutput, calls=%fused_computation.12 | convolution fusion | flops 3246391296 | bytes 25823232 | tf_op jit(solution)/shard_map/xyc,cd->xyd/dot_general | solution.py:79
  153.4 14.5 %gather_fusion.5 = f32[1376,128]{1,0:T(8,128)S(1)} fusion(f32[64,256,128]{2,1,0:T(8,128)} %fusion.4, s32[1376]{0:T(1024)S(1)} %reshape.571), kind=kCustom, calls=%fused_computation.5 | custom fusion | bytes 1420032 | tf_op jit(solution)/shard_map/gather | solution.py:113
  167.9 0.1 reshape.574
  168.0 0.4 convolution_add_fusion
  168.4 0.0 copy-start.2
  168.4 0.6 gather_fusion.3
  168.9 0.1 copy.11
  169.0 0.6 gather_fusion.4
  169.7 0.1 bitcast_select_fusion
  169.8 22.0 %all_gather.3 = f32[32,43,128]{2,1,0:T(8,128)S(1)} all-gather(f32[2,43,128]{2,1,0:T(8,128)S(1)} %copy.12), channel_id=1, replica_groups=mesh['tiles'=16,'nests'=8] {'tiles'}, dimensions={0}, use_global_device_ids=true | all-gather | bytes 748544 | tf_op jit(solution)/shard_map/all_gather | solution.py:105
  191.8 0.3 multiply_select_fusion
  192.1 0.1 reshape.579
  192.2 14.9 %scatter_fusion = f32[16384,128]{1,0:T(8,128)} fusion(f32[16384,128]{1,0:T(8,128)} %bitcast.58, s32[1376]{0:T(1024)S(1)} %reshape.577, f32[1376,128]{1,0:T(8,128)S(1)} %reshape.579), kind=kCustom, calls=%fused_computation.6 | custom fusion | flops 176128 | bytes 2119040
  (38 shorter events, 0.2 us)
Async XLA Ops:
  7.2 119.2 %copy-start = (f32[128,128]{1,0:T(8,128)S(1)}, f32[128,128]{1,0:T(8,128)}, u32[]{:S(2)}) copy-start(f32[128,128]{1,0:T(8,128)} %param.8) | copy-start | bytes 196612
  7.2 24.4 %copy-start.6 = (s32[2]{0:T(128)S(1)}, s32[2]{0:T(128)}, u32[]{:S(2)}) copy-start(s32[2]{0:T(128)} %constant.162) | copy-start | bytes 28
  7.2 24.4 %copy-start.5 = (s32[2]{0:T(128)S(1)}, s32[2]{0:T(128)}, u32[]{:S(2)}) copy-start(s32[2]{0:T(128)} %constant.165) | copy-start | bytes 28
  7.2 24.5 %copy-start.4 = (f32[2,128]{1,0:T(2,128)S(1)}, f32[2,128]{1,0:T(2,128)}, u32[]{:S(2)}) copy-start(f32[2,128]{1,0:T(2,128)} %param.10) | copy-start | bytes 3076
  7.2 93.9 %reduce-scatter.4.cloned.1.call-start = ((), (), s32[]{:S(2)}) async-start(), calls=%async_computation.1 | async-start | bytes 1671168
  8.3 23.9 %collective-permute-start.1 = (f32[1,256,128]{2,1,0:T(8,128)S(1)}, f32[1,256,128]{2,1,0:T(8,128)S(1)}, u32[]{:S(2)}, u32[]{:S(2)}) collective-permute-start(f32[1,256,128]{2,1,0:T(8,128)S(1)} %get-tuple-element.13), channel_id=1, source_target_pairs={{0,8},{8,16},{16,24},{24,32},{32,40},{40,48},{48,56},{56,64},{64,7... | collective-permute-start | bytes 393224 | tf_op jit(solution)/shard_map/ppermute | solution.py:19
  12.6 94.7 %collective-permute-start = (f32[1,256,128]{2,1,0:T(8,128)S(1)}, f32[1,256,128]{2,1,0:T(8,128)S(1)}, u32[]{:S(2)}, u32[]{:S(2)}) collective-permute-start(f32[1,256,128]{2,1,0:T(8,128)S(1)} %get-tuple-element.12), channel_id=1, source_target_pairs={{8,0},{16,8},{24,16},{32,24},{40,32},{48,40},{56,48},{64,56},{72,6... | collective-permute-start | bytes 393224 | tf_op jit(solution)/shard_map/ppermute | solution.py:22
  32.9 71.6 %copy-start.3 = (f32[1,4,128,128]{3,2,1,0:T(8,128)S(1)}, f32[1,4,128,128]{3,2,1,0:T(8,128)}, u32[]{:S(2)}) copy-start(f32[1,4,128,128]{3,2,1,0:T(8,128)} %param.7) | copy-start | bytes 786436
  32.9 75.8 %copy-start.1 = (f32[128,128]{1,0:T(8,128)S(1)}, f32[128,128]{1,0:T(8,128)}, u32[]{:S(2)}) copy-start(f32[128,128]{1,0:T(8,128)} %param.9) | copy-start | bytes 196612
  104.9 3.7 %collective-permute-start.4 = (f32[1,128,128]{2,1,0:T(8,128)S(1)}, f32[1,128,128]{2,1,0:T(8,128)S(1)}, u32[]{:S(2)}, u32[]{:S(2)}) collective-permute-start(f32[1,128,128]{2,1,0:T(8,128)S(1)} %slice.129), channel_id=1, source_target_pairs={{0,8},{8,16},{16,24},{24,32},{32,40},{40,48},{48,56},{56,64},{64,7... | collective-permute-start | bytes 196616 | tf_op jit(solution)/shard_map/ppermute | solution.py:30
  109.0 13.8 %collective-permute-start.5 = (f32[1,128,128]{2,1,0:T(8,128)S(1)}, f32[1,128,128]{2,1,0:T(8,128)S(1)}, u32[]{:S(2)}, u32[]{:S(2)}) collective-permute-start(f32[1,128,128]{2,1,0:T(8,128)S(1)} %slice.133), channel_id=1, source_target_pairs={{0,8},{8,16},{16,24},{24,32},{32,40},{40,48},{48,56},{56,64},{64,7... | collective-permute-start | bytes 196616 | tf_op jit(solution)/shard_map/ppermute | solution.py:30
  113.8 12.5 %collective-permute-start.3 = (f32[66,1,128]{2,1,0:T(1,128)S(1)}, f32[66,1,128]{2,1,0:T(1,128)S(1)}, u32[]{:S(2)}, u32[]{:S(2)}) collective-permute-start(f32[66,1,128]{2,1,0:T(1,128)S(1)} %get-tuple-element.11), channel_id=1, source_target_pairs={{0,1},{1,2},{2,3},{3,4},{4,5},{5,6},{6,7},{8,9},{9,10},{10,11},{11... | collective-permute-start | bytes 101384 | tf_op jit(solution)/shard_map/ppermute | solution.py:19
  120.9 5.4 %collective-permute-start.2 = (f32[66,1,128]{2,1,0:T(1,128)S(1)}, f32[66,1,128]{2,1,0:T(1,128)S(1)}, u32[]{:S(2)}, u32[]{:S(2)}) collective-permute-start(f32[66,1,128]{2,1,0:T(1,128)S(1)} %get-tuple-element.10), channel_id=1, source_target_pairs={{1,0},{2,1},{3,2},{4,3},{5,4},{6,5},{7,6},{9,8},{10,9},{11,10},{12... | collective-permute-start | bytes 101384 | tf_op jit(solution)/shard_map/ppermute | solution.py:22
  123.3 44.7 %collective-permute-start.6 = (f32[1,128,128]{2,1,0:T(8,128)S(1)}, f32[1,128,128]{2,1,0:T(8,128)S(1)}, u32[]{:S(2)}, u32[]{:S(2)}) collective-permute-start(f32[1,128,128]{2,1,0:T(8,128)S(1)} %slice.136), channel_id=1, source_target_pairs={{0,8},{8,16},{16,24},{24,32},{32,40},{40,48},{48,56},{56,64},{64,7... | collective-permute-start | bytes 196616 | tf_op jit(solution)/shard_map/ppermute | solution.py:30
  168.4 38.8 %copy-start.2 = (f32[4,128,128]{2,1,0:T(8,128)}, f32[4,128,128]{2,1,0:T(8,128)S(1)}, u32[]{:S(2)}) copy-start(f32[4,128,128]{2,1,0:T(8,128)S(1)} %convolution_add_fusion) | copy-start | bytes 786436
Sparse Core Ops, SparseCore 0:
  25.5 75.5 reduce-scatter.3
where the time goes:
time: 217 us; the launch traced here: 214 us
  waiting for transfers between devices  61.2 us (28%)
  local copies, waits for them, and re-layouts  35.4 us (16%)
  matrix products  29 us (13%)
  other arithmetic  24.7 us (11%)
  starting transfers between devices  23.8 us (11%)
  blocking collectives  22 us (10%)
  between operations  17.9 us (8%)
    unnamed x2, waiting for transfers between devices  60.6 us
    dot_general x1, matrix products, shards(): mixed = jnp.einsum('xyc,cd->xyd', parent, parent_mix, precision=HIGH)  27 us
    all_gather x1, blocking collectives, shards(): piece = lax.all_gather(own_values, 'tiles', axis=0, tiled=True)  22 us
    unnamed x4, other arithmetic  15.1 us
    gather x2, local copies, waits for them, and re-layouts, shards(): parent_new[jnp.clip(prow, 0, tile_rows - 1)[:, None], jnp.clip(pcol, 0, t...  14.5 us
    ppermute x2, starting transfers between devices, with_halo(): lax.ppermute(lax.slice_in_dim(block, block.shape[dim] - width, None, axis...  11.5 us
    ppermute x3, starting transfers between devices, passed_along(): return lax.ppermute(block, axis, route)  9.08 us
    unnamed x17, local copies, waits for them, and re-layouts  8.47 us
  transfers between devices with their start and end apart: 8, of which 2 were waited for; matrix products, arithmetic and copies ran while one was open for 33% of the time, Pallas kernels for 0%

commit v1 on v0

v1 whole, which is shorter than its diff:
```python
import functools

import jax
import jax.numpy as jnp
from jax import lax
from jax.experimental import pallas as pl
from jax.experimental.pallas import tpu as pltpu
from jax.sharding import PartitionSpec as P

STEPS = 3
KAPPA = 0.125
C = 48
WIDE = 56
SIDE = 4
GROUP_ROWS = 8
DEV_ROWS = 4
FB_SLOTS = 2
FB_GROUP = 6
FB_WINDOW = 22
F32 = jnp.float32
BF16 = jnp.bfloat16


def third(value):
    return lax.div(value, jnp.int32(3))


def wrap(value):
    return lax.rem(value + 2 * SIDE, jnp.int32(SIDE))


def split(value):
    high = value.astype(BF16)
    return high, (value - high.astype(F32)).astype(BF16)


def wide_weights(matrix):
    high, low = split(matrix)
    row = jnp.concatenate([high, low], axis=1)
    return jnp.concatenate([row, row], axis=0)


def mix(value, weights):
    lhs = jnp.concatenate(split(value), axis=1)
    both = jnp.dot(lhs, weights, preferred_element_type=F32)
    half = both.shape[1] // 2
    return both[:, :half] + both[:, half:]


def eye(size):
    shape = (size, size)
    return lax.broadcasted_iota(jnp.int32, shape, 0) == lax.broadcasted_iota(jnp.int32, shape, 1)


def owner_place(row, first, tile_rows):
    owner = lax.div(jnp.maximum(row, 0), jnp.int32(tile_rows))
    base = owner * tile_rows
    begin = jnp.clip(first - base, 0, tile_rows - GROUP_ROWS)
    return owner, jnp.clip(row - base - begin, 0, GROUP_ROWS - 1)


def pack_kernel(tile_rows, tile_cols, nest_rows, pos, parent, nest, b0, b1, b2, b3, west, east, down, up, band, cols, sems):
    tile = lax.axis_index("tiles")
    line = lax.axis_index("nests")
    my_y = lax.div(tile, jnp.int32(SIDE))
    corner = third(pos[0, 1]) - line * tile_cols
    aligned = pl.multiple_of(lax.div(corner, jnp.int32(8)) * 8, 8)
    shift = corner - aligned
    copies = []
    for k in range(SIDE):
        group = wrap(my_y + k)
        first = third(pos[0, 0] + SIDE * nest_rows * group) - 1
        begin = jnp.clip(first - tile * tile_rows, 0, tile_rows - GROUP_ROWS)
        copies.append(
            pltpu.make_async_copy(
                parent.at[pl.ds(begin, GROUP_ROWS), pl.ds(aligned, WIDE)], band.at[k], sems.at[k]
            )
        )
    halo = 3
    others = [
        pltpu.make_async_copy(parent.at[:, pl.ds(0, 8)], cols.at[0], sems.at[4]),
        pltpu.make_async_copy(parent.at[:, pl.ds(tile_cols - 8, 8)], cols.at[1], sems.at[5]),
        pltpu.make_async_copy(parent.at[tile_rows - 1], down.at[pl.ds(0, tile_cols)], sems.at[6]),
        pltpu.make_async_copy(parent.at[0], up, sems.at[7]),
    ]
    nest_cols = nest.shape[1]
    for r in range(halo):
        others.append(
            pltpu.make_async_copy(
                nest.at[nest_rows - halo + r],
                down.at[pl.ds(tile_cols + r * nest_cols, nest_cols)],
                sems.at[8 + r],
            )
        )
    for copy in copies + others:
        copy.start()
    for k, out in enumerate((b0, b1, b2, b3)):
        copies[k].wait()
        for r in range(GROUP_ROWS):
            out[r] = band[k, r, pl.ds(shift, C), :]
    others[0].wait()
    west[...] = cols[0, :, 0, :]
    others[1].wait()
    east[...] = cols[1, :, 7, :]
    for copy in others[2:]:
        copy.wait()


def pick_kernel(tile_rows, nest_rows, pos, r0, r1, r2, r3, o0, o1, o2, o3):
    tile = lax.axis_index("tiles")
    my_y, my_z = lax.div(tile, jnp.int32(SIDE)), lax.rem(tile, jnp.int32(SIDE))
    first = third(pos[0, 0] + SIDE * nest_rows * my_y) - 1
    for k, out in enumerate((o0, o1, o2, o3)):
        target = my_y * SIDE + wrap(my_z + k)
        top = third(pos[0, 0] + nest_rows * target) - 1
        for j in range(DEV_ROWS):
            owner, place = owner_place(top + j, first, tile_rows)
            way = wrap(my_y - lax.div(owner, jnp.int32(SIDE)))
            for source, ref in enumerate((r0, r1, r2, r3)):

                @pl.when(way == source)
                def _(out=out, j=j, ref=ref, place=place):
                    out[j] = ref[place]


def nest_kernel(tile_rows, tile_cols, pos, r0, r1, r2, r3, state, down, nest_mix, courant, out, fb, lines, start, cur):
    tile = lax.axis_index("tiles")
    my_y, my_z = lax.div(tile, jnp.int32(SIDE)), lax.rem(tile, jnp.int32(SIDE))
    nest_rows, ncols, width = state.shape
    halo = STEPS
    ox, oy = pos[0, 0], pos[0, 1]
    phase = lax.rem(oy, jnp.int32(3))
    top = third(ox + nest_rows * tile) - 1
    spot = lax.broadcasted_iota(jnp.int32, (ncols, C), 0) + phase
    near = third(spot)
    frac = spot - 3 * near
    place = lax.broadcasted_iota(jnp.int32, (ncols, C), 1)
    table = jnp.where(place == near, 3 - frac, jnp.where(place == near + 1, frac, 0))
    table = table.astype(F32).astype(BF16)
    for j in range(DEV_ROWS):
        owner = lax.div(jnp.maximum(top + j, 0), jnp.int32(tile_rows))
        way = wrap(my_z - lax.rem(owner, jnp.int32(SIDE)))
        row = jnp.where(way == 0, r0[j], jnp.where(way == 1, r1[j], jnp.where(way == 2, r2[j], r3[j])))
        high, low = split(row)
        lines[j] = jnp.dot(table, high, preferred_element_type=F32) + jnp.dot(
            table, low, preferred_element_type=F32
        )
    for x in range(-halo, nest_rows):
        at = ox + nest_rows * tile + x
        at = jnp.maximum(at, 0)
        near_row = jnp.clip(third(at) - top, 0, DEV_ROWS - 2)
        part = lax.rem(at, jnp.int32(3)).astype(F32)
        interp = (3.0 - part) * lines[near_row] + part * lines[near_row + 1]
        own = state[x] if x >= 0 else down[pl.ds(tile_cols + (x + halo) * ncols, ncols), :]
        start[x + halo] = 0.5 * (own + interp * (1.0 / 9.0))
    first = tile == 0

    @pl.when(first)
    def _():
        for x in range(halo):
            start[x] = start[halo]

    c0, c1 = courant[0:1, :], courant[1:2, :]
    weights = wide_weights(nest_mix[...] + jnp.where(eye(width), 1.0 - c0 - c1, 0.0))
    edge_row = lax.broadcasted_iota(jnp.int32, (ncols, width), 0) == 0
    source = start
    for step in range(STEPS):
        last = step == STEPS - 1
        for r in range(nest_rows + halo - 1, step, -1):
            value = source[r]
            left = jnp.where(edge_row, start[r, 0:1, :], pltpu.roll(value, 1, 0))
            value = mix(value, weights) + c0 * source[r - 1] + c1 * left
            if r < halo:
                value = jnp.where(first, start[halo], value)
            if last:
                out[r - halo] = value
            else:
                cur[step, r] = value
        source = cur.at[step]
    rem_y = lax.rem(3 - phase, jnp.int32(3))
    slot = lax.broadcasted_iota(jnp.int32, (C, ncols), 0)
    choose = (lax.broadcasted_iota(jnp.int32, (C, ncols), 1) == rem_y + 3 * slot).astype(F32).astype(BF16)
    x0 = lax.rem(3 * nest_rows * SIDE * SIDE - lax.rem(ox + nest_rows * tile, jnp.int32(3)), jnp.int32(3))
    for s in range(FB_SLOTS):
        high, low = split(out[jnp.minimum(x0 + 3 * s, nest_rows - 1)])
        fb[s] = jnp.dot(choose, high, preferred_element_type=F32) + jnp.dot(
            choose, low, preferred_element_type=F32
        )


def up_third(value):
    return third(value + 2)


def combine_kernel(nest_rows, pos, e0, e1, e2, e3, out):
    tile = lax.axis_index("tiles")
    my_y, my_z = lax.div(tile, jnp.int32(SIDE)), lax.rem(tile, jnp.int32(SIDE))
    ox = pos[0, 0]
    base = up_third(ox + SIDE * nest_rows * my_y)
    for r in range(FB_GROUP):
        out[r] = jnp.zeros(out.shape[1:], F32)
    for k, ref in enumerate((e0, e1, e2, e3)):
        origin = ox + nest_rows * (SIDE * my_y + wrap(my_z - k))
        row = up_third(origin)
        for s in range(FB_SLOTS):

            @pl.when(3 * (row + s) - origin < nest_rows)
            def _(ref=ref, row=row, s=s):
                out[row + s - base] = ref[s]


def patch_kernel(tile_rows, tile_cols, nest_rows, ncols, pos, parent, g0, g1, g2, g3, out, buf, sems):
    tile = lax.axis_index("tiles")
    line = lax.axis_index("nests")
    my_y = lax.div(tile, jnp.int32(SIDE))
    ox, oy = pos[0, 0], pos[0, 1]
    total = nest_rows * SIDE * SIDE
    low_row = up_third(ox)
    high_row = third(ox + total - 1)
    first_row = tile * tile_rows

    @pl.when((high_row >= first_row) & (low_row < first_row + tile_rows))
    def _():
        begin = jnp.clip(low_row - first_row, 0, tile_rows - FB_WINDOW)
        corner = up_third(oy) - line * tile_cols
        aligned = pl.multiple_of(lax.div(corner, jnp.int32(8)) * 8, 8)
        shift = corner - aligned
        rem_y = 3 * up_third(oy) - oy
        place = (pl.ds(begin, FB_WINDOW), pl.ds(aligned, WIDE))
        copy = pltpu.make_async_copy(parent.at[place], buf, sems.at[0])
        copy.start()
        copy.wait()
        live = rem_y + 3 * lax.broadcasted_iota(jnp.int32, (C, buf.shape[2]), 0) < ncols

        @pl.loop(0, FB_WINDOW)
        def _(j):
            row = first_row + begin + j
            x = 3 * row - ox

            @pl.when((x >= 0) & (x < total))
            def _():
                group = lax.div(x, jnp.int32(SIDE * nest_rows))
                way = wrap(my_y - group)
                r = row - up_third(ox + SIDE * nest_rows * group)
                value = jnp.where(way == 0, g0[r], jnp.where(way == 1, g1[r], jnp.where(way == 2, g2[r], g3[r])))
                old = buf[j, pl.ds(shift, C), :]
                buf[j, pl.ds(shift, C), :] = jnp.where(live, 0.5 * (old + value), old)

        back = pltpu.make_async_copy(buf, out.at[place], sems.at[1])
        back.start()
        back.wait()


def parent_kernel(rows, main, above, below, from_up, from_down, west, east, parent_mix, out, weights):
    step = pl.program_id(0)
    count = pl.num_programs(0)

    @pl.when(step == 0)
    def _():
        size = parent_mix.shape[0]
        weights[...] = wide_weights(parent_mix[...] + jnp.where(eye(size), 1.0 - 4.0 * KAPPA, 0.0))

    cols = main.shape[1]
    index = lax.broadcasted_iota(jnp.int32, main.shape[1:], 0)
    low_edge, high_edge = index == 0, index == cols - 1
    for r in range(rows):
        value = main[r]
        upper = jnp.where(step == 0, from_up[...], above[0]) if r == 0 else main[r - 1]
        lower = jnp.where(step == count - 1, from_down[...], below[0]) if r == rows - 1 else main[r + 1]
        left = jnp.where(low_edge, west[r : r + 1, :], pltpu.roll(value, 1, 0))
        right = jnp.where(high_edge, east[r : r + 1, :], pltpu.roll(value, cols - 1, 0))
        out[r] = mix(value, weights[...]) + KAPPA * ((upper + lower) + (left + right))


def smem():
    return pl.BlockSpec(memory_space=pltpu.SMEM)


def vmem():
    return pl.BlockSpec(memory_space=pltpu.VMEM)


def hbm():
    return pl.BlockSpec(memory_space=pl.ANY)


def send(block, axis, route):
    return lax.ppermute(block, axis, route)


def y_route(k):
    return [(t, (t + SIDE * k) % (SIDE * SIDE)) for t in range(SIDE * SIDE)]


def z_route(k):
    return [(t, t // SIDE * SIDE + (t + k) % SIDE) for t in range(SIDE * SIDE)]


def shards(parent, nest_state, parent_mix, nest_mix, courant, nest_pos):
    tile_rows, tile_cols, width = parent.shape
    state = nest_state[0]
    nest_rows, ncols, _ = state.shape
    f = lambda *shape: jax.ShapeDtypeStruct(shape, F32)
    limit = pltpu.CompilerParams(vmem_limit_bytes=40 << 20)

    band = [f(GROUP_ROWS, C, width)] * SIDE
    packed = pl.pallas_call(
        functools.partial(pack_kernel, tile_rows, tile_cols, nest_rows),
        out_shape=band
        + [f(tile_rows, width)] * 2
        + [f(tile_cols + STEPS * ncols, width), f(tile_cols, width)],
        in_specs=[smem(), hbm(), hbm()],
        out_specs=[vmem()] * 6 + [hbm()] * 2,
        scratch_shapes=[
            pltpu.VMEM((SIDE, GROUP_ROWS, WIDE, width), F32),
            pltpu.VMEM((2, tile_rows, 8, width), F32),
            pltpu.SemaphoreType.DMA((11,)),
        ],
        compiler_params=limit,
        name="pack",
    )(nest_pos, parent, state)
    b, (west_out, east_out, down_out, up_out) = packed[:4], packed[4:]
    got = [b[0]] + [send(b[k], "tiles", y_route(k)) for k in range(1, SIDE)]

    count = SIDE * SIDE
    forward = [(i, i + 1) for i in range(count - 1)]
    backward = [(i + 1, i) for i in range(count - 1)]
    lines = lax.axis_size("nests")
    from_down = send(up_out, "tiles", backward)
    from_up = send(down_out, "tiles", forward)
    west = send(east_out, "nests", [(i, i + 1) for i in range(lines - 1)])
    east = send(west_out, "nests", [(i + 1, i) for i in range(lines - 1)])

    picked = pl.pallas_call(
        functools.partial(pick_kernel, tile_rows, nest_rows),
        out_shape=[f(DEV_ROWS, C, width)] * SIDE,
        in_specs=[smem()] + [vmem()] * 4,
        out_specs=[vmem()] * 4,
        name="pick",
    )(nest_pos, *got)
    mine = [picked[0]] + [send(picked[k], "tiles", z_route(k)) for k in range(1, SIDE)]

    rows = 8
    blocks = tile_rows // rows
    whole = lambda *shape: pl.BlockSpec(shape, lambda i: (0,) * len(shape))
    parent_new = pl.pallas_call(
        functools.partial(parent_kernel, rows),
        out_shape=f(tile_rows, tile_cols, width),
        grid=(blocks,),
        in_specs=[
            pl.BlockSpec((rows, tile_cols, width), lambda i: (i, 0, 0)),
            pl.BlockSpec((1, tile_cols, width), lambda i: (jnp.maximum(i * rows - 1, 0), 0, 0)),
            pl.BlockSpec((1, tile_cols, width), lambda i: (jnp.minimum(i * rows + rows, tile_rows - 1), 0, 0)),
            whole(tile_cols, width),
            whole(tile_cols, width),
            pl.BlockSpec((rows, width), lambda i: (i, 0)),
            pl.BlockSpec((rows, width), lambda i: (i, 0)),
            whole(width, width),
        ],
        out_specs=pl.BlockSpec((rows, tile_cols, width), lambda i: (i, 0, 0)),
        scratch_shapes=[pltpu.VMEM((2 * width, 2 * width), BF16)],
        compiler_params=limit,
        cost_estimate=pl.CostEstimate(flops=2 * 16384 * 256 * 256, bytes_accessed=20 << 20, transcendentals=0),
        name="parent_step",
    )(parent, parent, parent, from_up, from_down, west, east, parent_mix)

    total_rows = nest_rows + STEPS
    nest_out, fed = pl.pallas_call(
        functools.partial(nest_kernel, tile_rows, tile_cols),
        out_shape=[f(nest_rows, ncols, width), f(FB_SLOTS, C, width)],
        in_specs=[smem()] + [vmem()] * 8,
        out_specs=[vmem()] * 2,
        scratch_shapes=[
            pltpu.VMEM((DEV_ROWS, ncols, width), F32),
            pltpu.VMEM((total_rows, ncols, width), F32),
            pltpu.VMEM((STEPS - 1, total_rows, ncols, width), F32),
        ],
        compiler_params=limit,
        name="nest_steps",
    )(nest_pos, *mine, state, from_up, nest_mix, courant)

    feeds = [fed] + [send(fed, "tiles", z_route(k)) for k in range(1, SIDE)]
    joined = pl.pallas_call(
        functools.partial(combine_kernel, nest_rows),
        out_shape=f(FB_GROUP, C, width),
        in_specs=[smem()] + [vmem()] * 4,
        out_specs=vmem(),
        name="combine",
    )(nest_pos, *feeds)
    groups = [joined] + [send(joined, "tiles", y_route(k)) for k in range(1, SIDE)]
    parent_out = pl.pallas_call(
        functools.partial(patch_kernel, tile_rows, tile_cols, nest_rows, ncols),
        out_shape=f(tile_rows, tile_cols, width),
        in_specs=[smem(), hbm()] + [vmem()] * 4,
        out_specs=hbm(),
        scratch_shapes=[pltpu.VMEM((FB_WINDOW, WIDE, width), F32), pltpu.SemaphoreType.DMA((2,))],
        input_output_aliases={1: 0},
        compiler_params=limit,
        name="patch",
    )(nest_pos, parent_new, *groups)
    return parent_out, nest_out[None]


def solution(mesh):
    placed = (
        P("tiles", "nests", None),
        P("nests", "tiles", None, None),
        P(),
        P(),
        P(),
        P("nests", None),
    )
    return jax.shard_map(
        shards,
        mesh=mesh,
        in_specs=placed,
        out_specs=(P("tiles", "nests", None), P("nests", "tiles", None, None)),
        check_vma=False,
    )
```

time: 217 us -> 75 us (0.35)
  waiting for transfers between devices: 61.2 us -> 10.5 us
  matrix products: 29 us -> 0 us
  other arithmetic: 24.7 us -> 0 us
  local copies, waits for them, and re-layouts: 35.4 us -> 11.9 us
  blocking collectives: 22 us -> 0 us
  Pallas kernels: 0 us -> 17.8 us
  between operations: 17.9 us -> 0.85 us
  starting transfers between devices: 23.8 us -> 32.7 us
    unnamed x2 -> x0, waiting for transfers between devices: 60.6 us -> none
    dot_general x6 -> x0, matrix products: 29 us -> none  [the longest x1 27 us: shards(): mixed = jnp.einsum('xyc,cd->xyd', parent, parent_mix, precision=HIGH)]
    all_gather x1 -> x0, blocking collectives: 22 us -> none  [shards(): piece = lax.all_gather(own_values, 'tiles', axis=0, tiled=True)]
    gather x8 -> x0, local copies, waits for them, and re-layouts: 20.5 us -> none  [the longest x2 14.5 us: shards(): parent_new[jnp.clip(prow, 0, tile_rows - 1)[:, None], jnp.clip(pcol, 0, t...]
    pallas_call x0 -> x6, Pallas kernels: none -> 17.8 us  [the longest x1 6.69 us: shards(): pl.pallas_call(functools.partial(parent_kernel, rows), out_shape=f(tile_r...]
    unnamed x4 -> x0, other arithmetic: 15.1 us -> none
    ppermute x7 -> x16, waiting for transfers between devices: 0.63 us -> 10.5 us  [send(): return lax.ppermute(block, axis, route)]
    ppermute x7 -> x16, starting transfers between devices: 23.8 us -> 32.7 us  [send(): return lax.ppermute(block, axis, route)]
  transfers between devices with their start and end apart: 8 -> 16, of which waited for: 2 -> 4; matrix products, arithmetic and copies ran while one was open for 33% -> 0% of each run, Pallas kernels for 0% -> 18%
where the time goes in v1:
time: 75 us; the launch traced here: 73.8 us
  starting transfers between devices  32.7 us (44%)
  Pallas kernels  17.8 us (24%)
  local copies, waits for them, and re-layouts  11.9 us (16%)
  waiting for transfers between devices  10.5 us (14%)
  between operations  0.85 us (1%)
    ppermute x16, starting transfers between devices, send(): return lax.ppermute(block, axis, route)  32.7 us
    unnamed x40, local copies, waits for them, and re-layouts  11.9 us
    ppermute x16, waiting for transfers between devices, send(): return lax.ppermute(block, axis, route)  10.5 us
    pallas_call x1, Pallas kernels, shards(): pl.pallas_call(functools.partial(parent_kernel, rows), out_shape=f(tile_r...  6.69 us
    pallas_call x1, Pallas kernels, shards(): pl.pallas_call(functools.partial(patch_kernel, tile_rows, tile_cols, nest...  3.19 us
    pallas_call x1, Pallas kernels, shards(): pl.pallas_call(functools.partial(pick_kernel, tile_rows, nest_rows), out_...  2.51 us
    pallas_call x1, Pallas kernels, shards(): pl.pallas_call(functools.partial(nest_kernel, tile_rows, tile_cols), out_...  2.19 us
    pallas_call x1, Pallas kernels, shards(): pl.pallas_call(functools.partial(combine_kernel, nest_rows), out_shape=f(...  1.64 us
  transfers between devices with their start and end apart: 16, of which 4 were waited for; matrix products, arithmetic and copies ran while one was open for 0% of the time, Pallas kernels for 18%

profile of v1, /device:TPU:1, one launch (start us, length us, event | category | flops | bytes accessed | tf_op | source)
XLA Modules:
  0.0 73.8 jit_solution(4578112364253964013)
XLA Ops:
  0.6 0.0 copy-start.11
  0.6 0.0 copy-start.13
  0.7 0.0 copy-start
  0.7 3.4 %copy-done = f32[64,256,128]{2,1,0:T(8,128)S(1)} copy-done((f32[64,256,128]{2,1,0:T(8,128)S(1)}, f32[64,256,128]{2,1,0:T(8,128)}, u32[]{:S(2)}) %copy-start) | copy-done | bytes 8388632
  4.0 0.9 %copy-done.2 = f32[1,4,128,128]{3,2,1,0:T(8,128)S(1)} copy-done((f32[1,4,128,128]{3,2,1,0:T(8,128)S(1)}, f32[1,4,128,128]{3,2,1,0:T(8,128)}, u32[]{:S(2)}) %copy-start.2) | copy-done | bytes 262168
  5.0 0.7 copy-done.10
  5.7 1.6 %pack.1 = (f32[8,48,128]{2,1,0:T(8,128)S(1)}, f32[8,48,128]{2,1,0:T(8,128)S(1)}, f32[8,48,128]{2,1,0:T(8,128)S(1)}, f32[8,48,128]{2,1,0:T(8,128)S(1)}, f32[64,12...) custom-call(s32[1,2]{1,0:T(1,128)S(1)} %copy-done.10, ...), custom_call_target="tpu_custom_call" | custom-call | tf_op jit(solution)/shard_map/pack/pallas_call | solution.py:307
  7.3 0.0 copy-start.5
  7.3 0.7 copy-done.5
  8.0 4.4 %collective-permute-start = (f32[640,128]{1,0:T(8,128)S(1)}, f32[640,128]{1,0:T(8,128)S(1)}, u32[]{:S(2)}, u32[]{:S(2)}) collective-permute-start(f32[640,128]{1,0:T(8,128)S(1)} %get-tuple-element.16), channel_id=1, source_target_pairs={{0,8},{8,16},{16,24},{24,32},{32,40},{40,48},{48,56},{56,64},{64,7... | collective-permute-start | bytes 983048 | tf_op jit(solution)/shard_map/ppermute | solution.py:288
  12.3 1.3 %collective-permute-start.4 = (f32[8,48,128]{2,1,0:T(8,128)S(1)}, f32[8,48,128]{2,1,0:T(8,128)S(1)}, u32[]{:S(2)}, u32[]{:S(2)}) collective-permute-start(f32[8,48,128]{2,1,0:T(8,128)S(1)} %get-tuple-element.21), channel_id=1, source_target_pairs={{0,32},{8,40},{16,48},{24,56},{32,64},{40,72},{48,80},{56,88},{64,... | collective-permute-start | bytes 589832 | tf_op jit(solution)/shard_map/ppermute | solution.py:288
  13.7 2.6 %collective-permute-start.5 = (f32[8,48,128]{2,1,0:T(8,128)S(1)}, f32[8,48,128]{2,1,0:T(8,128)S(1)}, u32[]{:S(2)}, u32[]{:S(2)}) collective-permute-start(f32[8,48,128]{2,1,0:T(8,128)S(1)} %get-tuple-element.22), channel_id=1, source_target_pairs={{0,64},{8,72},{16,80},{24,88},{32,96},{40,104},{48,112},{56,120},{... | collective-permute-start | bytes 589832 | tf_op jit(solution)/shard_map/ppermute | solution.py:288
  16.3 1.1 %collective-permute-start.6 = (f32[8,48,128]{2,1,0:T(8,128)S(1)}, f32[8,48,128]{2,1,0:T(8,128)S(1)}, u32[]{:S(2)}, u32[]{:S(2)}) collective-permute-start(f32[8,48,128]{2,1,0:T(8,128)S(1)} %get-tuple-element.23), channel_id=1, source_target_pairs={{0,96},{8,104},{16,112},{24,120},{32,0},{40,8},{48,16},{56,24},{64... | collective-permute-start | bytes 589832 | tf_op jit(solution)/shard_map/ppermute | solution.py:288
  17.4 1.8 %collective-permute-done.4.r1 = f32[8,48,128]{2,1,0:T(8,128)S(1)} collective-permute-done((f32[8,48,128]{2,1,0:T(8,128)S(1)}, f32[8,48,128]{2,1,0:T(8,128)S(1)}, u32[]{:S(2)}, u32[]{:S(2)}) %collective-permute-start.4) | collective-permute-done | bytes 196640 | tf_op jit(solution)/shard_map/ppermute | solution.py:288
  19.2 5.3 %collective-permute-done.5.r2 = f32[8,48,128]{2,1,0:T(8,128)S(1)} collective-permute-done((f32[8,48,128]{2,1,0:T(8,128)S(1)}, f32[8,48,128]{2,1,0:T(8,128)S(1)}, u32[]{:S(2)}, u32[]{:S(2)}) %collective-permute-start.5) | collective-permute-done | bytes 196640 | tf_op jit(solution)/shard_map/ppermute | solution.py:288
  24.5 0.0 collective-permute-done.6.r3
  24.5 0.0 copy-done.14
  24.5 0.7 copy-done.15
  25.2 0.1 copy-done.16
  25.3 2.5 %pick.1 = (f32[4,48,128]{2,1,0:T(8,128)}, f32[4,48,128]{2,1,0:T(8,128)}, f32[4,48,128]{2,1,0:T(8,128)}, f32[4,48,128]{2,1,0:T(8,128)}) custom-call(s32[1,2]{1,0:T(1,128)} %pos.9, f32[8,48,128]{2,1,0:T(8,128)} %copy-done.5, f32[8,48,128]{2,1,0:T(8,128)} %copy-done.14, f32[8,48,128]{2,1,0:T(8,128)} %copy-done.15, f32[8,48,128]{2,1,0:T(8,128)} %copy-done.16), custom_call_target="tpu_custom_call" | custom-call | tf_op jit(solution)/shard_map/pick/pallas_call | solution.py:334
  27.8 1.6 %collective-permute-start.7 = (f32[4,48,128]{2,1,0:T(8,128)}, f32[4,48,128]{2,1,0:T(8,128)S(1)}, u32[]{:S(2)}, u32[]{:S(2)}) collective-permute-start(f32[4,48,128]{2,1,0:T(8,128)} %get-tuple-element.25), channel_id=1, source_target_pairs={{0,8},{8,16},{16,24},{24,0},{32,40},{40,48},{48,56},{56,32},{64,72... | collective-permute-start | bytes 294920 | tf_op jit(solution)/shard_map/ppermute | solution.py:288
  29.4 8.2 %collective-permute-start.8 = (f32[4,48,128]{2,1,0:T(8,128)}, f32[4,48,128]{2,1,0:T(8,128)S(1)}, u32[]{:S(2)}, u32[]{:S(2)}) collective-permute-start(f32[4,48,128]{2,1,0:T(8,128)} %get-tuple-element.26), channel_id=1, source_target_pairs={{0,16},{8,24},{16,0},{24,8},{32,48},{40,56},{48,32},{56,40},{64,80... | collective-permute-start | bytes 294920 | tf_op jit(solution)/shard_map/ppermute | solution.py:288
  37.7 0.0 collective-permute-start.9
  37.7 1.3 %collective-permute-start.1 = (f32[256,128]{1,0:T(8,128)S(1)}, f32[256,128]{1,0:T(8,128)S(1)}, u32[]{:S(2)}, u32[]{:S(2)}) collective-permute-start(f32[256,128]{1,0:T(8,128)S(1)} %get-tuple-element.17), channel_id=1, source_target_pairs={{8,0},{16,8},{24,16},{32,24},{40,32},{48,40},{56,48},{64,56},{72,6... | collective-permute-start | bytes 393224 | tf_op jit(solution)/shard_map/ppermute | solution.py:288
  39.0 0.0 collective-permute-done.7.r1
  39.0 2.3 %collective-permute-done.8.r2 = f32[4,48,128]{2,1,0:T(8,128)S(1)} collective-permute-done((f32[4,48,128]{2,1,0:T(8,128)}, f32[4,48,128]{2,1,0:T(8,128)S(1)}, u32[]{:S(2)}, u32[]{:S(2)}) %collective-permute-start.8) | collective-permute-done | bytes 98336 | tf_op jit(solution)/shard_map/ppermute | solution.py:288
  41.3 1.1 %collective-permute-done.9.r3 = f32[4,48,128]{2,1,0:T(8,128)S(1)} collective-permute-done((f32[4,48,128]{2,1,0:T(8,128)}, f32[4,48,128]{2,1,0:T(8,128)S(1)}, u32[]{:S(2)}, u32[]{:S(2)}) %collective-permute-start.9) | collective-permute-done | bytes 98336 | tf_op jit(solution)/shard_map/ppermute | solution.py:288
  42.4 0.0 collective-permute-done.from_up.down
  42.4 0.0 copy-done.11
  42.4 0.0 copy-done.13
  42.4 0.0 copy-done.3
  42.4 0.0 copy-done.8
  42.4 0.0 copy-start.6
  42.4 0.9 %copy-done.6 = f32[4,48,128]{2,1,0:T(8,128)S(1)} copy-done((f32[4,48,128]{2,1,0:T(8,128)S(1)}, f32[4,48,128]{2,1,0:T(8,128)}, u32[]{:S(2)}) %copy-start.6) | copy-done | bytes 98328
  43.3 2.2 %nest_steps.1 = (f32[4,128,128]{2,1,0:T(8,128)}, f32[2,48,128]{2,1,0:T(8,128)S(1)}) custom-call(s32[1,2]{1,0:T(1,128)S(1)} %copy-done.11, f32[4,48,128]{2,1,0:T(8,128)S(1)} %copy-done.6, f32[4,48,128]{2,1,0:T(8,128)S(1)} %collective-permute-done.7.r1, f32[4,48,128]{2,1,0:T(8,128)S(1)} %collective-permute-done.8.r2, ...), custom_call_target="tpu_custom_call" | custom-call | tf_op jit(solution)/shard_map/nest_steps/pallas_call | solution.py:368
  45.5 1.4 %collective-permute-start.12 = (f32[2,48,128]{2,1,0:T(8,128)S(1)}, f32[2,48,128]{2,1,0:T(8,128)S(1)}, u32[]{:S(2)}, u32[]{:S(2)}) collective-permute-start(f32[2,48,128]{2,1,0:T(8,128)S(1)} %get-tuple-element.28.e0), channel_id=1, source_target_pairs={{0,24},{8,0},{16,8},{24,16},{32,56},{40,32},{48,40},{56,48},{64,88... | collective-permute-start | bytes 147464 | tf_op jit(solution)/shard_map/ppermute | solution.py:288
  46.9 0.0 collective-permute-start.11
  47.0 0.5 collective-permute-start.10
  47.5 6.7 %collective-permute-start.2 = (f32[64,128]{1,0:T(8,128)S(1)}, f32[64,128]{1,0:T(8,128)S(1)}, u32[]{:S(2)}, u32[]{:S(2)}) collective-permute-start(f32[64,128]{1,0:T(8,128)S(1)} %get-tuple-element.18), channel_id=1, source_target_pairs={{0,1},{1,2},{2,3},{3,4},{4,5},{5,6},{6,7},{8,9},{9,10},{10,11},{11... | collective-permute-start | bytes 98312 | tf_op jit(solution)/shard_map/ppermute | solution.py:288
  54.2 0.0 collective-permute-done.12.e3
  54.2 0.0 copy-start.17
  54.2 1.9 %collective-permute-start.3 = (f32[64,128]{1,0:T(8,128)S(1)}, f32[64,128]{1,0:T(8,128)S(1)}, u32[]{:S(2)}, u32[]{:S(2)}) collective-permute-start(f32[64,128]{1,0:T(8,128)S(1)} %get-tuple-element.19), channel_id=1, source_target_pairs={{1,0},{2,1},{3,2},{4,3},{5,4},{6,5},{7,6},{9,8},{10,9},{11,10},{12... | collective-permute-start | bytes 98312 | tf_op jit(solution)/shard_map/ppermute | solution.py:288
  56.2 0.0 collective-permute-done.11.e2
  56.2 0.0 copy-start.18
  56.2 0.0 collective-permute-done.10.e1
  56.2 0.0 copy-done.9
  56.2 0.0 copy-done.17
  56.2 0.6 copy-done.18
  56.8 0.6 copy-done.19
  57.4 1.6 %combine.1.g0 = f32[6,48,128]{2,1,0:T(8,128)} custom-call(s32[1,2]{1,0:T(1,128)} %pos.9, f32[2,48,128]{2,1,0:T(8,128)} %copy-done.9, f32[2,48,128]{2,1,0:T(8,128)} %copy-done.19, f32[2,48,128]{2,1,0:T(8,128)} %copy-done.18, f32[2,48,128]{2,1,0:T(8,128)} %copy-done.17), custom_call_target="tpu_custom_call" | custom-call | tf_op jit(solution)/shard_map/combine/pallas_call | solution.py:383
  59.0 0.0 collective-permute-start.15
  59.0 0.4 collective-permute-start.14
  59.4 0.0 collective-permute-done.2.west
  59.4 1.1 %collective-permute-start.13 = (f32[6,48,128]{2,1,0:T(8,128)}, f32[6,48,128]{2,1,0:T(8,128)S(1)}, u32[]{:S(2)}, u32[]{:S(2)}) collective-permute-start(f32[6,48,128]{2,1,0:T(8,128)} %combine.1.g0), channel_id=1, source_target_pairs={{0,32},{8,40},{16,48},{24,56},{32,64},{40,72},{48,80},{56,88},{64,... | collective-permute-start | bytes 442376 | tf_op jit(solution)/shard_map/ppermute | solution.py:288
  60.5 0.0 collective-permute-done.3.east
  60.5 0.0 collective-permute-done.1.from_down
  60.5 0.0 copy-done.7
  60.5 0.0 copy-start.1
  60.5 3.4 %copy-done.1 = f32[64,256,128]{2,1,0:T(8,128)S(1)} copy-done((f32[64,256,128]{2,1,0:T(8,128)S(1)}, f32[64,256,128]{2,1,0:T(8,128)}, u32[]{:S(2)}) %copy-start.1) | copy-done | bytes 8388632
  63.9 6.7 %parent_step.1.parent = f32[64,256,128]{2,1,0:T(8,128)} custom-call(f32[64,256,128]{2,1,0:T(8,128)S(1)} %copy-done.1, f32[64,256,128]{2,1,0:T(8,128)S(1)} %copy-done.1, f32[64,256,128]{2,1,0:T(8,128)S(1)} %copy-done.1, f32[640,128]{1,0:T(8,128)S(1)} %collective-permute-done.from_up.down, f32[256,128]{1,0:T(8,128)S(1)} %collective-permute-done.1.from_down, ...), custom_call_target="tpu_custom_call" | custom-call | flops 2147483648 | bytes 20971520 | tf_op jit(solution)/shard_map/parent_step/pallas_call | solution.py:346
  70.6 0.0 collective-permute-done.15.g3
  70.6 0.0 collective-permute-done.14.g2
  70.6 0.0 collective-permute-done.13.g1
  70.6 3.2 %patch.1 = f32[64,256,128]{2,1,0:T(8,128)} custom-call(s32[1,2]{1,0:T(1,128)S(1)} %copy-done.12, f32[64,256,128]{2,1,0:T(8,128)} %parent_step.1.parent, f32[6,48,128]{2,1,0:T(8,128)S(1)} %copy-done.4, f32[6,48,128]{2,1,0:T(8,128)S(1)} %collective-permute-done.13.g1, f32[6,48,128]{2,1,0:T(8,128)S(1)} %collective-permute-done.14.g2, ...), custom_call_target="tpu_custom_call", output_to_operand_aliasing={{}: (1, {})} | custom-call | tf_op jit(solution)/shard_map/patch/pallas_call | solution.py:391
  (14 shorter events, 0.0 us)
Async XLA Ops:
  0.6 41.7 %copy-start.11 = (s32[1,2]{1,0:T(1,128)S(1)}, s32[1,2]{1,0:T(1,128)}, u32[]{:S(2)}) copy-start(s32[1,2]{1,0:T(1,128)} %pos.9) | copy-start | bytes 28
  0.6 41.7 %copy-start.13 = (f32[2,128]{1,0:T(2,128)S(1)}, f32[2,128]{1,0:T(2,128)}, u32[]{:S(2)}) copy-start(f32[2,128]{1,0:T(2,128)} %courant.1) | copy-start | bytes 3076
  0.7 3.4 %copy-start = (f32[64,256,128]{2,1,0:T(8,128)S(1)}, f32[64,256,128]{2,1,0:T(8,128)}, u32[]{:S(2)}) copy-start(f32[64,256,128]{2,1,0:T(8,128)} %below.1) | copy-start | bytes 25165828
  4.0 0.9 %copy-start.2 = (f32[1,4,128,128]{3,2,1,0:T(8,128)S(1)}, f32[1,4,128,128]{3,2,1,0:T(8,128)}, u32[]{:S(2)}) copy-start(f32[1,4,128,128]{3,2,1,0:T(8,128)} %param.7) | copy-start | bytes 786436
  5.0 0.7 copy-start.10
  5.7 36.7 %copy-start.3 = (f32[1,4,128,128]{3,2,1,0:T(8,128)S(1)}, f32[1,4,128,128]{3,2,1,0:T(8,128)}, u32[]{:S(2)}) copy-start(f32[1,4,128,128]{3,2,1,0:T(8,128)} %param.7) | copy-start | bytes 786436
  5.7 36.7 %copy-start.8 = (f32[128,128]{1,0:T(8,128)S(1)}, f32[128,128]{1,0:T(8,128)}, u32[]{:S(2)}) copy-start(f32[128,128]{1,0:T(8,128)} %nest_mix.1) | copy-start | bytes 196612
  5.7 54.9 %copy-start.7 = (f32[128,128]{1,0:T(8,128)S(1)}, f32[128,128]{1,0:T(8,128)}, u32[]{:S(2)}) copy-start(f32[128,128]{1,0:T(8,128)} %parent_mix.1) | copy-start | bytes 196612
  7.3 0.7 copy-start.5
  8.0 34.4 %collective-permute-start = (f32[640,128]{1,0:T(8,128)S(1)}, f32[640,128]{1,0:T(8,128)S(1)}, u32[]{:S(2)}, u32[]{:S(2)}) collective-permute-start(f32[640,128]{1,0:T(8,128)S(1)} %get-tuple-element.16), channel_id=1, source_target_pairs={{0,8},{8,16},{16,24},{24,32},{32,40},{40,48},{48,56},{56,64},{64,7... | collective-permute-start | bytes 983048 | tf_op jit(solution)/shard_map/ppermute | solution.py:288
  12.3 6.8 %collective-permute-start.4 = (f32[8,48,128]{2,1,0:T(8,128)S(1)}, f32[8,48,128]{2,1,0:T(8,128)S(1)}, u32[]{:S(2)}, u32[]{:S(2)}) collective-permute-start(f32[8,48,128]{2,1,0:T(8,128)S(1)} %get-tuple-element.21), channel_id=1, source_target_pairs={{0,32},{8,40},{16,48},{24,56},{32,64},{40,72},{48,80},{56,88},{64,... | collective-permute-start | bytes 589832 | tf_op jit(solution)/shard_map/ppermute | solution.py:288
  13.7 10.8 %collective-permute-start.5 = (f32[8,48,128]{2,1,0:T(8,128)S(1)}, f32[8,48,128]{2,1,0:T(8,128)S(1)}, u32[]{:S(2)}, u32[]{:S(2)}) collective-permute-start(f32[8,48,128]{2,1,0:T(8,128)S(1)} %get-tuple-element.22), channel_id=1, source_target_pairs={{0,64},{8,72},{16,80},{24,88},{32,96},{40,104},{48,112},{56,120},{... | collective-permute-start | bytes 589832 | tf_op jit(solution)/shard_map/ppermute | solution.py:288
  16.3 8.2 %collective-permute-start.6 = (f32[8,48,128]{2,1,0:T(8,128)S(1)}, f32[8,48,128]{2,1,0:T(8,128)S(1)}, u32[]{:S(2)}, u32[]{:S(2)}) collective-permute-start(f32[8,48,128]{2,1,0:T(8,128)S(1)} %get-tuple-element.23), channel_id=1, source_target_pairs={{0,96},{8,104},{16,112},{24,120},{32,0},{40,8},{48,16},{56,24},{64... | collective-permute-start | bytes 589832 | tf_op jit(solution)/shard_map/ppermute | solution.py:288
  19.2 5.3 %copy-start.14 = (f32[8,48,128]{2,1,0:T(8,128)}, f32[8,48,128]{2,1,0:T(8,128)S(1)}, u32[]{:S(2)}) copy-start(f32[8,48,128]{2,1,0:T(8,128)S(1)} %collective-permute-done.4.r1) | copy-start | bytes 589828
  24.5 0.7 copy-start.15
  24.5 0.8 %copy-start.16 = (f32[8,48,128]{2,1,0:T(8,128)}, f32[8,48,128]{2,1,0:T(8,128)S(1)}, u32[]{:S(2)}) copy-start(f32[8,48,128]{2,1,0:T(8,128)S(1)} %collective-permute-done.6.r3) | copy-start | bytes 589828
  27.8 11.2 %collective-permute-start.7 = (f32[4,48,128]{2,1,0:T(8,128)}, f32[4,48,128]{2,1,0:T(8,128)S(1)}, u32[]{:S(2)}, u32[]{:S(2)}) collective-permute-start(f32[4,48,128]{2,1,0:T(8,128)} %get-tuple-element.25), channel_id=1, source_target_pairs={{0,8},{8,16},{16,24},{24,0},{32,40},{40,48},{48,56},{56,32},{64,72... | collective-permute-start | bytes 294920 | tf_op jit(solution)/shard_map/ppermute | solution.py:288
  29.4 11.9 %collective-permute-start.8 = (f32[4,48,128]{2,1,0:T(8,128)}, f32[4,48,128]{2,1,0:T(8,128)S(1)}, u32[]{:S(2)}, u32[]{:S(2)}) collective-permute-start(f32[4,48,128]{2,1,0:T(8,128)} %get-tuple-element.26), channel_id=1, source_target_pairs={{0,16},{8,24},{16,0},{24,8},{32,48},{40,56},{48,32},{56,40},{64,80... | collective-permute-start | bytes 294920 | tf_op jit(solution)/shard_map/ppermute | solution.py:288
  37.7 4.7 %collective-permute-start.9 = (f32[4,48,128]{2,1,0:T(8,128)}, f32[4,48,128]{2,1,0:T(8,128)S(1)}, u32[]{:S(2)}, u32[]{:S(2)}) collective-permute-start(f32[4,48,128]{2,1,0:T(8,128)} %get-tuple-element.27), channel_id=1, source_target_pairs={{0,24},{8,0},{16,8},{24,16},{32,56},{40,32},{48,40},{56,48},{64,88... | collective-permute-start | bytes 294920 | tf_op jit(solution)/shard_map/ppermute | solution.py:288
  37.7 22.8 %collective-permute-start.1 = (f32[256,128]{1,0:T(8,128)S(1)}, f32[256,128]{1,0:T(8,128)S(1)}, u32[]{:S(2)}, u32[]{:S(2)}) collective-permute-start(f32[256,128]{1,0:T(8,128)S(1)} %get-tuple-element.17), channel_id=1, source_target_pairs={{8,0},{16,8},{24,16},{32,24},{40,32},{48,40},{56,48},{64,56},{72,6... | collective-permute-start | bytes 393224 | tf_op jit(solution)/shard_map/ppermute | solution.py:288
  42.4 0.9 %copy-start.6 = (f32[4,48,128]{2,1,0:T(8,128)S(1)}, f32[4,48,128]{2,1,0:T(8,128)}, u32[]{:S(2)}) copy-start(f32[4,48,128]{2,1,0:T(8,128)} %get-tuple-element.24.r0) | copy-start | bytes 294916
  45.5 10.7 %copy-start.9 = (f32[2,48,128]{2,1,0:T(8,128)}, f32[2,48,128]{2,1,0:T(8,128)S(1)}, u32[]{:S(2)}) copy-start(f32[2,48,128]{2,1,0:T(8,128)S(1)} %get-tuple-element.28.e0) | copy-start | bytes 147460
  45.5 8.7 %collective-permute-start.12 = (f32[2,48,128]{2,1,0:T(8,128)S(1)}, f32[2,48,128]{2,1,0:T(8,128)S(1)}, u32[]{:S(2)}, u32[]{:S(2)}) collective-permute-start(f32[2,48,128]{2,1,0:T(8,128)S(1)} %get-tuple-element.28.e0), channel_id=1, source_target_pairs={{0,24},{8,0},{16,8},{24,16},{32,56},{40,32},{48,40},{56,48},{64,88... | collective-permute-start | bytes 147464 | tf_op jit(solution)/shard_map/ppermute | solution.py:288
  46.9 9.2 %collective-permute-start.11 = (f32[2,48,128]{2,1,0:T(8,128)S(1)}, f32[2,48,128]{2,1,0:T(8,128)S(1)}, u32[]{:S(2)}, u32[]{:S(2)}) collective-permute-start(f32[2,48,128]{2,1,0:T(8,128)S(1)} %get-tuple-element.28.e0), channel_id=1, source_target_pairs={{0,16},{8,24},{16,0},{24,8},{32,48},{40,56},{48,32},{56,40},{64,80... | collective-permute-start | bytes 147464 | tf_op jit(solution)/shard_map/ppermute | solution.py:288
  47.0 9.2 %collective-permute-start.10 = (f32[2,48,128]{2,1,0:T(8,128)S(1)}, f32[2,48,128]{2,1,0:T(8,128)S(1)}, u32[]{:S(2)}, u32[]{:S(2)}) collective-permute-start(f32[2,48,128]{2,1,0:T(8,128)S(1)} %get-tuple-element.28.e0), channel_id=1, source_target_pairs={{0,8},{8,16},{16,24},{24,0},{32,40},{40,48},{48,56},{56,32},{64,72... | collective-permute-start | bytes 147464 | tf_op jit(solution)/shard_map/ppermute | solution.py:288
  47.5 11.9 %collective-permute-start.2 = (f32[64,128]{1,0:T(8,128)S(1)}, f32[64,128]{1,0:T(8,128)S(1)}, u32[]{:S(2)}, u32[]{:S(2)}) collective-permute-start(f32[64,128]{1,0:T(8,128)S(1)} %get-tuple-element.18), channel_id=1, source_target_pairs={{0,1},{1,2},{2,3},{3,4},{4,5},{5,6},{6,7},{8,9},{9,10},{10,11},{11... | collective-permute-start | bytes 98312 | tf_op jit(solution)/shard_map/ppermute | solution.py:288
  54.2 2.0 %copy-start.17 = (f32[2,48,128]{2,1,0:T(8,128)}, f32[2,48,128]{2,1,0:T(8,128)S(1)}, u32[]{:S(2)}) copy-start(f32[2,48,128]{2,1,0:T(8,128)S(1)} %collective-permute-done.12.e3) | copy-start | bytes 147460
  54.2 6.3 %collective-permute-start.3 = (f32[64,128]{1,0:T(8,128)S(1)}, f32[64,128]{1,0:T(8,128)S(1)}, u32[]{:S(2)}, u32[]{:S(2)}) collective-permute-start(f32[64,128]{1,0:T(8,128)S(1)} %get-tuple-element.19), channel_id=1, source_target_pairs={{1,0},{2,1},{3,2},{4,3},{5,4},{6,5},{7,6},{9,8},{10,9},{11,10},{12... | collective-permute-start | bytes 98312 | tf_op jit(solution)/shard_map/ppermute | solution.py:288
  56.2 0.6 copy-start.18
  56.8 0.6 copy-start.19
  57.4 13.2 %copy-start.12 = (s32[1,2]{1,0:T(1,128)S(1)}, s32[1,2]{1,0:T(1,128)}, u32[]{:S(2)}) copy-start(s32[1,2]{1,0:T(1,128)} %pos.9) | copy-start | bytes 28
  59.0 11.6 %collective-permute-start.15 = (f32[6,48,128]{2,1,0:T(8,128)}, f32[6,48,128]{2,1,0:T(8,128)S(1)}, u32[]{:S(2)}, u32[]{:S(2)}) collective-permute-start(f32[6,48,128]{2,1,0:T(8,128)} %combine.1.g0), channel_id=1, source_target_pairs={{0,96},{8,104},{16,112},{24,120},{32,0},{40,8},{48,16},{56,24},{64... | collective-permute-start | bytes 442376 | tf_op jit(solution)/shard_map/ppermute | solution.py:288
  59.0 11.6 %collective-permute-start.14 = (f32[6,48,128]{2,1,0:T(8,128)}, f32[6,48,128]{2,1,0:T(8,128)S(1)}, u32[]{:S(2)}, u32[]{:S(2)}) collective-permute-start(f32[6,48,128]{2,1,0:T(8,128)} %combine.1.g0), channel_id=1, source_target_pairs={{0,64},{8,72},{16,80},{24,88},{32,96},{40,104},{48,112},{56,120},{... | collective-permute-start | bytes 442376 | tf_op jit(solution)/shard_map/ppermute | solution.py:288
  59.4 11.2 %collective-permute-start.13 = (f32[6,48,128]{2,1,0:T(8,128)}, f32[6,48,128]{2,1,0:T(8,128)S(1)}, u32[]{:S(2)}, u32[]{:S(2)}) collective-permute-start(f32[6,48,128]{2,1,0:T(8,128)} %combine.1.g0), channel_id=1, source_target_pairs={{0,32},{8,40},{16,48},{24,56},{32,64},{40,72},{48,80},{56,88},{64,... | collective-permute-start | bytes 442376 | tf_op jit(solution)/shard_map/ppermute | solution.py:288
  60.5 3.4 %copy-start.1 = (f32[64,256,128]{2,1,0:T(8,128)S(1)}, f32[64,256,128]{2,1,0:T(8,128)}, u32[]{:S(2)}) copy-start(f32[64,256,128]{2,1,0:T(8,128)} %below.1) | copy-start | bytes 25165828
  63.9 6.7 %copy-start.4 = (f32[6,48,128]{2,1,0:T(8,128)S(1)}, f32[6,48,128]{2,1,0:T(8,128)}, u32[]{:S(2)}) copy-start(f32[6,48,128]{2,1,0:T(8,128)} %combine.1.g0) | copy-start | bytes 442372

commit v2 on v1

v2 whole, which is shorter than its diff:
```python
import functools

import jax
import jax.numpy as jnp
from jax import lax
from jax.experimental import pallas as pl
from jax.experimental.pallas import tpu as pltpu
from jax.sharding import PartitionSpec as P

STEPS = 3
KAPPA = 0.125
C = 48
WIDE = 56
SIDE = 4
GROUP_ROWS = 8
DEV_ROWS = 4
FB_SLOTS = 3
FB_GROUP = 7
FB_WINDOW = 22
F32 = jnp.float32
BF16 = jnp.bfloat16


def third(value):
    return lax.div(value, jnp.int32(3))


def wrap(value):
    return lax.rem(value + 2 * SIDE, jnp.int32(SIDE))


def split(value):
    high = value.astype(BF16)
    return high, (value - high.astype(F32)).astype(BF16)


def wide_weights(matrix):
    high, low = split(matrix)
    row = jnp.concatenate([high, low], axis=1)
    return jnp.concatenate([row, row], axis=0)


def mix(value, weights):
    lhs = jnp.concatenate(split(value), axis=1)
    both = jnp.dot(lhs, weights, preferred_element_type=F32)
    half = both.shape[1] // 2
    return both[:, :half] + both[:, half:]


def choose(way, values):
    result = values[-1]
    for k in range(len(values) - 2, -1, -1):
        result = jnp.where(way == k, values[k], result)
    return result


def eye(size):
    shape = (size, size)
    return lax.broadcasted_iota(jnp.int32, shape, 0) == lax.broadcasted_iota(jnp.int32, shape, 1)


def nest_weights(nest_mix, courant):
    c0, c1 = courant[0:1, :], courant[1:2, :]
    stay = jnp.where(eye(nest_mix.shape[0]), 1.0 - c0 - c1, 0.0)
    return c0, c1, wide_weights(nest_mix[...] + stay)


def owner_place(row, first, tile_rows):
    owner = lax.div(jnp.maximum(row, 0), jnp.int32(tile_rows))
    base = owner * tile_rows
    begin = jnp.clip(first - base, 0, tile_rows - GROUP_ROWS)
    return owner, jnp.clip(row - base - begin, 0, GROUP_ROWS - 1)


def pack_kernel(tile_rows, tile_cols, nest_rows, pos, parent, nest, b0, b1, b2, b3, west, east, down, up, band, cols, sems):
    tile = lax.axis_index("tiles")
    line = lax.axis_index("nests")
    my_y = lax.div(tile, jnp.int32(SIDE))
    corner = third(pos[0, 1]) - line * tile_cols
    aligned = pl.multiple_of(lax.div(corner, jnp.int32(8)) * 8, 8)
    shift = corner - aligned
    copies = []
    for k in range(SIDE):
        group = wrap(my_y + k)
        first = third(pos[0, 0] + SIDE * nest_rows * group) - 1
        begin = jnp.clip(first - tile * tile_rows, 0, tile_rows - GROUP_ROWS)
        copies.append(
            pltpu.make_async_copy(
                parent.at[pl.ds(begin, GROUP_ROWS), pl.ds(aligned, WIDE)], band.at[k], sems.at[k]
            )
        )
    halo = 3
    others = [
        pltpu.make_async_copy(parent.at[:, pl.ds(0, 8)], cols.at[0], sems.at[4]),
        pltpu.make_async_copy(parent.at[:, pl.ds(tile_cols - 8, 8)], cols.at[1], sems.at[5]),
        pltpu.make_async_copy(parent.at[tile_rows - 1], down.at[pl.ds(0, tile_cols)], sems.at[6]),
        pltpu.make_async_copy(parent.at[0], up, sems.at[7]),
    ]
    nest_cols = nest.shape[1]
    for r in range(halo):
        others.append(
            pltpu.make_async_copy(
                nest.at[nest_rows - halo + r],
                down.at[pl.ds(tile_cols + r * nest_cols, nest_cols)],
                sems.at[8 + r],
            )
        )
    for copy in copies + others:
        copy.start()
    for k, out in enumerate((b0, b1, b2, b3)):
        copies[k].wait()
        for r in range(GROUP_ROWS):
            out[r] = band[k, r, pl.ds(shift, C), :]
    others[0].wait()
    west[...] = cols[0, :, 0, :]
    others[1].wait()
    east[...] = cols[1, :, 7, :]
    for copy in others[2:]:
        copy.wait()


def pick_kernel(tile_rows, nest_rows, pos, fed, west, east, r0, r1, r2, r3, o0, o1, o2, o3, west_out, east_out):
    tile = lax.axis_index("tiles")
    my_y, my_z = lax.div(tile, jnp.int32(SIDE)), lax.rem(tile, jnp.int32(SIDE))
    first = third(pos[0, 0] + SIDE * nest_rows * my_y) - 1
    west_out[...] = west[...]
    east_out[...] = east[...]
    for k, out in enumerate((o0, o1, o2, o3)):
        target = my_y * SIDE + wrap(my_z + k)
        top = third(pos[0, 0] + nest_rows * target) - 1
        for j in range(DEV_ROWS):
            owner, place = owner_place(top + j, first, tile_rows)
            way = wrap(my_y - lax.div(owner, jnp.int32(SIDE)))
            out[j] = choose(way, [ref[place] for ref in (r0, r1, r2, r3)])
        for s in range(FB_SLOTS):
            out[DEV_ROWS + s] = fed[s]


def nest_kernel(tile_rows, tile_cols, pos, r0, r1, r2, r3, state, down, nest_mix, courant, out, lines, start, cur):
    tile = lax.axis_index("tiles")
    my_y, my_z = lax.div(tile, jnp.int32(SIDE)), lax.rem(tile, jnp.int32(SIDE))
    nest_rows, ncols, width = state.shape
    halo = STEPS
    ox, oy = pos[0, 0], pos[0, 1]
    phase = lax.rem(oy, jnp.int32(3))
    top = third(ox + nest_rows * tile) - 1
    spot = lax.broadcasted_iota(jnp.int32, (ncols, C), 0) + phase
    near = third(spot)
    frac = spot - 3 * near
    place = lax.broadcasted_iota(jnp.int32, (ncols, C), 1)
    table = jnp.where(place == near, 3 - frac, jnp.where(place == near + 1, frac, 0))
    table = table.astype(F32).astype(BF16)
    for j in range(DEV_ROWS):
        owner = lax.div(jnp.maximum(top + j, 0), jnp.int32(tile_rows))
        way = wrap(my_z - lax.rem(owner, jnp.int32(SIDE)))
        high, low = split(choose(way, [ref[j] for ref in (r0, r1, r2, r3)]))
        lines[j] = jnp.dot(table, high, preferred_element_type=F32) + jnp.dot(
            table, low, preferred_element_type=F32
        )
    for x in range(-halo, nest_rows):
        at = ox + nest_rows * tile + x
        at = jnp.maximum(at, 0)
        near_row = jnp.clip(third(at) - top, 0, DEV_ROWS - 2)
        part = lax.rem(at, jnp.int32(3)).astype(F32)
        interp = (3.0 - part) * lines[near_row] + part * lines[near_row + 1]
        own = state[x] if x >= 0 else down[pl.ds(tile_cols + (x + halo) * ncols, ncols), :]
        start[x + halo] = 0.5 * (own + interp * (1.0 / 9.0))
    first = tile == 0

    @pl.when(first)
    def _():
        for x in range(halo):
            start[x] = start[halo]

    c0, c1, weights = nest_weights(nest_mix, courant)
    edge_row = lax.broadcasted_iota(jnp.int32, (ncols, width), 0) == 0
    source = start
    for step in range(STEPS):
        last = step == STEPS - 1
        for r in range(nest_rows + halo - 1, step, -1):
            value = source[r]
            left = jnp.where(edge_row, start[r, 0:1, :], pltpu.roll(value, 1, 0))
            value = mix(value, weights) + c0 * source[r - 1] + c1 * left
            if r < halo:
                value = jnp.where(first, start[halo], value)
            if last:
                out[r - halo] = value
            else:
                cur[step, r] = value
        source = cur.at[step]


def up_third(value):
    return third(value + 2)


def feed_kernel(pos, state, nest_mix, courant, fb, start, cur):
    tile = lax.axis_index("tiles")
    nest_rows, ncols, width = state.shape
    rows = nest_rows + STEPS
    ox, oy = pos[0, 0], pos[0, 1]
    for x in range(rows):
        start[x] = 0.5 * state[x] if x < nest_rows else jnp.zeros((ncols, width), F32)
    above = jnp.where(tile == 0, start[0], 0.0)
    c0, c1, weights = nest_weights(nest_mix, courant)
    edge_row = lax.broadcasted_iota(jnp.int32, (ncols, width), 0) == 0

    def advanced(value, upper, edge):
        left = jnp.where(edge_row, edge, pltpu.roll(value, 1, 0))
        return mix(value, weights) + c0 * upper + c1 * left

    source = start
    for step in range(STEPS - 1):
        for r in range(nest_rows + step + 1):
            upper = above if r == 0 else source[r - 1]
            cur[step, r] = advanced(source[r], upper, start[r, 0:1, :])
        for r in range(nest_rows + step + 1, rows):
            cur[step, r] = jnp.zeros((ncols, width), F32)
        source = cur.at[step]
    rem_y = lax.rem(3 - lax.rem(oy, jnp.int32(3)), jnp.int32(3))
    slot = lax.broadcasted_iota(jnp.int32, (C, ncols), 0)
    pick = (lax.broadcasted_iota(jnp.int32, (C, ncols), 1) == rem_y + 3 * slot).astype(F32).astype(BF16)
    pick = jnp.concatenate([pick, pick], axis=1)
    first = up_third(ox + nest_rows * tile) * 3 - ox - nest_rows * tile
    for s in range(FB_SLOTS):
        r = jnp.minimum(first + 3 * s, rows - 1)
        upper = source[jnp.maximum(r - 1, 0)]
        if s == 0:
            upper = jnp.where(r == 0, above, upper)
        value = advanced(source[r], upper, start[r, 0:1, :])
        fb[s] = jnp.dot(pick, jnp.concatenate(split(value), axis=0), preferred_element_type=F32)


def combine_kernel(nest_rows, pos, e0, e1, e2, e3, out):
    tile = lax.axis_index("tiles")
    my_y, my_z = lax.div(tile, jnp.int32(SIDE)), lax.rem(tile, jnp.int32(SIDE))
    ox = pos[0, 0]
    base = up_third(ox + SIDE * nest_rows * my_y)
    for r in range(FB_GROUP):
        out[r] = jnp.zeros(out.shape[1:], F32)
    for k, ref in enumerate((e0, e1, e2, e3)):
        origin = ox + nest_rows * (SIDE * my_y + wrap(my_z - k))
        row = up_third(origin)
        for s in range(FB_SLOTS):

            @pl.when(3 * (row + s) - origin < nest_rows + STEPS)
            def _(ref=ref, row=row, s=s):
                out[row + s - base] += ref[DEV_ROWS + s]


def window(pos, tile_rows, tile_cols, total):
    ox, oy = pos[0, 0], pos[0, 1]
    first_row = lax.axis_index("tiles") * tile_rows
    low_row, high_row = up_third(ox), third(ox + total - 1)
    owns = (high_row >= first_row) & (low_row < first_row + tile_rows)
    begin = jnp.clip(low_row - first_row, 0, tile_rows - FB_WINDOW)
    corner = third(oy) - lax.axis_index("nests") * tile_cols
    aligned = pl.multiple_of(lax.div(corner, jnp.int32(8)) * 8, 8)
    shift = corner - aligned + up_third(oy) - third(oy)
    return owns, first_row, begin, aligned, shift, up_third(oy) * 3 - oy


def own_kernel(tile_rows, tile_cols, total, pos, parent, from_up, nest_mix, courant, out, buf, parts, sems):
    owns, first_row, begin, aligned, shift, rem_y = window(pos, tile_rows, tile_cols, total)
    ox = pos[0, 0]
    width = buf.shape[2]

    @pl.when(owns)
    def _():
        cols = pl.ds(aligned, WIDE)
        main = pltpu.make_async_copy(
            parent.at[pl.ds(begin, FB_WINDOW), cols], buf.at[pl.ds(1, FB_WINDOW), pl.ds(8, WIDE)], sems.at[0]
        )
        edge = pltpu.make_async_copy(
            parent.at[jnp.maximum(begin - 1, 0), cols], buf.at[0, pl.ds(8, WIDE)], sems.at[1]
        )
        main.start()
        edge.start()
        buf[:, 0:8, :] = jnp.zeros((FB_WINDOW + 1, 8, width), F32)

        c0, c1 = courant[0:1, :], courant[1:2, :]
        diagonal = eye(width)
        r0 = jnp.sum(jnp.where(diagonal, c0, 0.0), axis=1, keepdims=True)
        r1 = jnp.sum(jnp.where(diagonal, c1, 0.0), axis=1, keepdims=True)
        one = nest_mix[...] + jnp.where(diagonal, 1.0 - c0 - c1, 0.0)
        weights = wide_weights(one)
        many = mix(jnp.concatenate([one, one * c0, one * c1], axis=0), weights)
        two, by0, by1 = many[:width], many[width : 2 * width], many[2 * width :]
        paths = {
            (0, 0): mix(two, weights),
            (1, 0): r0 * two + by0 + two * c0,
            (0, 1): r1 * two + by1 + two * c1,
            (2, 0): (r0 * r0) * one + (r0 * one) * c0 + one * (c0 * c0),
            (0, 2): (r1 * r1) * one + (r1 * one) * c1 + one * (c1 * c1),
            (1, 1): (2.0 * r0 * r1) * one + (r0 * one) * c1 + (r1 * one) * c0 + one * (2.0 * c0 * c1),
            (3, 0): jnp.where(diagonal, c0 * c0 * c0, 0.0),
            (0, 3): jnp.where(diagonal, c1 * c1 * c1, 0.0),
            (2, 1): jnp.where(diagonal, 3.0 * c0 * c0 * c1, 0.0),
            (1, 2): jnp.where(diagonal, 3.0 * c0 * c1 * c1, 0.0),
        }

        def corner(low_row, low_col):
            sum_of = jnp.zeros((width, width), F32)
            for (i, j), path in paths.items():
                weight = (i if low_row else 3 - i) * (j if low_col else 3 - j) * (0.5 / 9.0)
                if weight:
                    sum_of = sum_of + weight * path
            return wide_weights(sum_of)

        this_row = jnp.concatenate([corner(False, False), corner(False, True)], axis=0)
        row_before = jnp.concatenate([corner(True, False), corner(True, True)], axis=0)

        main.wait()
        edge.wait()

        @pl.when(begin == 0)
        def _():
            buf[0, pl.ds(8, WIDE), :] = from_up[pl.ds(aligned, WIDE), :]

        for w in range(FB_WINDOW + 1):
            near = buf[w, pl.ds(8 + shift, C), :]
            back = buf[w, pl.ds(7 + shift, C), :]
            parts[w] = jnp.concatenate(split(near) + split(back), axis=1)
        batch = FB_WINDOW // 2
        for w in range(0, FB_WINDOW, batch):
            this = parts[w + 1 : w + 1 + batch].reshape(batch * C, 4 * width)
            before = parts[w : w + batch].reshape(batch * C, 4 * width)
            both = jnp.dot(this, this_row, preferred_element_type=F32) + jnp.dot(
                before, row_before, preferred_element_type=F32
            )
            out[w : w + batch] = (both[:, :width] + both[:, width:]).reshape(batch, C, width)

        first = up_third(ox) - first_row - begin
        at = jnp.clip(first, 0, FB_WINDOW - 1)
        pad = jnp.zeros((24 - FB_WINDOW, width), F32)

        def gather(k, offset):
            column = buf[pl.ds(k, FB_WINDOW), pl.ds(offset + shift, 1), :].reshape(FB_WINDOW, width)
            return jnp.concatenate([buf[at + k, pl.ds(offset + shift, C), :], column, pad], axis=0)

        near = [gather(k, 8) for k in range(2)]
        back = [gather(k, 7) for k in range(2)]
        line = lax.broadcasted_iota(jnp.int32, near[0].shape, 0)
        in_row = line < C
        x = 3 * (first_row + begin + jnp.where(in_row, at, line - C)) - ox
        y = rem_y + 3 * jnp.where(in_row, line, 0)
        start = {}
        for i in range(STEPS + 1):
            lean = jnp.minimum(x, i).astype(F32) * (0.5 / 9.0)
            rest = 0.5 / 3.0 - lean
            right = rest * near[1] + lean * near[0]
            left = rest * back[1] + lean * back[0]
            for j in range(STEPS + 1 - i):
                tilt = jnp.minimum(y, j).astype(F32)
                start[i, j] = right * (3.0 - tilt) + left * tilt
        cells = start
        size = C + 24
        for step in range(STEPS):
            keys = [(i, j) for i in range(STEPS - step) for j in range(STEPS - step - i)]
            mixed = mix(jnp.concatenate([cells[key] for key in keys], axis=0), weights)
            fresh = {}
            for n, (i, j) in enumerate(keys):
                value = mixed[n * size : (n + 1) * size] + c0 * cells[i + 1, j] + c1 * cells[i, j + 1]
                fresh[i, j] = jnp.where((x < i) | (y < j), start[i, j], value)
            cells = fresh
        edges = cells[0, 0]

        @pl.when((first >= 0) & (first < FB_WINDOW))
        def _():
            out[at] = edges[:C]

        for w in range(FB_WINDOW):
            out[w, 0:1, :] = edges[C + w : C + w + 1]


def patch_kernel(tile_rows, tile_cols, nest_rows, ncols, pos, parent, own, g0, g1, g2, g3, out, buf, sems):
    total = nest_rows * SIDE * SIDE
    owns, first_row, begin, aligned, shift, rem_y = window(pos, tile_rows, tile_cols, total)
    my_y = lax.div(lax.axis_index("tiles"), jnp.int32(SIDE))
    ox = pos[0, 0]
    span = SIDE * nest_rows

    @pl.when(owns)
    def _():
        place = (pl.ds(begin, FB_WINDOW), pl.ds(aligned, WIDE))
        copy = pltpu.make_async_copy(parent.at[place], buf, sems.at[0])
        copy.start()
        copy.wait()
        live = rem_y + 3 * lax.broadcasted_iota(jnp.int32, (C, buf.shape[2]), 0) < ncols

        @pl.loop(0, FB_WINDOW)
        def _(w):
            row = first_row + begin + w
            x = 3 * row - ox

            @pl.when((x >= 0) & (x < total))
            def _():
                def from_group(group):
                    r = jnp.clip(row - up_third(ox + span * group), 0, FB_GROUP - 1)
                    return choose(wrap(my_y - group), [ref[r] for ref in (g0, g1, g2, g3)])

                group = lax.div(x, jnp.int32(span))
                value = own[w] + from_group(group)
                spilt = (group > 0) & (x - span * group < STEPS)
                value = value + jnp.where(spilt, from_group(jnp.maximum(group - 1, 0)), 0.0)
                old = buf[w, pl.ds(shift, C), :]
                buf[w, pl.ds(shift, C), :] = jnp.where(live, 0.5 * (old + value), old)

        back = pltpu.make_async_copy(buf, out.at[place], sems.at[1])
        back.start()
        back.wait()


def parent_kernel(rows, parent, from_up, from_down, west, east, parent_mix, out, token, full, done, weights, in_sems, out_sems):
    height, cols = parent.shape[0], parent.shape[1]
    count = height // rows

    def fetch(i):
        return pltpu.make_async_copy(
            parent.at[pl.ds(i * rows, rows)], full.at[pl.ds(1 + i * rows, rows)], in_sems.at[i]
        )

    def store(i):
        slot = lax.rem(i, 2)
        return pltpu.make_async_copy(done.at[slot], out.at[pl.ds(i * rows, rows)], out_sems.at[slot])

    for i in range(count):
        fetch(i).start()
    size = parent_mix.shape[0]
    weights[...] = wide_weights(parent_mix[...] + jnp.where(eye(size), 1.0 - 4.0 * KAPPA, 0.0))
    full[0] = from_up[pl.ds(0, cols), :]
    full[height + 1] = from_down[...]
    index = lax.broadcasted_iota(jnp.int32, (cols, size), 0)
    low_edge, high_edge = index == 0, index == cols - 1
    fetch(0).wait()

    @pl.loop(0, count)
    def _(i):
        @pl.when(i + 1 < count)
        def _():
            fetch(i + 1).wait()

        @pl.when(i >= 2)
        def _():
            store(i - 2).wait()

        slot = lax.rem(i, 2)
        for r in range(rows):
            at = i * rows + r
            value = full[at + 1]
            left = jnp.where(low_edge, west[pl.ds(at, 1), :], pltpu.roll(value, 1, 0))
            right = jnp.where(high_edge, east[pl.ds(at, 1), :], pltpu.roll(value, cols - 1, 0))
            beside = (full[at] + full[at + 2]) + (left + right)
            done[slot, r] = mix(value, weights[...]) + KAPPA * beside
        store(i).start()

    store(count - 2).wait()
    store(count - 1).wait()
    token[...] = jnp.zeros(token.shape, F32)


def smem():
    return pl.BlockSpec(memory_space=pltpu.SMEM)


def vmem():
    return pl.BlockSpec(memory_space=pltpu.VMEM)


def hbm():
    return pl.BlockSpec(memory_space=pltpu.HBM)


def run(name, kernel, ins, outs, scratch=(), after=(), room=50, flops=0, moved=1, **options):
    given, held = len(ins), len(after)

    def body(*refs):
        kernel(*refs[:given], *refs[given + held :])

    return pl.pallas_call(
        body,
        out_shape=[shape for _, shape in outs],
        in_specs=[spec for spec, _ in ins] + [pl.BlockSpec(memory_space=pl.ANY)] * held,
        out_specs=[spec for spec, _ in outs],
        scratch_shapes=list(scratch),
        compiler_params=pltpu.CompilerParams(vmem_limit_bytes=room << 20),
        cost_estimate=pl.CostEstimate(flops=flops, bytes_accessed=moved << 20, transcendentals=0),
        name=name,
        **options,
    )(*[value for _, value in ins], *after)


def y_route(k):
    return [(t, (t + SIDE * k) % (SIDE * SIDE)) for t in range(SIDE * SIDE)]


def z_route(k):
    return [(t, t // SIDE * SIDE + (t + k) % SIDE) for t in range(SIDE * SIDE)]


def shards(parent, nest_state, parent_mix, nest_mix, courant, nest_pos):
    tile_rows, tile_cols, width = parent.shape
    state = nest_state[0]
    nest_rows, ncols, _ = state.shape
    total = nest_rows * SIDE * SIDE
    count = SIDE * SIDE
    lines = lax.axis_size("nests")
    S, V, H = smem(), vmem(), hbm()
    big = 50

    def f(*shape):
        return jax.ShapeDtypeStruct(shape, F32)

    def on_tiles(block, route):
        return lax.ppermute(block, "tiles", route)

    packed = run(
        "pack",
        functools.partial(pack_kernel, tile_rows, tile_cols, nest_rows),
        [(S, nest_pos), (H, parent), (H, state)],
        [(V, f(GROUP_ROWS, C, width))] * SIDE
        + [(V, f(tile_rows, width))] * 2
        + [(V, f(tile_cols + STEPS * ncols, width)), (V, f(tile_cols, width))],
        [
            pltpu.VMEM((SIDE, GROUP_ROWS, WIDE, width), F32),
            pltpu.VMEM((2, tile_rows, 8, width), F32),
            pltpu.SemaphoreType.DMA((11,)),
        ],
        moved=4,
    )
    b, (west_out, east_out, down_out, up_out) = packed[:4], packed[4:]
    got = {k: on_tiles(b[k], y_route(k)) for k in (1, 3, 2)}
    from_up = on_tiles(down_out, [(i, i + 1) for i in range(count - 1)])
    from_down = on_tiles(up_out, [(i + 1, i) for i in range(count - 1)])

    (fed,) = run(
        "feed",
        feed_kernel,
        [(S, nest_pos), (V, state), (V, nest_mix), (V, courant)],
        [(V, f(FB_SLOTS, C, width))],
        [
            pltpu.VMEM((nest_rows + STEPS, ncols, width), F32),
            pltpu.VMEM((STEPS - 1, nest_rows + STEPS, ncols, width), F32),
        ],
        after=[west_out],
        flops=1 << 28,
        moved=4,
    )
    picked = run(
        "pick",
        functools.partial(pick_kernel, tile_rows, nest_rows),
        [(S, nest_pos)] + [(V, x) for x in (fed, west_out, east_out, b[0], got[1], got[2], got[3])],
        [(V, f(DEV_ROWS + FB_SLOTS, C, width))] * SIDE + [(V, f(tile_rows, width))] * 2,
    )
    mine = {k: on_tiles(picked[k], z_route(k)) for k in (1, 3, 2)}
    west = lax.ppermute(picked[5], "nests", [(i, i + 1) for i in range(lines - 1)])
    east = lax.ppermute(picked[4], "nests", [(i + 1, i) for i in range(lines - 1)])
    (own,) = run(
        "own_feed",
        functools.partial(own_kernel, tile_rows, tile_cols, total),
        [(S, nest_pos), (H, parent), (V, from_up), (V, nest_mix), (V, courant)],
        [(V, f(FB_WINDOW, C, width))],
        [
            pltpu.VMEM((FB_WINDOW + 1, WIDE + 8, width), F32),
            pltpu.VMEM((FB_WINDOW + 1, C, 4 * width), BF16),
            pltpu.SemaphoreType.DMA((2,)),
        ],
        after=[picked[0]],
        flops=1 << 30,
        moved=8,
    )
    (joined,) = run(
        "combine",
        functools.partial(combine_kernel, nest_rows),
        [(S, nest_pos), (V, picked[0])] + [(V, mine[k]) for k in (1, 2, 3)],
        [(V, f(FB_GROUP, C, width))],
        after=[own],
    )
    groups = {k: on_tiles(joined, y_route(k)) for k in (1, 3, 2)}

    rows = 8
    parent_new, token = run(
        "parent_step",
        functools.partial(parent_kernel, rows),
        [(H, parent)] + [(V, x) for x in (from_up, from_down, west, east, parent_mix)],
        [(H, f(tile_rows, tile_cols, width)), (V, f(8, width))],
        [
            pltpu.VMEM((tile_rows + 2, tile_cols, width), F32),
            pltpu.VMEM((2, rows, tile_cols, width), F32),
            pltpu.VMEM((2 * width, 2 * width), BF16),
            pltpu.SemaphoreType.DMA((tile_rows // rows,)),
            pltpu.SemaphoreType.DMA((2,)),
        ],
        after=[joined],
        room=big,
        flops=2 * tile_rows * tile_cols * 256 * 256,
        moved=20,
    )
    (nest_out,) = run(
        "nest_steps",
        functools.partial(nest_kernel, tile_rows, tile_cols),
        [(S, nest_pos), (V, picked[0])]
        + [(V, mine[k]) for k in (1, 2, 3)]
        + [(V, x) for x in (state, from_up, nest_mix, courant)],
        [(V, f(nest_rows, ncols, width))],
        [
            pltpu.VMEM((DEV_ROWS, ncols, width), F32),
            pltpu.VMEM((nest_rows + STEPS, ncols, width), F32),
            pltpu.VMEM((STEPS - 1, nest_rows + STEPS, ncols, width), F32),
        ],
        after=[token],
        flops=1 << 28,
        moved=6,
    )
    (parent_out,) = run(
        "patch",
        functools.partial(patch_kernel, tile_rows, tile_cols, nest_rows, ncols),
        [(S, nest_pos), (H, parent_new), (V, own), (V, joined)] + [(V, groups[k]) for k in (1, 2, 3)],
        [(H, f(tile_rows, tile_cols, width))],
        [pltpu.VMEM((FB_WINDOW, WIDE, width), F32), pltpu.SemaphoreType.DMA((2,))],
        room=big,
        moved=2,
        input_output_aliases={1: 0},
    )
    return parent_out, nest_out[None]


def solution(mesh):
    placed = (
        P("tiles", "nests", None),
        P("nests", "tiles", None, None),
        P(),
        P(),
        P(),
        P("nests", None),
    )
    return jax.shard_map(
        shards,
        mesh=mesh,
        in_specs=placed,
        out_specs=(P("tiles", "nests", None), P("nests", "tiles", None, None)),
        check_vma=False,
    )
```

time: 75 us -> 56.3 us (0.75); the launches traced: 73.8 us -> 55.9 us
  local copies, waits for them, and re-layouts: 11.9 us -> 1.62 us
  waiting for transfers between devices: 10.5 us -> 2.58 us
  Pallas kernels: 17.8 us -> 21.9 us
  starting transfers between devices: 32.7 us -> 29.1 us
    unnamed x40 -> x12, local copies, waits for them, and re-layouts: 11.9 us -> 1.62 us
    ppermute x16 -> x13, waiting for transfers between devices: 10.5 us -> 2.58 us  [the longest x11 2.58 us: on_tiles(): return lax.ppermute(block, 'tiles', route)]
    pallas_call x6 -> x8, Pallas kernels: 17.8 us -> 21.9 us  [run(): pl.pallas_call(body, out_shape=[shape for _, shape in outs], in_specs=[sp...]
    ppermute x16 -> x13, starting transfers between devices: 32.7 us -> 29.1 us  [the longest x11 21.5 us: on_tiles(): return lax.ppermute(block, 'tiles', route)]
  transfers between devices with their start and end apart: 16 -> 13, of which waited for: 4 -> 2; matrix products, arithmetic and copies ran while one was open for 0% -> 0% of each run, Pallas kernels for 18% -> 29%
where the time goes in v2:
time: 56.3 us; the launch traced here: 55.9 us
  starting transfers between devices  29.1 us (52%)
  Pallas kernels  21.9 us (39%)
  waiting for transfers between devices  2.58 us (5%)
  local copies, waits for them, and re-layouts  1.62 us (3%)
  between operations  0.82 us (1%)
    pallas_call x8, Pallas kernels, run(): pl.pallas_call(body, out_shape=[shape for _, shape in outs], in_specs=[sp...  21.9 us
    ppermute x11, starting transfers between devices, on_tiles(): return lax.ppermute(block, 'tiles', route)  21.5 us
    ppermute x1, starting transfers between devices, shards(): lax.ppermute(picked[5], 'nests', [(i, i + 1) for i in range(lines - 1)])  5.63 us
    ppermute x11, waiting for transfers between devices, on_tiles(): return lax.ppermute(block, 'tiles', route)  2.58 us
    ppermute x1, starting transfers between devices, shards(): lax.ppermute(picked[4], 'nests', [(i + 1, i) for i in range(lines - 1)])  1.92 us
    unnamed x12, local copies, waits for them, and re-layouts  1.62 us
  transfers between devices with their start and end apart: 13, of which 2 were waited for; matrix products, arithmetic and copies ran while one was open for 0% of the time, Pallas kernels for 29%

profile of v2, /device:TPU:1, one launch (start us, length us, event | category | flops | bytes accessed | tf_op | source)
XLA Modules:
  0.0 55.9 jit_solution(3117559103724508130)
XLA Ops:
  0.6 0.0 copy-start.5
  0.6 0.0 copy-start
  0.7 0.9 %copy-done = f32[1,4,128,128]{3,2,1,0:T(8,128)S(1)} copy-done((f32[1,4,128,128]{3,2,1,0:T(8,128)S(1)}, f32[1,4,128,128]{3,2,1,0:T(8,128)}, u32[]{:S(2)}) %copy-start) | copy-done | bytes 262168
  1.6 0.0 copy-start.4
  1.6 0.7 %copy-done.4 = s32[1,2]{1,0:T(1,128)S(1)} copy-done((s32[1,2]{1,0:T(1,128)S(1)}, s32[1,2]{1,0:T(1,128)}, u32[]{:S(2)}) %copy-start.4) | copy-done | bytes 32
  2.3 0.0 copy-start.2
  2.3 2.2 %pack.1 = (f32[8,48,128]{2,1,0:T(8,128)S(1)}, f32[8,48,128]{2,1,0:T(8,128)S(1)}, f32[8,48,128]{2,1,0:T(8,128)S(1)}, f32[8,48,128]{2,1,0:T(8,128)S(1)}, f32[64,12...) custom-call(s32[1,2]{1,0:T(1,128)S(1)} %copy-done.4, ...), custom_call_target="tpu_custom_call" | custom-call | bytes 4194304 | tf_op jit(solution)/shard_map/pack/pallas_call | solution.py:480
  4.5 0.0 copy-start.3
  4.5 2.2 %collective-permute-start.2 = (f32[8,48,128]{2,1,0:T(8,128)S(1)}, f32[8,48,128]{2,1,0:T(8,128)S(1)}, u32[]{:S(2)}, u32[]{:S(2)}) collective-permute-start(f32[8,48,128]{2,1,0:T(8,128)S(1)} %get-tuple-element.23), channel_id=1, source_target_pairs={{0,32},{8,40},{16,48},{24,56},{32,64},{40,72},{48,80},{56,88},{64,... | collective-permute-start | bytes 589832 | tf_op jit(solution)/shard_map/ppermute | solution.py:515
  6.7 2.6 %collective-permute-start.3 = (f32[8,48,128]{2,1,0:T(8,128)S(1)}, f32[8,48,128]{2,1,0:T(8,128)S(1)}, u32[]{:S(2)}, u32[]{:S(2)}) collective-permute-start(f32[8,48,128]{2,1,0:T(8,128)S(1)} %get-tuple-element.24), channel_id=1, source_target_pairs={{0,64},{8,72},{16,80},{24,88},{32,96},{40,104},{48,112},{56,120},{... | collective-permute-start | bytes 589832 | tf_op jit(solution)/shard_map/ppermute | solution.py:515
  9.3 1.1 %collective-permute-start.4 = (f32[8,48,128]{2,1,0:T(8,128)S(1)}, f32[8,48,128]{2,1,0:T(8,128)S(1)}, u32[]{:S(2)}, u32[]{:S(2)}) collective-permute-start(f32[8,48,128]{2,1,0:T(8,128)S(1)} %get-tuple-element.25), channel_id=1, source_target_pairs={{0,96},{8,104},{16,112},{24,120},{32,0},{40,8},{48,16},{56,24},{64... | collective-permute-start | bytes 589832 | tf_op jit(solution)/shard_map/ppermute | solution.py:515
  10.4 3.5 %collective-permute-start = (f32[640,128]{1,0:T(8,128)S(1)}, f32[640,128]{1,0:T(8,128)S(1)}, u32[]{:S(2)}, u32[]{:S(2)}) collective-permute-start(f32[640,128]{1,0:T(8,128)S(1)} %get-tuple-element.18), channel_id=1, source_target_pairs={{0,8},{8,16},{16,24},{24,32},{32,40},{40,48},{48,56},{56,64},{64,7... | collective-permute-start | bytes 983048 | tf_op jit(solution)/shard_map/ppermute | solution.py:515
  13.9 0.0 copy-done.5
  13.9 0.0 copy-done.2
  13.9 1.4 %feed.1.refs_1_ = f32[3,48,128]{2,1,0:T(8,128)S(1)} custom-call(s32[1,2]{1,0:T(1,128)S(1)} %copy-done.4, f32[4,128,128]{2,1,0:T(8,128)S(1)} %bitcast.3, f32[128,128]{1,0:T(8,128)S(1)} %copy-done.2, f32[2,128]{1,0:T(2,128)S(1)} %copy-done.5, f32[64,128]{1,0:T(8,128)S(1)} %get-tuple-element.20.refs_4_.refs_2_), custom_call_target="tpu_custom_call" | custom-call | flops 268435456 | bytes 4194304 | tf_op jit(solution)/shard_map/feed/pallas_call | solution.py:480
  15.3 0.0 collective-permute-done.2.refs_5_
  15.3 2.4 %collective-permute-done.3.refs_6_ = f32[8,48,128]{2,1,0:T(8,128)S(1)} collective-permute-done((f32[8,48,128]{2,1,0:T(8,128)S(1)}, f32[8,48,128]{2,1,0:T(8,128)S(1)}, u32[]{:S(2)}, u32[]{:S(2)}) %collective-permute-start.3) | collective-permute-done | bytes 196640 | tf_op jit(solution)/shard_map/ppermute | solution.py:515
  17.8 0.0 collective-permute-done.4.refs_7_
  17.8 0.8 %pick.1 = (f32[7,48,128]{2,1,0:T(8,128)S(1)}, f32[7,48,128]{2,1,0:T(8,128)S(1)}, f32[7,48,128]{2,1,0:T(8,128)S(1)}, f32[7,48,128]{2,1,0:T(8,128)S(1)}, f32[64,128]{1,0:T(8,128)S(1)}, /*index=5*/f32[64,128]{1,0:T(8,128)S(1)}) custom-call(s32[1,2]{1,0:T(1,128)S(1)} %copy-done.4, f32[3,48,128]{2,1,0:T(8,128)S(1)} %feed.1.refs_1_, ...), custom_call_target="tpu_custom_call" | custom-call | bytes 1048576 | tf_op jit(solution)/shard_map/pick/pallas_call | solution.py:480
  18.5 1.7 %collective-permute-start.7 = (f32[7,48,128]{2,1,0:T(8,128)S(1)}, f32[7,48,128]{2,1,0:T(8,128)S(1)}, u32[]{:S(2)}, u32[]{:S(2)}) collective-permute-start(f32[7,48,128]{2,1,0:T(8,128)S(1)} %get-tuple-element.29), channel_id=1, source_target_pairs={{0,8},{8,16},{16,24},{24,0},{32,40},{40,48},{48,56},{56,32},{64,72... | collective-permute-start | bytes 516104 | tf_op jit(solution)/shard_map/ppermute | solution.py:515
  20.2 3.3 %collective-permute-start.8 = (f32[7,48,128]{2,1,0:T(8,128)S(1)}, f32[7,48,128]{2,1,0:T(8,128)S(1)}, u32[]{:S(2)}, u32[]{:S(2)}) collective-permute-start(f32[7,48,128]{2,1,0:T(8,128)S(1)} %get-tuple-element.30), channel_id=1, source_target_pairs={{0,16},{8,24},{16,0},{24,8},{32,48},{40,56},{48,32},{56,40},{64,80... | collective-permute-start | bytes 516104 | tf_op jit(solution)/shard_map/ppermute | solution.py:515
  23.6 0.7 %collective-permute-start.9 = (f32[7,48,128]{2,1,0:T(8,128)S(1)}, f32[7,48,128]{2,1,0:T(8,128)S(1)}, u32[]{:S(2)}, u32[]{:S(2)}) collective-permute-start(f32[7,48,128]{2,1,0:T(8,128)S(1)} %get-tuple-element.31), channel_id=1, source_target_pairs={{0,24},{8,0},{16,8},{24,16},{32,56},{40,32},{48,40},{56,48},{64,88... | collective-permute-start | bytes 516104 | tf_op jit(solution)/shard_map/ppermute | solution.py:515
  24.3 1.3 %collective-permute-start.1 = (f32[256,128]{1,0:T(8,128)S(1)}, f32[256,128]{1,0:T(8,128)S(1)}, u32[]{:S(2)}, u32[]{:S(2)}) collective-permute-start(f32[256,128]{1,0:T(8,128)S(1)} %get-tuple-element.19), channel_id=1, source_target_pairs={{8,0},{16,8},{24,16},{32,24},{40,32},{48,40},{56,48},{64,56},{72,6... | collective-permute-start | bytes 393224 | tf_op jit(solution)/shard_map/ppermute | solution.py:515
  25.6 0.0 collective-permute-done.refs_2_.refs_1_.refs_6_
  25.6 5.6 %collective-permute-start.5 = (f32[64,128]{1,0:T(8,128)S(1)}, f32[64,128]{1,0:T(8,128)S(1)}, u32[]{:S(2)}, u32[]{:S(2)}) collective-permute-start(f32[64,128]{1,0:T(8,128)S(1)} %get-tuple-element.26), channel_id=1, source_target_pairs={{0,1},{1,2},{2,3},{3,4},{4,5},{5,6},{6,7},{8,9},{9,10},{10,11},{11... | collective-permute-start | bytes 98312 | tf_op jit(solution)/shard_map/ppermute | solution.py:556
  31.2 0.0 collective-permute-done.7.refs_2_
  31.2 1.9 %collective-permute-start.6 = (f32[64,128]{1,0:T(8,128)S(1)}, f32[64,128]{1,0:T(8,128)S(1)}, u32[]{:S(2)}, u32[]{:S(2)}) collective-permute-start(f32[64,128]{1,0:T(8,128)S(1)} %get-tuple-element.27), channel_id=1, source_target_pairs={{1,0},{2,1},{3,2},{4,3},{5,4},{6,5},{7,6},{9,8},{10,9},{11,10},{12... | collective-permute-start | bytes 98312 | tf_op jit(solution)/shard_map/ppermute | solution.py:557
  33.2 0.0 copy-start.1
  33.2 2.9 %own_feed.1.refs_5_.refs_2_ = f32[22,48,128]{2,1,0:T(8,128)S(1)} custom-call(s32[1,2]{1,0:T(1,128)S(1)} %copy-done.4, f32[64,256,128]{2,1,0:T(8,128)} %refs_0_.13, f32[640,128]{1,0:T(8,128)S(1)} %collective-permute-done.refs_2_.refs_1_.refs_6_, f32[128,128]{1,0:T(8,128)S(1)} %copy-done.2, f32[2,128]{1,0:T(2,128)S(1)} %copy-done.5, ...), custom_call_target="tpu_custom_call" | custom-call | flops 1073741824 | bytes 8388608 | tf_op jit(solution)/shard_map/own_feed/pallas_call | solution.py:480
  36.1 0.0 collective-permute-done.8.refs_3_
  36.1 0.0 collective-permute-done.9.refs_4_
  36.1 0.7 %combine.1.refs_6_.refs_3_ = f32[7,48,128]{2,1,0:T(8,128)S(1)} custom-call(s32[1,2]{1,0:T(1,128)S(1)} %copy-done.4, f32[7,48,128]{2,1,0:T(8,128)S(1)} %get-tuple-element.28.refs_5_.refs_1_, f32[7,48,128]{2,1,0:T(8,128)S(1)} %collective-permute-done.7.refs_2_, f32[7,48,128]{2,1,0:T(8,128)S(1)} %collective-permute-done.8.refs_3_, ...), custom_call_target="tpu_custom_call" | custom-call | bytes 1048576 | tf_op jit(solution)/shard_map/combine/pallas_call | solution.py:480
  36.8 4.0 %collective-permute-start.12 = (f32[7,48,128]{2,1,0:T(8,128)S(1)}, f32[7,48,128]{2,1,0:T(8,128)S(1)}, u32[]{:S(2)}, u32[]{:S(2)}) collective-permute-start(f32[7,48,128]{2,1,0:T(8,128)S(1)} %combine.1.refs_6_.refs_3_), channel_id=1, source_target_pairs={{0,96},{8,104},{16,112},{24,120},{32,0},{40,8},{48,16},{56,24},{64... | collective-permute-start | bytes 516104 | tf_op jit(solution)/shard_map/ppermute | solution.py:515
  40.8 0.4 collective-permute-start.11
  41.2 0.0 collective-permute-done.1.refs_2_
  41.2 0.6 %collective-permute-start.10 = (f32[7,48,128]{2,1,0:T(8,128)S(1)}, f32[7,48,128]{2,1,0:T(8,128)S(1)}, u32[]{:S(2)}, u32[]{:S(2)}) collective-permute-start(f32[7,48,128]{2,1,0:T(8,128)S(1)} %combine.1.refs_6_.refs_3_), channel_id=1, source_target_pairs={{0,32},{8,40},{16,48},{24,56},{32,64},{40,72},{48,80},{56,88},{64,... | collective-permute-start | bytes 516104 | tf_op jit(solution)/shard_map/ppermute | solution.py:515
  41.8 0.0 collective-permute-done.5.refs_3_
  41.8 0.0 collective-permute-done.6.refs_4_
  41.8 0.0 copy-done.3
  41.9 8.2 %parent_step.1 = (f32[64,256,128]{2,1,0:T(8,128)}, f32[8,128]{1,0:T(8,128)S(1)}) custom-call(f32[64,256,128]{2,1,0:T(8,128)} %refs_0_.13, f32[640,128]{1,0:T(8,128)S(1)} %collective-permute-done.refs_2_.refs_1_.refs_6_, f32[256,128]{1,0:T(8,128)S(1)} %collective-permute-done.1.refs_2_, f32[64,128]{1,0:T(8,128)S(1)} %collective-permute-done.5.refs_3_, ...), custom_call_target="tpu_custom_call" | custom-call | flops 2147483648 | bytes 20971520 | tf_op jit(solution)/shard_map/parent_step/pallas_call | solution.py:480
  50.0 0.0 copy-done.1
  50.0 2.2 %nest_steps.1 = f32[4,128,128]{2,1,0:T(8,128)} custom-call(s32[1,2]{1,0:T(1,128)S(1)} %copy-done.4, f32[7,48,128]{2,1,0:T(8,128)S(1)} %get-tuple-element.28.refs_5_.refs_1_, f32[7,48,128]{2,1,0:T(8,128)S(1)} %collective-permute-done.7.refs_2_, f32[7,48,128]{2,1,0:T(8,128)S(1)} %collective-permute-done.8.refs_3_, ...), custom_call_target="tpu_custom_call" | custom-call | flops 268435456 | bytes 6291456 | tf_op jit(solution)/shard_map/nest_steps/pallas_call | solution.py:480
  52.2 0.0 collective-permute-done.12.refs_6_
  52.2 0.0 collective-permute-done.11.refs_5_
  52.2 0.1 collective-permute-done.10.refs_4_
  52.3 3.6 %patch.1 = f32[64,256,128]{2,1,0:T(8,128)} custom-call(s32[1,2]{1,0:T(1,128)S(1)} %copy-done.4, f32[64,256,128]{2,1,0:T(8,128)} %get-tuple-element.32.refs_1_, f32[22,48,128]{2,1,0:T(8,128)S(1)} %own_feed.1.refs_5_.refs_2_, f32[7,48,128]{2,1,0:T(8,128)S(1)} %combine.1.refs_6_.refs_3_, ...), custom_call_target="tpu_custom_call", output_to_operand_aliasing={{}: (1, {})} | custom-call | bytes 2097152 | tf_op jit(solution)/shard_map/patch/pallas_call | solution.py:480
Async XLA Ops:
  0.6 13.3 %copy-start.5 = (f32[2,128]{1,0:T(2,128)S(1)}, f32[2,128]{1,0:T(2,128)}, u32[]{:S(2)}) copy-start(f32[2,128]{1,0:T(2,128)} %refs_8_.1) | copy-start | bytes 3076
  0.6 1.0 %copy-start = (f32[1,4,128,128]{3,2,1,0:T(8,128)S(1)}, f32[1,4,128,128]{3,2,1,0:T(8,128)}, u32[]{:S(2)}) copy-start(f32[1,4,128,128]{3,2,1,0:T(8,128)} %param.7) | copy-start | bytes 786436
  1.6 0.7 %copy-start.4 = (s32[1,2]{1,0:T(1,128)S(1)}, s32[1,2]{1,0:T(1,128)}, u32[]{:S(2)}) copy-start(s32[1,2]{1,0:T(1,128)} %refs_0_.15) | copy-start | bytes 28
  2.3 11.7 %copy-start.2 = (f32[128,128]{1,0:T(8,128)S(1)}, f32[128,128]{1,0:T(8,128)}, u32[]{:S(2)}) copy-start(f32[128,128]{1,0:T(8,128)} %refs_7_.1) | copy-start | bytes 196612
  4.5 37.4 %copy-start.3 = (f32[128,128]{1,0:T(8,128)S(1)}, f32[128,128]{1,0:T(8,128)}, u32[]{:S(2)}) copy-start(f32[128,128]{1,0:T(8,128)} %refs_5_.1) | copy-start | bytes 196612
  4.5 10.8 %collective-permute-start.2 = (f32[8,48,128]{2,1,0:T(8,128)S(1)}, f32[8,48,128]{2,1,0:T(8,128)S(1)}, u32[]{:S(2)}, u32[]{:S(2)}) collective-permute-start(f32[8,48,128]{2,1,0:T(8,128)S(1)} %get-tuple-element.23), channel_id=1, source_target_pairs={{0,32},{8,40},{16,48},{24,56},{32,64},{40,72},{48,80},{56,88},{64,... | collective-permute-start | bytes 589832 | tf_op jit(solution)/shard_map/ppermute | solution.py:515
  6.7 11.1 %collective-permute-start.3 = (f32[8,48,128]{2,1,0:T(8,128)S(1)}, f32[8,48,128]{2,1,0:T(8,128)S(1)}, u32[]{:S(2)}, u32[]{:S(2)}) collective-permute-start(f32[8,48,128]{2,1,0:T(8,128)S(1)} %get-tuple-element.24), channel_id=1, source_target_pairs={{0,64},{8,72},{16,80},{24,88},{32,96},{40,104},{48,112},{56,120},{... | collective-permute-start | bytes 589832 | tf_op jit(solution)/shard_map/ppermute | solution.py:515
  9.3 8.5 %collective-permute-start.4 = (f32[8,48,128]{2,1,0:T(8,128)S(1)}, f32[8,48,128]{2,1,0:T(8,128)S(1)}, u32[]{:S(2)}, u32[]{:S(2)}) collective-permute-start(f32[8,48,128]{2,1,0:T(8,128)S(1)} %get-tuple-element.25), channel_id=1, source_target_pairs={{0,96},{8,104},{16,112},{24,120},{32,0},{40,8},{48,16},{56,24},{64... | collective-permute-start | bytes 589832 | tf_op jit(solution)/shard_map/ppermute | solution.py:515
  10.4 15.2 %collective-permute-start = (f32[640,128]{1,0:T(8,128)S(1)}, f32[640,128]{1,0:T(8,128)S(1)}, u32[]{:S(2)}, u32[]{:S(2)}) collective-permute-start(f32[640,128]{1,0:T(8,128)S(1)} %get-tuple-element.18), channel_id=1, source_target_pairs={{0,8},{8,16},{16,24},{24,32},{32,40},{40,48},{48,56},{56,64},{64,7... | collective-permute-start | bytes 983048 | tf_op jit(solution)/shard_map/ppermute | solution.py:515
  18.5 12.7 %collective-permute-start.7 = (f32[7,48,128]{2,1,0:T(8,128)S(1)}, f32[7,48,128]{2,1,0:T(8,128)S(1)}, u32[]{:S(2)}, u32[]{:S(2)}) collective-permute-start(f32[7,48,128]{2,1,0:T(8,128)S(1)} %get-tuple-element.29), channel_id=1, source_target_pairs={{0,8},{8,16},{16,24},{24,0},{32,40},{40,48},{48,56},{56,32},{64,72... | collective-permute-start | bytes 516104 | tf_op jit(solution)/shard_map/ppermute | solution.py:515
  20.2 15.8 %collective-permute-start.8 = (f32[7,48,128]{2,1,0:T(8,128)S(1)}, f32[7,48,128]{2,1,0:T(8,128)S(1)}, u32[]{:S(2)}, u32[]{:S(2)}) collective-permute-start(f32[7,48,128]{2,1,0:T(8,128)S(1)} %get-tuple-element.30), channel_id=1, source_target_pairs={{0,16},{8,24},{16,0},{24,8},{32,48},{40,56},{48,32},{56,40},{64,80... | collective-permute-start | bytes 516104 | tf_op jit(solution)/shard_map/ppermute | solution.py:515
  23.6 12.5 %collective-permute-start.9 = (f32[7,48,128]{2,1,0:T(8,128)S(1)}, f32[7,48,128]{2,1,0:T(8,128)S(1)}, u32[]{:S(2)}, u32[]{:S(2)}) collective-permute-start(f32[7,48,128]{2,1,0:T(8,128)S(1)} %get-tuple-element.31), channel_id=1, source_target_pairs={{0,24},{8,0},{16,8},{24,16},{32,56},{40,32},{48,40},{56,48},{64,88... | collective-permute-start | bytes 516104 | tf_op jit(solution)/shard_map/ppermute | solution.py:515
  24.3 16.9 %collective-permute-start.1 = (f32[256,128]{1,0:T(8,128)S(1)}, f32[256,128]{1,0:T(8,128)S(1)}, u32[]{:S(2)}, u32[]{:S(2)}) collective-permute-start(f32[256,128]{1,0:T(8,128)S(1)} %get-tuple-element.19), channel_id=1, source_target_pairs={{8,0},{16,8},{24,16},{32,24},{40,32},{48,40},{56,48},{64,56},{72,6... | collective-permute-start | bytes 393224 | tf_op jit(solution)/shard_map/ppermute | solution.py:515
  25.6 16.3 %collective-permute-start.5 = (f32[64,128]{1,0:T(8,128)S(1)}, f32[64,128]{1,0:T(8,128)S(1)}, u32[]{:S(2)}, u32[]{:S(2)}) collective-permute-start(f32[64,128]{1,0:T(8,128)S(1)} %get-tuple-element.26), channel_id=1, source_target_pairs={{0,1},{1,2},{2,3},{3,4},{4,5},{5,6},{6,7},{8,9},{9,10},{10,11},{11... | collective-permute-start | bytes 98312 | tf_op jit(solution)/shard_map/ppermute | solution.py:556
  31.2 10.6 %collective-permute-start.6 = (f32[64,128]{1,0:T(8,128)S(1)}, f32[64,128]{1,0:T(8,128)S(1)}, u32[]{:S(2)}, u32[]{:S(2)}) collective-permute-start(f32[64,128]{1,0:T(8,128)S(1)} %get-tuple-element.27), channel_id=1, source_target_pairs={{1,0},{2,1},{3,2},{4,3},{5,4},{6,5},{7,6},{9,8},{10,9},{11,10},{12... | collective-permute-start | bytes 98312 | tf_op jit(solution)/shard_map/ppermute | solution.py:557
  33.2 16.9 %copy-start.1 = (f32[1,4,128,128]{3,2,1,0:T(8,128)S(1)}, f32[1,4,128,128]{3,2,1,0:T(8,128)}, u32[]{:S(2)}) copy-start(f32[1,4,128,128]{3,2,1,0:T(8,128)} %param.7) | copy-start | bytes 786436
  36.8 15.4 %collective-permute-start.12 = (f32[7,48,128]{2,1,0:T(8,128)S(1)}, f32[7,48,128]{2,1,0:T(8,128)S(1)}, u32[]{:S(2)}, u32[]{:S(2)}) collective-permute-start(f32[7,48,128]{2,1,0:T(8,128)S(1)} %combine.1.refs_6_.refs_3_), channel_id=1, source_target_pairs={{0,96},{8,104},{16,112},{24,120},{32,0},{40,8},{48,16},{56,24},{64... | collective-permute-start | bytes 516104 | tf_op jit(solution)/shard_map/ppermute | solution.py:515
  40.8 11.4 %collective-permute-start.11 = (f32[7,48,128]{2,1,0:T(8,128)S(1)}, f32[7,48,128]{2,1,0:T(8,128)S(1)}, u32[]{:S(2)}, u32[]{:S(2)}) collective-permute-start(f32[7,48,128]{2,1,0:T(8,128)S(1)} %combine.1.refs_6_.refs_3_), channel_id=1, source_target_pairs={{0,64},{8,72},{16,80},{24,88},{32,96},{40,104},{48,112},{56,120},{... | collective-permute-start | bytes 516104 | tf_op jit(solution)/shard_map/ppermute | solution.py:515
  41.2 11.1 %collective-permute-start.10 = (f32[7,48,128]{2,1,0:T(8,128)S(1)}, f32[7,48,128]{2,1,0:T(8,128)S(1)}, u32[]{:S(2)}, u32[]{:S(2)}) collective-permute-start(f32[7,48,128]{2,1,0:T(8,128)S(1)} %combine.1.refs_6_.refs_3_), channel_id=1, source_target_pairs={{0,32},{8,40},{16,48},{24,56},{32,64},{40,72},{48,80},{56,88},{64,... | collective-permute-start | bytes 516104 | tf_op jit(solution)/shard_map/ppermute | solution.py:515

commit v3 on v2

--- a/solution.py
+++ b/solution.py
@@ -72,7 +72,7 @@
     return owner, jnp.clip(row - base - begin, 0, GROUP_ROWS - 1)
 
 
-def pack_kernel(tile_rows, tile_cols, nest_rows, pos, parent, nest, b0, b1, b2, b3, west, east, down, up, band, cols, sems):
+def pack_kernel(tile_rows, tile_cols, nest_rows, pos, parent, b0, b1, b2, b3, west, east, down, up, band, cols, sems):
     tile = lax.axis_index("tiles")
     line = lax.axis_index("nests")
     my_y = lax.div(tile, jnp.int32(SIDE))
@@ -89,22 +89,12 @@
                 parent.at[pl.ds(begin, GROUP_ROWS), pl.ds(aligned, WIDE)], band.at[k], sems.at[k]
             )
         )
-    halo = 3
     others = [
         pltpu.make_async_copy(parent.at[:, pl.ds(0, 8)], cols.at[0], sems.at[4]),
         pltpu.make_async_copy(parent.at[:, pl.ds(tile_cols - 8, 8)], cols.at[1], sems.at[5]),
-        pltpu.make_async_copy(parent.at[tile_rows - 1], down.at[pl.ds(0, tile_cols)], sems.at[6]),
+        pltpu.make_async_copy(parent.at[tile_rows - 1], down, sems.at[6]),
         pltpu.make_async_copy(parent.at[0], up, sems.at[7]),
     ]
-    nest_cols = nest.shape[1]
-    for r in range(halo):
-        others.append(
-            pltpu.make_async_copy(
-                nest.at[nest_rows - halo + r],
-                down.at[pl.ds(tile_cols + r * nest_cols, nest_cols)],
-                sems.at[8 + r],
-            )
-        )
     for copy in copies + others:
         copy.start()
     for k, out in enumerate((b0, b1, b2, b3)):
@@ -136,7 +126,7 @@
             out[DEV_ROWS + s] = fed[s]
 
 
-def nest_kernel(tile_rows, tile_cols, pos, r0, r1, r2, r3, state, down, nest_mix, courant, out, lines, start, cur):
+def nest_kernel(tile_rows, tile_cols, pos, r0, r1, r2, r3, state, tail, nest_mix, courant, out, lines, start, cur):
     tile = lax.axis_index("tiles")
     my_y, my_z = lax.div(tile, jnp.int32(SIDE)), lax.rem(tile, jnp.int32(SIDE))
     nest_rows, ncols, width = state.shape
@@ -163,7 +153,7 @@
         near_row = jnp.clip(third(at) - top, 0, DEV_ROWS - 2)
         part = lax.rem(at, jnp.int32(3)).astype(F32)
         interp = (3.0 - part) * lines[near_row] + part * lines[near_row + 1]
-        own = state[x] if x >= 0 else down[pl.ds(tile_cols + (x + halo) * ncols, ncols), :]
+        own = state[x] if x >= 0 else tail[x + halo]
         start[x + halo] = 0.5 * (own + interp * (1.0 / 9.0))
     first = tile == 0
 
@@ -194,11 +184,12 @@
     return third(value + 2)
 
 
-def feed_kernel(pos, state, nest_mix, courant, fb, start, cur):
+def feed_kernel(pos, state, nest_mix, courant, fb, tail, start, cur):
     tile = lax.axis_index("tiles")
     nest_rows, ncols, width = state.shape
     rows = nest_rows + STEPS
     ox, oy = pos[0, 0], pos[0, 1]
+    tail[...] = state[nest_rows - STEPS :]
     for x in range(rows):
         start[x] = 0.5 * state[x] if x < nest_rows else jnp.zeros((ncols, width), F32)
     above = jnp.where(tile == 0, start[0], 0.0)
@@ -373,7 +364,7 @@
             out[w, 0:1, :] = edges[C + w : C + w + 1]
 
 
-def patch_kernel(tile_rows, tile_cols, nest_rows, ncols, pos, parent, own, g0, g1, g2, g3, out, buf, sems):
+def patch_kernel(tile_rows, tile_cols, nest_rows, ncols, pos, parent, own, kept, g0, g1, g2, g3, out, buf, sems):
     total = nest_rows * SIDE * SIDE
     owns, first_row, begin, aligned, shift, rem_y = window(pos, tile_rows, tile_cols, total)
     my_y = lax.div(lax.axis_index("tiles"), jnp.int32(SIDE))
@@ -383,9 +374,7 @@
     @pl.when(owns)
     def _():
         place = (pl.ds(begin, FB_WINDOW), pl.ds(aligned, WIDE))
-        copy = pltpu.make_async_copy(parent.at[place], buf, sems.at[0])
-        copy.start()
-        copy.wait()
+        buf[...] = kept[...]
         live = rem_y + 3 * lax.broadcasted_iota(jnp.int32, (C, buf.shape[2]), 0) < ncols
 
         @pl.loop(0, FB_WINDOW)
@@ -406,56 +395,58 @@
                 old = buf[w, pl.ds(shift, C), :]
                 buf[w, pl.ds(shift, C), :] = jnp.where(live, 0.5 * (old + value), old)
 
-        back = pltpu.make_async_copy(buf, out.at[place], sems.at[1])
+        back = pltpu.make_async_copy(buf, out.at[place], sems.at[0])
         back.start()
         back.wait()
 
 
-def parent_kernel(rows, parent, from_up, from_down, west, east, parent_mix, out, token, full, done, weights, in_sems, out_sems):
+def parent_kernel(
+    rows, total, pos, parent, from_up, from_down, west, east, parent_mix, out, kept, token, done, weights, out_sems
+):
     height, cols = parent.shape[0], parent.shape[1]
-    count = height // rows
-
-    def fetch(i):
-        return pltpu.make_async_copy(
-            parent.at[pl.ds(i * rows, rows)], full.at[pl.ds(1 + i * rows, rows)], in_sems.at[i]
-        )
+    count, slots = height // rows, done.shape[0]
+    owns, _, begin, aligned, _, _ = window(pos, height, cols, total)
 
     def store(i):
-        slot = lax.rem(i, 2)
+        slot = lax.rem(i, slots)
         return pltpu.make_async_copy(done.at[slot], out.at[pl.ds(i * rows, rows)], out_sems.at[slot])
 
-    for i in range(count):
-        fetch(i).start()
     size = parent_mix.shape[0]
     weights[...] = wide_weights(parent_mix[...] + jnp.where(eye(size), 1.0 - 4.0 * KAPPA, 0.0))
-    full[0] = from_up[pl.ds(0, cols), :]
-    full[height + 1] = from_down[...]
     index = lax.broadcasted_iota(jnp.int32, (cols, size), 0)
     low_edge, high_edge = index == 0, index == cols - 1
-    fetch(0).wait()
 
     @pl.loop(0, count)
     def _(i):
-        @pl.when(i + 1 < count)
+        @pl.when(i >= slots)
         def _():
-            fetch(i + 1).wait()
-
-        @pl.when(i >= 2)
-        def _():
-            store(i - 2).wait()
-
-        slot = lax.rem(i, 2)
+            store(i - slots).wait()
+
+        slot = lax.rem(i, slots)
         for r in range(rows):
             at = i * rows + r
-            value = full[at + 1]
+            value = parent[at]
+            upper = parent[at - 1] if r else jnp.where(i == 0, from_up[...], parent[jnp.maximum(at - 1, 0)])
+            if r < rows - 1:
+                lower = parent[at + 1]
+            else:
+                lower = jnp.where(i == count - 1, from_down[...], parent[jnp.minimum(at + 1, height - 1)])
             left = jnp.where(low_edge, west[pl.ds(at, 1), :], pltpu.roll(value, 1, 0))
             right = jnp.where(high_edge, east[pl.ds(at, 1), :], pltpu.roll(value, cols - 1, 0))
-            beside = (full[at] + full[at + 2]) + (left + right)
-            done[slot, r] = mix(value, weights[...]) + KAPPA * beside
+            done[slot, r] = mix(value, weights[...]) + KAPPA * ((upper + lower) + (left + right))
         store(i).start()
 
-    store(count - 2).wait()
-    store(count - 1).wait()
+        @pl.when(owns & (i * rows < begin + FB_WINDOW) & (i * rows + rows > begin))
+        def _():
+            for r in range(rows):
+                at = i * rows + r - begin
+
+                @pl.when((at >= 0) & (at < FB_WINDOW))
+                def _(r=r, at=at):
+                    kept[at] = done[slot, r, pl.ds(aligned, WIDE), :]
+
+    for k in range(slots):
+        store(count - slots + k).wait()
     token[...] = jnp.zeros(token.shape, F32)
 
 
@@ -471,7 +462,7 @@
     return pl.BlockSpec(memory_space=pltpu.HBM)
 
 
-def run(name, kernel, ins, outs, scratch=(), after=(), room=50, flops=0, moved=1, **options):
+def run(name, kernel, ins, outs, scratch=(), after=(), room=44, flops=0, moved=1, **options):
     given, held = len(ins), len(after)
 
     def body(*refs):
@@ -506,7 +497,7 @@
     count = SIDE * SIDE
     lines = lax.axis_size("nests")
     S, V, H = smem(), vmem(), hbm()
-    big = 50
+    big, mid = 52, 44
 
     def f(*shape):
         return jax.ShapeDtypeStruct(shape, F32)
@@ -517,15 +508,16 @@
     packed = run(
         "pack",
         functools.partial(pack_kernel, tile_rows, tile_cols, nest_rows),
-        [(S, nest_pos), (H, parent), (H, state)],
+        [(S, nest_pos), (H, parent)],
         [(V, f(GROUP_ROWS, C, width))] * SIDE
         + [(V, f(tile_rows, width))] * 2
-        + [(V, f(tile_cols + STEPS * ncols, width)), (V, f(tile_cols, width))],
+        + [(V, f(tile_cols, width))] * 2,
         [
             pltpu.VMEM((SIDE, GROUP_ROWS, WIDE, width), F32),
             pltpu.VMEM((2, tile_rows, 8, width), F32),
-            pltpu.SemaphoreType.DMA((11,)),
+            pltpu.SemaphoreType.DMA((8,)),
         ],
+        room=big,
         moved=4,
     )
     b, (west_out, east_out, down_out, up_out) = packed[:4], packed[4:]
@@ -533,11 +525,11 @@
     from_up = on_tiles(down_out, [(i, i + 1) for i in range(count - 1)])
     from_down = on_tiles(up_out, [(i + 1, i) for i in range(count - 1)])
 
-    (fed,) = run(
+    fed, tail = run(
         "feed",
         feed_kernel,
         [(S, nest_pos), (V, state), (V, nest_mix), (V, courant)],
-        [(V, f(FB_SLOTS, C, width))],
+        [(V, f(FB_SLOTS, C, width)), (V, f(STEPS, ncols, width))],
         [
             pltpu.VMEM((nest_rows + STEPS, ncols, width), F32),
             pltpu.VMEM((STEPS - 1, nest_rows + STEPS, ncols, width), F32),
@@ -551,6 +543,7 @@
         functools.partial(pick_kernel, tile_rows, nest_rows),
         [(S, nest_pos)] + [(V, x) for x in (fed, west_out, east_out, b[0], got[1], got[2], got[3])],
         [(V, f(DEV_ROWS + FB_SLOTS, C, width))] * SIDE + [(V, f(tile_rows, width))] * 2,
+        after=[from_up, from_down],
     )
     mine = {k: on_tiles(picked[k], z_route(k)) for k in (1, 3, 2)}
     west = lax.ppermute(picked[5], "nests", [(i, i + 1) for i in range(lines - 1)])
@@ -577,31 +570,31 @@
         after=[own],
     )
     groups = {k: on_tiles(joined, y_route(k)) for k in (1, 3, 2)}
+    tail, _ = lax.optimization_barrier((tail, joined))
+    tail_in = on_tiles(tail, [(i, i + 1) for i in range(count - 1)])
 
     rows = 8
-    parent_new, token = run(
+    parent_new, kept, token = run(
         "parent_step",
-        functools.partial(parent_kernel, rows),
-        [(H, parent)] + [(V, x) for x in (from_up, from_down, west, east, parent_mix)],
-        [(H, f(tile_rows, tile_cols, width)), (V, f(8, width))],
+        functools.partial(parent_kernel, rows, total),
+        [(S, nest_pos), (V, parent)] + [(V, x) for x in (from_up, from_down, west, east, parent_mix)],
+        [(H, f(tile_rows, tile_cols, width)), (V, f(FB_WINDOW, WIDE, width)), (V, f(8, width))],
         [
-            pltpu.VMEM((tile_rows + 2, tile_cols, width), F32),
-            pltpu.VMEM((2, rows, tile_cols, width), F32),
+            pltpu.VMEM((4, rows, tile_cols, width), F32),
             pltpu.VMEM((2 * width, 2 * width), BF16),
-            pltpu.SemaphoreType.DMA((tile_rows // rows,)),
-            pltpu.SemaphoreType.DMA((2,)),
+            pltpu.SemaphoreType.DMA((4,)),
         ],
         after=[joined],
-        room=big,
+        room=mid,
         flops=2 * tile_rows * tile_cols * 256 * 256,
-        moved=20,
+        moved=10,
     )
     (nest_out,) = run(
         "nest_steps",
         functools.partial(nest_kernel, tile_rows, tile_cols),
         [(S, nest_pos), (V, picked[0])]
         + [(V, mine[k]) for k in (1, 2, 3)]
-        + [(V, x) for x in (state, from_up, nest_mix, courant)],
+        + [(V, x) for x in (state, tail_in, nest_mix, courant)],
         [(V, f(nest_rows, ncols, width))],
         [
             pltpu.VMEM((DEV_ROWS, ncols, width), F32),
@@ -615,9 +608,9 @@
     (parent_out,) = run(
         "patch",
         functools.partial(patch_kernel, tile_rows, tile_cols, nest_rows, ncols),
-        [(S, nest_pos), (H, parent_new), (V, own), (V, joined)] + [(V, groups[k]) for k in (1, 2, 3)],
+        [(S, nest_pos), (H, parent_new), (V, own), (V, kept), (V, joined)] + [(V, groups[k]) for k in (1, 2, 3)],
         [(H, f(tile_rows, tile_cols, width))],
-        [pltpu.VMEM((FB_WINDOW, WIDE, width), F32), pltpu.SemaphoreType.DMA((2,))],
+        [pltpu.VMEM((FB_WINDOW, WIDE, width), F32), pltpu.SemaphoreType.DMA((1,))],
         room=big,
         moved=2,
         input_output_aliases={1: 0},

time: 56.3 us -> 54.3 us (0.964)
  Pallas kernels: 21.9 us -> 18.6 us
  local copies, waits for them, and re-layouts: 1.62 us -> 3.44 us
    pallas_call x8, Pallas kernels: 21.9 us -> 18.6 us  [run(): pl.pallas_call(body, out_shape=[shape for _, shape in outs], in_specs=[sp...]
    unnamed x12 -> x18, local copies, waits for them, and re-layouts: 1.62 us -> 3.44 us
    ppermute x11 -> x12, starting transfers between devices: 21.5 us -> 20 us  [on_tiles(): return lax.ppermute(block, 'tiles', route)]
    ppermute x1, starting transfers between devices: 5.63 us -> 6.72 us  [shards(): lax.ppermute(picked[5], 'nests', [(i, i + 1) for i in range(lines - 1)])]
    ppermute x11 -> x12, waiting for transfers between devices: 2.58 us -> 2.38 us  [on_tiles(): return lax.ppermute(block, 'tiles', route)]
  transfers between devices with their start and end apart: 13 -> 14, of which waited for: 2 -> 2; matrix products, arithmetic and copies ran while one was open for 0% -> 0% of each run, Pallas kernels for 29% -> 25%
where the time goes in v3:
time: 54.3 us; the launch traced here: 53.9 us
  starting transfers between devices  28.6 us (53%)
  Pallas kernels  18.6 us (34%)
  local copies, waits for them, and re-layouts  3.44 us (6%)
  waiting for transfers between devices  2.39 us (4%)
  between operations  0.88 us (2%)
    ppermute x12, starting transfers between devices, on_tiles(): return lax.ppermute(block, 'tiles', route)  20 us
    pallas_call x8, Pallas kernels, run(): pl.pallas_call(body, out_shape=[shape for _, shape in outs], in_specs=[sp...  18.6 us
    ppermute x1, starting transfers between devices, shards(): lax.ppermute(picked[5], 'nests', [(i, i + 1) for i in range(lines - 1)])  6.72 us
    unnamed x18, local copies, waits for them, and re-layouts  3.44 us
    ppermute x12, waiting for transfers between devices, on_tiles(): return lax.ppermute(block, 'tiles', route)  2.38 us
    ppermute x1, starting transfers between devices, shards(): lax.ppermute(picked[4], 'nests', [(i + 1, i) for i in range(lines - 1)])  1.92 us
  transfers between devices with their start and end apart: 14, of which 2 were waited for; matrix products, arithmetic and copies ran while one was open for 0% of the time, Pallas kernels for 25%

profile of v3, /device:TPU:1, one launch (start us, length us, event | category | flops | bytes accessed | tf_op | source)
XLA Modules:
  0.0 53.9 jit_solution(11030648704896065977)
XLA Ops:
  0.6 0.0 copy-start
  0.6 0.0 copy-start.7
  0.6 0.8 %copy-done.7 = s32[1,2]{1,0:T(1,128)S(1)} copy-done((s32[1,2]{1,0:T(1,128)S(1)}, s32[1,2]{1,0:T(1,128)}, u32[]{:S(2)}) %copy-start.7) | copy-done | bytes 32
  1.4 0.0 copy-start.8
  1.4 2.3 %pack.1 = (f32[8,48,128]{2,1,0:T(8,128)S(1)}, f32[8,48,128]{2,1,0:T(8,128)S(1)}, f32[8,48,128]{2,1,0:T(8,128)S(1)}, f32[8,48,128]{2,1,0:T(8,128)S(1)}, f32[64,12...) custom-call(s32[1,2]{1,0:T(1,128)S(1)} %copy-done.7, ...), custom_call_target="tpu_custom_call" | custom-call | bytes 4194304 | tf_op jit(solution)/shard_map/pack/pallas_call | solution.py:471
  3.8 2.2 %collective-permute-start.2 = (f32[8,48,128]{2,1,0:T(8,128)S(1)}, f32[8,48,128]{2,1,0:T(8,128)S(1)}, u32[]{:S(2)}, u32[]{:S(2)}) collective-permute-start(f32[8,48,128]{2,1,0:T(8,128)S(1)} %get-tuple-element.28), channel_id=1, source_target_pairs={{0,32},{8,40},{16,48},{24,56},{32,64},{40,72},{48,80},{56,88},{64,... | collective-permute-start | bytes 589832 | tf_op jit(solution)/shard_map/ppermute | solution.py:506
  6.0 2.6 %collective-permute-start.3 = (f32[8,48,128]{2,1,0:T(8,128)S(1)}, f32[8,48,128]{2,1,0:T(8,128)S(1)}, u32[]{:S(2)}, u32[]{:S(2)}) collective-permute-start(f32[8,48,128]{2,1,0:T(8,128)S(1)} %get-tuple-element.29), channel_id=1, source_target_pairs={{0,64},{8,72},{16,80},{24,88},{32,96},{40,104},{48,112},{56,120},{... | collective-permute-start | bytes 589832 | tf_op jit(solution)/shard_map/ppermute | solution.py:506
  8.6 1.1 %collective-permute-start.4 = (f32[8,48,128]{2,1,0:T(8,128)S(1)}, f32[8,48,128]{2,1,0:T(8,128)S(1)}, u32[]{:S(2)}, u32[]{:S(2)}) collective-permute-start(f32[8,48,128]{2,1,0:T(8,128)S(1)} %get-tuple-element.30), channel_id=1, source_target_pairs={{0,96},{8,104},{16,112},{24,120},{32,0},{40,8},{48,16},{56,24},{64... | collective-permute-start | bytes 589832 | tf_op jit(solution)/shard_map/ppermute | solution.py:506
  9.7 3.5 %collective-permute-start = (f32[256,128]{1,0:T(8,128)S(1)}, f32[256,128]{1,0:T(8,128)S(1)}, u32[]{:S(2)}, u32[]{:S(2)}) collective-permute-start(f32[256,128]{1,0:T(8,128)S(1)} %get-tuple-element.22), channel_id=1, source_target_pairs={{0,8},{8,16},{16,24},{24,32},{32,40},{40,48},{48,56},{56,64},{64,7... | collective-permute-start | bytes 393224 | tf_op jit(solution)/shard_map/ppermute | solution.py:506
  13.2 1.3 %collective-permute-start.1 = (f32[256,128]{1,0:T(8,128)S(1)}, f32[256,128]{1,0:T(8,128)S(1)}, u32[]{:S(2)}, u32[]{:S(2)}) collective-permute-start(f32[256,128]{1,0:T(8,128)S(1)} %get-tuple-element.23), channel_id=1, source_target_pairs={{8,0},{16,8},{24,16},{32,24},{40,32},{48,40},{56,48},{64,56},{72,6... | collective-permute-start | bytes 393224 | tf_op jit(solution)/shard_map/ppermute | solution.py:506
  14.5 0.0 copy-done.8
  14.5 0.0 copy-start.1
  14.5 0.8 %copy-done.1 = f32[128,128]{1,0:T(8,128)S(1)} copy-done((f32[128,128]{1,0:T(8,128)S(1)}, f32[128,128]{1,0:T(8,128)}, u32[]{:S(2)}) %copy-start.1) | copy-done | bytes 65560
  15.4 0.0 copy-start.4
  15.4 0.9 %copy-done.4 = f32[1,4,128,128]{3,2,1,0:T(8,128)S(1)} copy-done((f32[1,4,128,128]{3,2,1,0:T(8,128)S(1)}, f32[1,4,128,128]{3,2,1,0:T(8,128)}, u32[]{:S(2)}) %copy-start.4) | copy-done | bytes 262168
  16.3 0.0 copy-start.6
  16.3 1.4 %feed.1 = (f32[3,48,128]{2,1,0:T(8,128)S(1)}, f32[3,128,128]{2,1,0:T(8,128)S(1)}) custom-call(s32[1,2]{1,0:T(1,128)S(1)} %copy-done.7, f32[4,128,128]{2,1,0:T(8,128)S(1)} %bitcast.2, f32[128,128]{1,0:T(8,128)S(1)} %copy-done.1, f32[2,128]{1,0:T(2,128)S(1)} %copy-done.8, f32[64,128]{1,0:T(8,128)S(1)} %get-tuple-element.24.refs_4_.refs_2_), custom_call_target="tpu_custom_call" | custom-call | flops 268435456 | bytes 4194304 | tf_op jit(solution)/shard_map/feed/pallas_call | solution.py:471
  17.7 0.0 collective-permute-done.refs_8_.refs_2_
  17.7 1.4 %collective-permute-done.1.refs_9_.refs_3_ = f32[256,128]{1,0:T(8,128)S(1)} collective-permute-done((f32[256,128]{1,0:T(8,128)S(1)}, f32[256,128]{1,0:T(8,128)S(1)}, u32[]{:S(2)}, u32[]{:S(2)}) %collective-permute-start.1) | collective-permute-done | bytes 131104 | tf_op jit(solution)/shard_map/ppermute | solution.py:506
  19.1 0.0 collective-permute-done.2.refs_5_
  19.1 0.0 collective-permute-done.3.refs_6_
  19.1 0.0 collective-permute-done.4.refs_7_
  19.1 0.8 %pick.1 = (f32[7,48,128]{2,1,0:T(8,128)S(1)}, f32[7,48,128]{2,1,0:T(8,128)S(1)}, f32[7,48,128]{2,1,0:T(8,128)S(1)}, f32[7,48,128]{2,1,0:T(8,128)S(1)}, f32[64,128]{1,0:T(8,128)S(1)}, /*index=5*/f32[64,128]{1,0:T(8,128)S(1)}) custom-call(s32[1,2]{1,0:T(1,128)S(1)} %copy-done.7, f32[3,48,128]{2,1,0:T(8,128)S(1)} %get-tuple-element.25.refs_1_, ...), custom_call_target="tpu_custom_call" | custom-call | bytes 1048576 | tf_op jit(solution)/shard_map/pick/pallas_call | solution.py:471
  19.9 1.5 %collective-permute-start.7 = (f32[7,48,128]{2,1,0:T(8,128)S(1)}, f32[7,48,128]{2,1,0:T(8,128)S(1)}, u32[]{:S(2)}, u32[]{:S(2)}) collective-permute-start(f32[7,48,128]{2,1,0:T(8,128)S(1)} %get-tuple-element.34), channel_id=1, source_target_pairs={{0,8},{8,16},{16,24},{24,0},{32,40},{40,48},{48,56},{56,32},{64,72... | collective-permute-start | bytes 516104 | tf_op jit(solution)/shard_map/ppermute | solution.py:506
  21.4 3.8 %collective-permute-start.8 = (f32[7,48,128]{2,1,0:T(8,128)S(1)}, f32[7,48,128]{2,1,0:T(8,128)S(1)}, u32[]{:S(2)}, u32[]{:S(2)}) collective-permute-start(f32[7,48,128]{2,1,0:T(8,128)S(1)} %get-tuple-element.35), channel_id=1, source_target_pairs={{0,16},{8,24},{16,0},{24,8},{32,48},{40,56},{48,32},{56,40},{64,80... | collective-permute-start | bytes 516104 | tf_op jit(solution)/shard_map/ppermute | solution.py:506
  25.2 0.0 collective-permute-start.9
  25.2 6.7 %collective-permute-start.5 = (f32[64,128]{1,0:T(8,128)S(1)}, f32[64,128]{1,0:T(8,128)S(1)}, u32[]{:S(2)}, u32[]{:S(2)}) collective-permute-start(f32[64,128]{1,0:T(8,128)S(1)} %get-tuple-element.31), channel_id=1, source_target_pairs={{0,1},{1,2},{2,3},{3,4},{4,5},{5,6},{6,7},{8,9},{9,10},{10,11},{11... | collective-permute-start | bytes 98312 | tf_op jit(solution)/shard_map/ppermute | solution.py:549
  31.9 1.9 %collective-permute-start.6 = (f32[64,128]{1,0:T(8,128)S(1)}, f32[64,128]{1,0:T(8,128)S(1)}, u32[]{:S(2)}, u32[]{:S(2)}) collective-permute-start(f32[64,128]{1,0:T(8,128)S(1)} %get-tuple-element.32), channel_id=1, source_target_pairs={{1,0},{2,1},{3,2},{4,3},{5,4},{6,5},{7,6},{9,8},{10,9},{11,10},{12... | collective-permute-start | bytes 98312 | tf_op jit(solution)/shard_map/ppermute | solution.py:550
  33.9 0.0 copy-done
  33.9 0.0 copy-start.2
  33.9 0.8 %copy-done.2 = f32[128,128]{1,0:T(8,128)S(1)} copy-done((f32[128,128]{1,0:T(8,128)S(1)}, f32[128,128]{1,0:T(8,128)}, u32[]{:S(2)}) %copy-start.2) | copy-done | bytes 65560
  34.7 2.0 %own_feed.1.refs_5_.refs_2_ = f32[22,48,128]{2,1,0:T(8,128)S(1)} custom-call(s32[1,2]{1,0:T(1,128)S(1)} %copy-done.7, f32[64,256,128]{2,1,0:T(8,128)S(1)} %copy-done, f32[256,128]{1,0:T(8,128)S(1)} %collective-permute-done.refs_8_.refs_2_, f32[128,128]{1,0:T(8,128)S(1)} %copy-done.2, f32[2,128]{1,0:T(2,128)S(1)} %copy-done.8, ...), custom_call_target="tpu_custom_call" | custom-call | flops 1073741824 | bytes 8388608 | tf_op jit(solution)/shard_map/own_feed/pallas_call | solution.py:471
  36.8 0.0 collective-permute-done.7.refs_2_
  36.8 0.0 collective-permute-done.8.refs_3_
  36.8 0.0 collective-permute-done.9.refs_4_
  36.8 0.7 %combine.1.refs_7_.refs_4_ = f32[7,48,128]{2,1,0:T(8,128)S(1)} custom-call(s32[1,2]{1,0:T(1,128)S(1)} %copy-done.7, f32[7,48,128]{2,1,0:T(8,128)S(1)} %get-tuple-element.33.refs_5_.refs_1_, f32[7,48,128]{2,1,0:T(8,128)S(1)} %collective-permute-done.7.refs_2_, f32[7,48,128]{2,1,0:T(8,128)S(1)} %collective-permute-done.8.refs_3_, ...), custom_call_target="tpu_custom_call" | custom-call | bytes 1048576 | tf_op jit(solution)/shard_map/combine/pallas_call | solution.py:471
  37.5 0.1 collective-permute-start.12
  37.6 0.7 %collective-permute-start.11 = (f32[7,48,128]{2,1,0:T(8,128)S(1)}, f32[7,48,128]{2,1,0:T(8,128)S(1)}, u32[]{:S(2)}, u32[]{:S(2)}) collective-permute-start(f32[7,48,128]{2,1,0:T(8,128)S(1)} %combine.1.refs_7_.refs_4_), channel_id=1, source_target_pairs={{0,64},{8,72},{16,80},{24,88},{32,96},{40,104},{48,112},{56,120},{... | collective-permute-start | bytes 516104 | tf_op jit(solution)/shard_map/ppermute | solution.py:506
  38.3 0.7 %collective-permute-start.10 = (f32[7,48,128]{2,1,0:T(8,128)S(1)}, f32[7,48,128]{2,1,0:T(8,128)S(1)}, u32[]{:S(2)}, u32[]{:S(2)}) collective-permute-start(f32[7,48,128]{2,1,0:T(8,128)S(1)} %combine.1.refs_7_.refs_4_), channel_id=1, source_target_pairs={{0,32},{8,40},{16,48},{24,56},{32,64},{40,72},{48,80},{56,88},{64,... | collective-permute-start | bytes 516104 | tf_op jit(solution)/shard_map/ppermute | solution.py:506
  39.0 0.0 collective-permute-done.5.refs_4_
  39.0 2.4 %collective-permute-start.13 = (f32[3,128,128]{2,1,0:T(8,128)S(1)}, f32[3,128,128]{2,1,0:T(8,128)S(1)}, u32[]{:S(2)}, u32[]{:S(2)}) collective-permute-start(f32[3,128,128]{2,1,0:T(8,128)S(1)} %get-tuple-element.40), channel_id=1, source_target_pairs={{0,8},{8,16},{16,24},{24,32},{32,40},{40,48},{48,56},{56,64},{64,7... | collective-permute-start | bytes 589832 | tf_op jit(solution)/shard_map/ppermute | solution.py:506
  41.4 0.0 collective-permute-done.6.refs_5_
  41.5 0.0 copy-done.6
  41.5 6.7 %parent_step.1 = (f32[64,256,128]{2,1,0:T(8,128)}, f32[22,56,128]{2,1,0:T(8,128)S(1)}, f32[8,128]{1,0:T(8,128)S(1)}) custom-call(s32[1,2]{1,0:T(1,128)S(1)} %copy-done.7, f32[64,256,128]{2,1,0:T(8,128)S(1)} %copy-done, f32[256,128]{1,0:T(8,128)S(1)} %collective-permute-done.refs_8_.refs_2_, f32[256,128]{1,0:T(8,128)S(1)} %collective-permute-done.1.refs_9_.refs_3_, ...), custom_call_target="tpu_custom_call" | custom-call | flops 2147483648 | bytes 10485760 | tf_op jit(solution)/shard_map/parent_step/pallas_call | solution.py:471
  48.2 0.0 collective-permute-done.12.refs_7_
  48.2 0.0 collective-permute-done.11.refs_6_
  48.2 1.0 %collective-permute-done.10.refs_5_ = f32[7,48,128]{2,1,0:T(8,128)S(1)} collective-permute-done((f32[7,48,128]{2,1,0:T(8,128)S(1)}, f32[7,48,128]{2,1,0:T(8,128)S(1)}, u32[]{:S(2)}, u32[]{:S(2)}) %collective-permute-start.10) | collective-permute-done | bytes 172064 | tf_op jit(solution)/shard_map/ppermute | solution.py:506
  49.2 0.0 copy-start.3
  49.2 0.0 copy-start.5
  49.2 2.5 %patch.1 = f32[64,256,128]{2,1,0:T(8,128)} custom-call(s32[1,2]{1,0:T(1,128)S(1)} %copy-done.7, f32[64,256,128]{2,1,0:T(8,128)} %get-tuple-element.37.refs_1_, f32[22,48,128]{2,1,0:T(8,128)S(1)} %own_feed.1.refs_5_.refs_2_, f32[22,56,128]{2,1,0:T(8,128)S(1)} %get-tuple-element.38.refs_3_, ...), custom_call_target="tpu_custom_call", output_to_operand_aliasing={{}: (1, {})} | custom-call | bytes 2097152 | tf_op jit(solution)/shard_map/patch/pallas_call | solution.py:471
  51.7 0.0 collective-permute-done.13.refs_6_
  51.7 0.0 copy-done.3
  51.7 0.0 copy-done.5
  51.8 2.2 %nest_steps.1 = f32[4,128,128]{2,1,0:T(8,128)} custom-call(s32[1,2]{1,0:T(1,128)S(1)} %copy-done.7, f32[7,48,128]{2,1,0:T(8,128)S(1)} %get-tuple-element.33.refs_5_.refs_1_, f32[7,48,128]{2,1,0:T(8,128)S(1)} %collective-permute-done.7.refs_2_, f32[7,48,128]{2,1,0:T(8,128)S(1)} %collective-permute-done.8.refs_3_, ...), custom_call_target="tpu_custom_call" | custom-call | flops 268435456 | bytes 6291456 | tf_op jit(solution)/shard_map/nest_steps/pallas_call | solution.py:471
Async XLA Ops:
  0.6 33.2 %copy-start = (f32[64,256,128]{2,1,0:T(8,128)S(1)}, f32[64,256,128]{2,1,0:T(8,128)}, u32[]{:S(2)}) copy-start(f32[64,256,128]{2,1,0:T(8,128)} %refs_1_.5) | copy-start | bytes 25165828
  0.6 0.8 %copy-start.7 = (s32[1,2]{1,0:T(1,128)S(1)}, s32[1,2]{1,0:T(1,128)}, u32[]{:S(2)}) copy-start(s32[1,2]{1,0:T(1,128)} %refs_0_.15) | copy-start | bytes 28
  1.4 13.1 %copy-start.8 = (f32[2,128]{1,0:T(2,128)S(1)}, f32[2,128]{1,0:T(2,128)}, u32[]{:S(2)}) copy-start(f32[2,128]{1,0:T(2,128)} %refs_8_.1) | copy-start | bytes 3076
  3.8 15.3 %collective-permute-start.2 = (f32[8,48,128]{2,1,0:T(8,128)S(1)}, f32[8,48,128]{2,1,0:T(8,128)S(1)}, u32[]{:S(2)}, u32[]{:S(2)}) collective-permute-start(f32[8,48,128]{2,1,0:T(8,128)S(1)} %get-tuple-element.28), channel_id=1, source_target_pairs={{0,32},{8,40},{16,48},{24,56},{32,64},{40,72},{48,80},{56,88},{64,... | collective-permute-start | bytes 589832 | tf_op jit(solution)/shard_map/ppermute | solution.py:506
  6.0 13.1 %collective-permute-start.3 = (f32[8,48,128]{2,1,0:T(8,128)S(1)}, f32[8,48,128]{2,1,0:T(8,128)S(1)}, u32[]{:S(2)}, u32[]{:S(2)}) collective-permute-start(f32[8,48,128]{2,1,0:T(8,128)S(1)} %get-tuple-element.29), channel_id=1, source_target_pairs={{0,64},{8,72},{16,80},{24,88},{32,96},{40,104},{48,112},{56,120},{... | collective-permute-start | bytes 589832 | tf_op jit(solution)/shard_map/ppermute | solution.py:506
  8.6 10.5 %collective-permute-start.4 = (f32[8,48,128]{2,1,0:T(8,128)S(1)}, f32[8,48,128]{2,1,0:T(8,128)S(1)}, u32[]{:S(2)}, u32[]{:S(2)}) collective-permute-start(f32[8,48,128]{2,1,0:T(8,128)S(1)} %get-tuple-element.30), channel_id=1, source_target_pairs={{0,96},{8,104},{16,112},{24,120},{32,0},{40,8},{48,16},{56,24},{64... | collective-permute-start | bytes 589832 | tf_op jit(solution)/shard_map/ppermute | solution.py:506
  9.7 8.0 %collective-permute-start = (f32[256,128]{1,0:T(8,128)S(1)}, f32[256,128]{1,0:T(8,128)S(1)}, u32[]{:S(2)}, u32[]{:S(2)}) collective-permute-start(f32[256,128]{1,0:T(8,128)S(1)} %get-tuple-element.22), channel_id=1, source_target_pairs={{0,8},{8,16},{16,24},{24,32},{32,40},{40,48},{48,56},{56,64},{64,7... | collective-permute-start | bytes 393224 | tf_op jit(solution)/shard_map/ppermute | solution.py:506
  13.2 5.9 %collective-permute-start.1 = (f32[256,128]{1,0:T(8,128)S(1)}, f32[256,128]{1,0:T(8,128)S(1)}, u32[]{:S(2)}, u32[]{:S(2)}) collective-permute-start(f32[256,128]{1,0:T(8,128)S(1)} %get-tuple-element.23), channel_id=1, source_target_pairs={{8,0},{16,8},{24,16},{32,24},{40,32},{48,40},{56,48},{64,56},{72,6... | collective-permute-start | bytes 393224 | tf_op jit(solution)/shard_map/ppermute | solution.py:506
  14.5 0.8 %copy-start.1 = (f32[128,128]{1,0:T(8,128)S(1)}, f32[128,128]{1,0:T(8,128)}, u32[]{:S(2)}) copy-start(f32[128,128]{1,0:T(8,128)} %refs_7_.1) | copy-start | bytes 196612
  15.4 0.9 %copy-start.4 = (f32[1,4,128,128]{3,2,1,0:T(8,128)S(1)}, f32[1,4,128,128]{3,2,1,0:T(8,128)}, u32[]{:S(2)}) copy-start(f32[1,4,128,128]{3,2,1,0:T(8,128)} %param.7) | copy-start | bytes 786436
  16.3 25.1 %copy-start.6 = (f32[128,128]{1,0:T(8,128)S(1)}, f32[128,128]{1,0:T(8,128)}, u32[]{:S(2)}) copy-start(f32[128,128]{1,0:T(8,128)} %refs_6_.1) | copy-start | bytes 196612
  19.9 16.9 %collective-permute-start.7 = (f32[7,48,128]{2,1,0:T(8,128)S(1)}, f32[7,48,128]{2,1,0:T(8,128)S(1)}, u32[]{:S(2)}, u32[]{:S(2)}) collective-permute-start(f32[7,48,128]{2,1,0:T(8,128)S(1)} %get-tuple-element.34), channel_id=1, source_target_pairs={{0,8},{8,16},{16,24},{24,0},{32,40},{40,48},{48,56},{56,32},{64,72... | collective-permute-start | bytes 516104 | tf_op jit(solution)/shard_map/ppermute | solution.py:506
  21.4 15.4 %collective-permute-start.8 = (f32[7,48,128]{2,1,0:T(8,128)S(1)}, f32[7,48,128]{2,1,0:T(8,128)S(1)}, u32[]{:S(2)}, u32[]{:S(2)}) collective-permute-start(f32[7,48,128]{2,1,0:T(8,128)S(1)} %get-tuple-element.35), channel_id=1, source_target_pairs={{0,16},{8,24},{16,0},{24,8},{32,48},{40,56},{48,32},{56,40},{64,80... | collective-permute-start | bytes 516104 | tf_op jit(solution)/shard_map/ppermute | solution.py:506
  25.2 11.6 %collective-permute-start.9 = (f32[7,48,128]{2,1,0:T(8,128)S(1)}, f32[7,48,128]{2,1,0:T(8,128)S(1)}, u32[]{:S(2)}, u32[]{:S(2)}) collective-permute-start(f32[7,48,128]{2,1,0:T(8,128)S(1)} %get-tuple-element.36), channel_id=1, source_target_pairs={{0,24},{8,0},{16,8},{24,16},{32,56},{40,32},{48,40},{56,48},{64,88... | collective-permute-start | bytes 516104 | tf_op jit(solution)/shard_map/ppermute | solution.py:506
  25.2 13.8 %collective-permute-start.5 = (f32[64,128]{1,0:T(8,128)S(1)}, f32[64,128]{1,0:T(8,128)S(1)}, u32[]{:S(2)}, u32[]{:S(2)}) collective-permute-start(f32[64,128]{1,0:T(8,128)S(1)} %get-tuple-element.31), channel_id=1, source_target_pairs={{0,1},{1,2},{2,3},{3,4},{4,5},{5,6},{6,7},{8,9},{9,10},{10,11},{11... | collective-permute-start | bytes 98312 | tf_op jit(solution)/shard_map/ppermute | solution.py:549
  31.9 9.5 %collective-permute-start.6 = (f32[64,128]{1,0:T(8,128)S(1)}, f32[64,128]{1,0:T(8,128)S(1)}, u32[]{:S(2)}, u32[]{:S(2)}) collective-permute-start(f32[64,128]{1,0:T(8,128)S(1)} %get-tuple-element.32), channel_id=1, source_target_pairs={{1,0},{2,1},{3,2},{4,3},{5,4},{6,5},{7,6},{9,8},{10,9},{11,10},{12... | collective-permute-start | bytes 98312 | tf_op jit(solution)/shard_map/ppermute | solution.py:550
  33.9 0.8 %copy-start.2 = (f32[128,128]{1,0:T(8,128)S(1)}, f32[128,128]{1,0:T(8,128)}, u32[]{:S(2)}) copy-start(f32[128,128]{1,0:T(8,128)} %refs_7_.1) | copy-start | bytes 196612
  37.5 10.7 %collective-permute-start.12 = (f32[7,48,128]{2,1,0:T(8,128)S(1)}, f32[7,48,128]{2,1,0:T(8,128)S(1)}, u32[]{:S(2)}, u32[]{:S(2)}) collective-permute-start(f32[7,48,128]{2,1,0:T(8,128)S(1)} %combine.1.refs_7_.refs_4_), channel_id=1, source_target_pairs={{0,96},{8,104},{16,112},{24,120},{32,0},{40,8},{48,16},{56,24},{64... | collective-permute-start | bytes 516104 | tf_op jit(solution)/shard_map/ppermute | solution.py:506
  37.6 10.6 %collective-permute-start.11 = (f32[7,48,128]{2,1,0:T(8,128)S(1)}, f32[7,48,128]{2,1,0:T(8,128)S(1)}, u32[]{:S(2)}, u32[]{:S(2)}) collective-permute-start(f32[7,48,128]{2,1,0:T(8,128)S(1)} %combine.1.refs_7_.refs_4_), channel_id=1, source_target_pairs={{0,64},{8,72},{16,80},{24,88},{32,96},{40,104},{48,112},{56,120},{... | collective-permute-start | bytes 516104 | tf_op jit(solution)/shard_map/ppermute | solution.py:506
  38.3 10.9 %collective-permute-start.10 = (f32[7,48,128]{2,1,0:T(8,128)S(1)}, f32[7,48,128]{2,1,0:T(8,128)S(1)}, u32[]{:S(2)}, u32[]{:S(2)}) collective-permute-start(f32[7,48,128]{2,1,0:T(8,128)S(1)} %combine.1.refs_7_.refs_4_), channel_id=1, source_target_pairs={{0,32},{8,40},{16,48},{24,56},{32,64},{40,72},{48,80},{56,88},{64,... | collective-permute-start | bytes 516104 | tf_op jit(solution)/shard_map/ppermute | solution.py:506
  39.0 12.7 %collective-permute-start.13 = (f32[3,128,128]{2,1,0:T(8,128)S(1)}, f32[3,128,128]{2,1,0:T(8,128)S(1)}, u32[]{:S(2)}, u32[]{:S(2)}) collective-permute-start(f32[3,128,128]{2,1,0:T(8,128)S(1)} %get-tuple-element.40), channel_id=1, source_target_pairs={{0,8},{8,16},{16,24},{24,32},{32,40},{40,48},{48,56},{56,64},{64,7... | collective-permute-start | bytes 589832 | tf_op jit(solution)/shard_map/ppermute | solution.py:506
  49.2 2.6 %copy-start.3 = (f32[128,128]{1,0:T(8,128)S(1)}, f32[128,128]{1,0:T(8,128)}, u32[]{:S(2)}) copy-start(f32[128,128]{1,0:T(8,128)} %refs_7_.1) | copy-start | bytes 196612
  49.2 2.6 %copy-start.5 = (f32[1,4,128,128]{3,2,1,0:T(8,128)S(1)}, f32[1,4,128,128]{3,2,1,0:T(8,128)}, u32[]{:S(2)}) copy-start(f32[1,4,128,128]{3,2,1,0:T(8,128)} %param.7) | copy-start | bytes 786436

commit v4 on v3

--- a/solution.py
+++ b/solution.py
@@ -109,12 +109,10 @@
         copy.wait()
 
 
-def pick_kernel(tile_rows, nest_rows, pos, fed, west, east, r0, r1, r2, r3, o0, o1, o2, o3, west_out, east_out):
+def pick_kernel(tile_rows, nest_rows, pos, fed, r0, r1, r2, r3, o0, o1, o2, o3):
     tile = lax.axis_index("tiles")
     my_y, my_z = lax.div(tile, jnp.int32(SIDE)), lax.rem(tile, jnp.int32(SIDE))
     first = third(pos[0, 0] + SIDE * nest_rows * my_y) - 1
-    west_out[...] = west[...]
-    east_out[...] = east[...]
     for k, out in enumerate((o0, o1, o2, o3)):
         target = my_y * SIDE + wrap(my_z + k)
         top = third(pos[0, 0] + nest_rows * target) - 1
@@ -126,7 +124,7 @@
             out[DEV_ROWS + s] = fed[s]
 
 
-def nest_kernel(tile_rows, tile_cols, pos, r0, r1, r2, r3, state, tail, nest_mix, courant, out, lines, start, cur):
+def nest_kernel(tile_rows, tile_cols, pos, r0, r1, r2, r3, state, tail, nest_mix, courant, out, token, lines, start, cur):
     tile = lax.axis_index("tiles")
     my_y, my_z = lax.div(tile, jnp.int32(SIDE)), lax.rem(tile, jnp.int32(SIDE))
     nest_rows, ncols, width = state.shape
@@ -178,18 +176,20 @@
             else:
                 cur[step, r] = value
         source = cur.at[step]
+    token[...] = jnp.zeros(token.shape, F32)
 
 
 def up_third(value):
     return third(value + 2)
 
 
-def feed_kernel(pos, state, nest_mix, courant, fb, tail, start, cur):
+def feed_kernel(pos, state, nest_mix, courant, fb, tail, mix_out, start, cur):
     tile = lax.axis_index("tiles")
     nest_rows, ncols, width = state.shape
     rows = nest_rows + STEPS
     ox, oy = pos[0, 0], pos[0, 1]
     tail[...] = state[nest_rows - STEPS :]
+    mix_out[...] = nest_mix[...]
     for x in range(rows):
         start[x] = 0.5 * state[x] if x < nest_rows else jnp.zeros((ncols, width), F32)
     above = jnp.where(tile == 0, start[0], 0.0)
@@ -401,11 +401,12 @@
 
 
 def parent_kernel(
-    rows, total, pos, parent, from_up, from_down, west, east, parent_mix, out, kept, token, done, weights, out_sems
+    rows, total, tiles, lines, pos, parent, from_up, from_down, west, east, parent_mix, out, kept, token, done, weights, out_sems
 ):
     height, cols = parent.shape[0], parent.shape[1]
     count, slots = height // rows, done.shape[0]
     owns, _, begin, aligned, _, _ = window(pos, height, cols, total)
+    tile, line = lax.axis_index("tiles"), lax.axis_index("nests")
 
     def store(i):
         slot = lax.rem(i, slots)
@@ -426,13 +427,17 @@
         for r in range(rows):
             at = i * rows + r
             value = parent[at]
-            upper = parent[at - 1] if r else jnp.where(i == 0, from_up[...], parent[jnp.maximum(at - 1, 0)])
+            upper = parent[at - 1] if r else jnp.where(i == 0, jnp.where(tile > 0, from_up[...], 0.0), parent[jnp.maximum(at - 1, 0)])
             if r < rows - 1:
                 lower = parent[at + 1]
             else:
-                lower = jnp.where(i == count - 1, from_down[...], parent[jnp.minimum(at + 1, height - 1)])
-            left = jnp.where(low_edge, west[pl.ds(at, 1), :], pltpu.roll(value, 1, 0))
-            right = jnp.where(high_edge, east[pl.ds(at, 1), :], pltpu.roll(value, cols - 1, 0))
+                lower = jnp.where(
+                    i == count - 1, jnp.where(tile < tiles - 1, from_down[...], 0.0), parent[jnp.minimum(at + 1, height - 1)]
+                )
+            left = jnp.where(low_edge, jnp.where(line > 0, west[pl.ds(at, 1), :], 0.0), pltpu.roll(value, 1, 0))
+            right = jnp.where(
+                high_edge, jnp.where(line < lines - 1, east[pl.ds(at, 1), :], 0.0), pltpu.roll(value, cols - 1, 0)
+            )
             done[slot, r] = mix(value, weights[...]) + KAPPA * ((upper + lower) + (left + right))
         store(i).start()
 
@@ -479,6 +484,10 @@
         name=name,
         **options,
     )(*[value for _, value in ins], *after)
+
+
+def around(count, step):
+    return [(i, (i + step) % count) for i in range(count)]
 
 
 def y_route(k):
@@ -522,14 +531,14 @@
     )
     b, (west_out, east_out, down_out, up_out) = packed[:4], packed[4:]
     got = {k: on_tiles(b[k], y_route(k)) for k in (1, 3, 2)}
-    from_up = on_tiles(down_out, [(i, i + 1) for i in range(count - 1)])
-    from_down = on_tiles(up_out, [(i + 1, i) for i in range(count - 1)])
-
-    fed, tail = run(
+    from_up = on_tiles(down_out, around(count, 1))
+    from_down = on_tiles(up_out, around(count, -1))
+
+    fed, tail, mix_kept = run(
         "feed",
         feed_kernel,
         [(S, nest_pos), (V, state), (V, nest_mix), (V, courant)],
-        [(V, f(FB_SLOTS, C, width)), (V, f(STEPS, ncols, width))],
+        [(V, f(FB_SLOTS, C, width)), (V, f(STEPS, ncols, width)), (V, f(width, width))],
         [
             pltpu.VMEM((nest_rows + STEPS, ncols, width), F32),
             pltpu.VMEM((STEPS - 1, nest_rows + STEPS, ncols, width), F32),
@@ -538,20 +547,24 @@
         flops=1 << 28,
         moved=4,
     )
+    east_out, west_out, _ = lax.optimization_barrier((east_out, west_out, fed))
+    west = lax.ppermute(east_out, "nests", around(lines, 1))
+    east = lax.ppermute(west_out, "nests", around(lines, -1))
     picked = run(
         "pick",
         functools.partial(pick_kernel, tile_rows, nest_rows),
-        [(S, nest_pos)] + [(V, x) for x in (fed, west_out, east_out, b[0], got[1], got[2], got[3])],
-        [(V, f(DEV_ROWS + FB_SLOTS, C, width))] * SIDE + [(V, f(tile_rows, width))] * 2,
-        after=[from_up, from_down],
+        [(S, nest_pos)] + [(V, x) for x in (fed, b[0], got[1], got[2], got[3])],
+        [(V, f(DEV_ROWS + FB_SLOTS, C, width))] * SIDE,
+        after=[from_down],
     )
     mine = {k: on_tiles(picked[k], z_route(k)) for k in (1, 3, 2)}
-    west = lax.ppermute(picked[5], "nests", [(i, i + 1) for i in range(lines - 1)])
-    east = lax.ppermute(picked[4], "nests", [(i + 1, i) for i in range(lines - 1)])
+    tail, _ = lax.optimization_barrier((tail, picked[1]))
+    tail_in = on_tiles(tail, around(count, 1))
+
     (own,) = run(
         "own_feed",
         functools.partial(own_kernel, tile_rows, tile_cols, total),
-        [(S, nest_pos), (H, parent), (V, from_up), (V, nest_mix), (V, courant)],
+        [(S, nest_pos), (H, parent), (V, from_up), (V, mix_kept), (V, courant)],
         [(V, f(FB_WINDOW, C, width))],
         [
             pltpu.VMEM((FB_WINDOW + 1, WIDE + 8, width), F32),
@@ -562,21 +575,10 @@
         flops=1 << 30,
         moved=8,
     )
-    (joined,) = run(
-        "combine",
-        functools.partial(combine_kernel, nest_rows),
-        [(S, nest_pos), (V, picked[0])] + [(V, mine[k]) for k in (1, 2, 3)],
-        [(V, f(FB_GROUP, C, width))],
-        after=[own],
-    )
-    groups = {k: on_tiles(joined, y_route(k)) for k in (1, 3, 2)}
-    tail, _ = lax.optimization_barrier((tail, joined))
-    tail_in = on_tiles(tail, [(i, i + 1) for i in range(count - 1)])
-
     rows = 8
     parent_new, kept, token = run(
         "parent_step",
-        functools.partial(parent_kernel, rows, total),
+        functools.partial(parent_kernel, rows, total, count, lines),
         [(S, nest_pos), (V, parent)] + [(V, x) for x in (from_up, from_down, west, east, parent_mix)],
         [(H, f(tile_rows, tile_cols, width)), (V, f(FB_WINDOW, WIDE, width)), (V, f(8, width))],
         [
@@ -584,24 +586,33 @@
             pltpu.VMEM((2 * width, 2 * width), BF16),
             pltpu.SemaphoreType.DMA((4,)),
         ],
-        after=[joined],
+        after=[own],
         room=mid,
         flops=2 * tile_rows * tile_cols * 256 * 256,
         moved=10,
     )
-    (nest_out,) = run(
+    (joined,) = run(
+        "combine",
+        functools.partial(combine_kernel, nest_rows),
+        [(S, nest_pos), (V, picked[0])] + [(V, mine[k]) for k in (1, 2, 3)],
+        [(V, f(FB_GROUP, C, width))],
+        after=[token],
+    )
+    groups = {k: on_tiles(joined, y_route(k)) for k in (1, 3, 2)}
+
+    nest_out, moved_on = run(
         "nest_steps",
         functools.partial(nest_kernel, tile_rows, tile_cols),
         [(S, nest_pos), (V, picked[0])]
         + [(V, mine[k]) for k in (1, 2, 3)]
-        + [(V, x) for x in (state, tail_in, nest_mix, courant)],
-        [(V, f(nest_rows, ncols, width))],
+        + [(V, x) for x in (state, tail_in, mix_kept, courant)],
+        [(V, f(nest_rows, ncols, width)), (V, f(8, width))],
         [
             pltpu.VMEM((DEV_ROWS, ncols, width), F32),
             pltpu.VMEM((nest_rows + STEPS, ncols, width), F32),
             pltpu.VMEM((STEPS - 1, nest_rows + STEPS, ncols, width), F32),
         ],
-        after=[token],
+        after=[joined],
         flops=1 << 28,
         moved=6,
     )

time: 54.3 us -> 50.3 us (0.926)
  the two profiles are of different devices: /device:TPU:1 before, /device:TPU:0 now
where the time goes in v4:
time: 50.3 us; the launch traced here: 49.9 us
  starting transfers between devices  23.9 us (48%)
  Pallas kernels  14.7 us (29%)
  waiting for transfers between devices  7.96 us (16%)
  local copies, waits for them, and re-layouts  2.61 us (5%)
  between operations  0.74 us (1%)
    ppermute x12, starting transfers between devices, on_tiles(): return lax.ppermute(block, 'tiles', route)  20.9 us
    pallas_call x8, Pallas kernels, run(): pl.pallas_call(body, out_shape=[shape for _, shape in outs], in_specs=[sp...  14.7 us
    ppermute x12, waiting for transfers between devices, on_tiles(): return lax.ppermute(block, 'tiles', route)  7.95 us
    ppermute x1, starting transfers between devices, shards(): east = lax.ppermute(west_out, 'nests', around(lines, -1))  2.95 us
    unnamed x14, local copies, waits for them, and re-layouts  2.61 us
  transfers between devices with their start and end apart: 14, of which 5 were waited for; matrix products, arithmetic and copies ran while one was open for 0% of the time, Pallas kernels for 23%

profile of v4, /device:TPU:0, one launch (start us, length us, event | category | flops | bytes accessed | tf_op | source)
XLA Modules:
  0.0 49.9 jit_solution(1051333088009164212)
XLA Ops:
  0.6 0.0 copy-start
  0.6 0.0 copy-start.4
  0.6 0.8 %copy-done.4 = s32[1,2]{1,0:T(1,128)S(1)} copy-done((s32[1,2]{1,0:T(1,128)S(1)}, s32[1,2]{1,0:T(1,128)}, u32[]{:S(2)}) %copy-start.4) | copy-done | bytes 32
  1.4 0.0 copy-start.5
  1.4 2.4 %pack.1 = (f32[8,48,128]{2,1,0:T(8,128)S(1)}, f32[8,48,128]{2,1,0:T(8,128)S(1)}, f32[8,48,128]{2,1,0:T(8,128)S(1)}, f32[8,48,128]{2,1,0:T(8,128)S(1)}, f32[64,12...) custom-call(s32[1,2]{1,0:T(1,128)S(1)} %copy-done.4, ...), custom_call_target="tpu_custom_call" | custom-call | bytes 4194304 | tf_op jit(solution)/shard_map/pack/pallas_call | solution.py:476
  3.9 1.7 %collective-permute-start.4 = (f32[8,48,128]{2,1,0:T(8,128)S(1)}, f32[8,48,128]{2,1,0:T(8,128)S(1)}, u32[]{:S(2)}, u32[]{:S(2)}) collective-permute-start(f32[8,48,128]{2,1,0:T(8,128)S(1)} %get-tuple-element.33), channel_id=1, source_target_pairs={{0,32},{8,40},{16,48},{24,56},{32,64},{40,72},{48,80},{56,88},{64,... | collective-permute-start | bytes 589832 | tf_op jit(solution)/shard_map/ppermute | solution.py:515
  5.6 2.9 %collective-permute-start.5 = (f32[8,48,128]{2,1,0:T(8,128)S(1)}, f32[8,48,128]{2,1,0:T(8,128)S(1)}, u32[]{:S(2)}, u32[]{:S(2)}) collective-permute-start(f32[8,48,128]{2,1,0:T(8,128)S(1)} %get-tuple-element.34), channel_id=1, source_target_pairs={{0,64},{8,72},{16,80},{24,88},{32,96},{40,104},{48,112},{56,120},{... | collective-permute-start | bytes 589832 | tf_op jit(solution)/shard_map/ppermute | solution.py:515
  8.5 1.3 %collective-permute-start.6 = (f32[8,48,128]{2,1,0:T(8,128)S(1)}, f32[8,48,128]{2,1,0:T(8,128)S(1)}, u32[]{:S(2)}, u32[]{:S(2)}) collective-permute-start(f32[8,48,128]{2,1,0:T(8,128)S(1)} %get-tuple-element.35), channel_id=1, source_target_pairs={{0,96},{8,104},{16,112},{24,120},{32,0},{40,8},{48,16},{56,24},{64... | collective-permute-start | bytes 589832 | tf_op jit(solution)/shard_map/ppermute | solution.py:515
  9.9 3.5 %collective-permute-start.1 = (f32[256,128]{1,0:T(8,128)S(1)}, f32[256,128]{1,0:T(8,128)S(1)}, u32[]{:S(2)}, u32[]{:S(2)}) collective-permute-start(f32[256,128]{1,0:T(8,128)S(1)} %get-tuple-element.25), channel_id=1, source_target_pairs={{0,120},{8,0},{16,8},{24,16},{32,24},{40,32},{48,40},{56,48},{64,5... | collective-permute-start | bytes 393224 | tf_op jit(solution)/shard_map/ppermute | solution.py:515
  13.3 0.0 collective-permute-start
  13.3 0.0 copy-done.5
  13.4 0.0 copy-start.1
  13.4 0.9 %copy-done.1 = f32[1,4,128,128]{3,2,1,0:T(8,128)S(1)} copy-done((f32[1,4,128,128]{3,2,1,0:T(8,128)S(1)}, f32[1,4,128,128]{3,2,1,0:T(8,128)}, u32[]{:S(2)}) %copy-start.1) | copy-done | bytes 262168
  14.3 0.0 copy-start.6
  14.3 0.8 %copy-done.6 = f32[128,128]{1,0:T(8,128)S(1)} copy-done((f32[128,128]{1,0:T(8,128)S(1)}, f32[128,128]{1,0:T(8,128)}, u32[]{:S(2)}) %copy-start.6) | copy-done | bytes 65560
  15.1 0.0 copy-start.3
  15.1 1.4 %feed.1 = (f32[3,48,128]{2,1,0:T(8,128)S(1)}, f32[3,128,128]{2,1,0:T(8,128)S(1)}, f32[128,128]{1,0:T(8,128)S(1)}) custom-call(s32[1,2]{1,0:T(1,128)S(1)} %copy-done.4, f32[4,128,128]{2,1,0:T(8,128)S(1)} %bitcast.2, f32[128,128]{1,0:T(8,128)S(1)} %copy-done.6, f32[2,128]{1,0:T(2,128)S(1)} %copy-done.5, f32[64,128]{1,0:T(8,128)S(1)} %get-tuple-element.30.refs_4_), custom_call_target="tpu_custom_call" | custom-call | flops 268435456 | bytes 4194304 | tf_op jit(solution)/shard_map/feed/pallas_call | solution.py:476
  16.5 2.0 %collective-permute-done.1.refs_6_.refs_3_ = f32[256,128]{1,0:T(8,128)S(1)} collective-permute-done((f32[256,128]{1,0:T(8,128)S(1)}, f32[256,128]{1,0:T(8,128)S(1)}, u32[]{:S(2)}, u32[]{:S(2)}) %collective-permute-start.1) | collective-permute-done | bytes 131104 | tf_op jit(solution)/shard_map/ppermute | solution.py:515
  18.5 0.0 collective-permute-start.2
  18.5 0.0 collective-permute-done.4.refs_3_
  18.5 3.0 %collective-permute-start.3 = (f32[64,128]{1,0:T(8,128)S(1)}, f32[64,128]{1,0:T(8,128)S(1)}, u32[]{:S(2)}, u32[]{:S(2)}) collective-permute-start(f32[64,128]{1,0:T(8,128)S(1)} %get-tuple-element.30.refs_4_), channel_id=1, source_target_pairs={{0,7},{1,0},{2,1},{3,2},{4,3},{5,4},{6,5},{7,6},{8,15},{9,8},{10,9... | collective-permute-start | bytes 98312 | tf_op jit(solution)/shard_map/ppermute | solution.py:552
  21.5 0.0 collective-permute-done.5.refs_4_
  21.5 0.0 collective-permute-done.6.refs_5_
  21.5 0.8 %pick.1 = (f32[7,48,128]{2,1,0:T(8,128)S(1)}, f32[7,48,128]{2,1,0:T(8,128)S(1)}, f32[7,48,128]{2,1,0:T(8,128)S(1)}, f32[7,48,128]{2,1,0:T(8,128)S(1)}) custom-call(s32[1,2]{1,0:T(1,128)S(1)} %copy-done.4, f32[3,48,128]{2,1,0:T(8,128)S(1)} %get-tuple-element.28.refs_1_, f32[8,48,128]{2,1,0:T(8,128)S(1)} %get-tuple-element.32.refs_2_, ...), custom_call_target="tpu_custom_call" | custom-call | bytes 1048576 | tf_op jit(solution)/shard_map/pick/pallas_call | solution.py:476
  22.2 0.1 collective-permute-start.7
  22.3 5.1 %collective-permute-start.8 = (f32[7,48,128]{2,1,0:T(8,128)S(1)}, f32[7,48,128]{2,1,0:T(8,128)S(1)}, u32[]{:S(2)}, u32[]{:S(2)}) collective-permute-start(f32[7,48,128]{2,1,0:T(8,128)S(1)} %get-tuple-element.40), channel_id=1, source_target_pairs={{0,16},{8,24},{16,0},{24,8},{32,48},{40,56},{48,32},{56,40},{64,80... | collective-permute-start | bytes 516104 | tf_op jit(solution)/shard_map/ppermute | solution.py:515
  27.5 0.0 collective-permute-done.refs_2_
  27.5 0.0 collective-permute-start.9
  27.5 0.0 copy-done
  27.5 0.0 copy-start.2
  27.5 0.6 %own_feed.1.refs_7_.refs_2_ = f32[22,48,128]{2,1,0:T(8,128)S(1)} custom-call(s32[1,2]{1,0:T(1,128)S(1)} %copy-done.4, f32[64,256,128]{2,1,0:T(8,128)S(1)} %copy-done, f32[256,128]{1,0:T(8,128)S(1)} %collective-permute-done.refs_2_, f32[128,128]{1,0:T(8,128)S(1)} %get-tuple-element.31.refs_3_.refs_7_, f32[2,128]{1,0:T(2,128)S(1)} %copy-done.5, ...), custom_call_target="tpu_custom_call" | custom-call | flops 1073741824 | bytes 8388608 | tf_op jit(solution)/shard_map/own_feed/pallas_call | solution.py:476
  28.1 0.0 collective-permute-done.2.refs_4_
  28.1 2.1 %collective-permute-start.13 = (f32[3,128,128]{2,1,0:T(8,128)S(1)}, f32[3,128,128]{2,1,0:T(8,128)S(1)}, u32[]{:S(2)}, u32[]{:S(2)}) collective-permute-start(f32[3,128,128]{2,1,0:T(8,128)S(1)} %get-tuple-element.44), channel_id=1, source_target_pairs={{0,8},{8,16},{16,24},{24,32},{32,40},{40,48},{48,56},{56,64},{64,7... | collective-permute-start | bytes 589832 | tf_op jit(solution)/shard_map/ppermute | solution.py:515
  30.2 0.0 collective-permute-done.3.refs_5_
  30.2 0.0 copy-done.3
  30.2 6.1 %parent_step.1 = (f32[64,256,128]{2,1,0:T(8,128)}, f32[22,56,128]{2,1,0:T(8,128)S(1)}, f32[8,128]{1,0:T(8,128)S(1)}) custom-call(s32[1,2]{1,0:T(1,128)S(1)} %copy-done.4, f32[64,256,128]{2,1,0:T(8,128)S(1)} %copy-done, f32[256,128]{1,0:T(8,128)S(1)} %collective-permute-done.refs_2_, f32[256,128]{1,0:T(8,128)S(1)} %collective-permute-done.1.refs_6_.refs_3_, ...), custom_call_target="tpu_custom_call" | custom-call | flops 2147483648 | bytes 10485760 | tf_op jit(solution)/shard_map/parent_step/pallas_call | solution.py:476
  36.3 1.2 %collective-permute-done.8.refs_3_ = f32[7,48,128]{2,1,0:T(8,128)S(1)} collective-permute-done((f32[7,48,128]{2,1,0:T(8,128)S(1)}, f32[7,48,128]{2,1,0:T(8,128)S(1)}, u32[]{:S(2)}, u32[]{:S(2)}) %collective-permute-start.8) | collective-permute-done | bytes 172064 | tf_op jit(solution)/shard_map/ppermute | solution.py:515
  37.5 0.0 collective-permute-done.9.refs_4_
  37.5 0.0 collective-permute-done.7.refs_2_
  37.5 0.7 %combine.1.refs_4_.refs_9_ = f32[7,48,128]{2,1,0:T(8,128)S(1)} custom-call(s32[1,2]{1,0:T(1,128)S(1)} %copy-done.4, f32[7,48,128]{2,1,0:T(8,128)S(1)} %get-tuple-element.36.refs_5_.refs_1_, f32[7,48,128]{2,1,0:T(8,128)S(1)} %collective-permute-done.7.refs_2_, f32[7,48,128]{2,1,0:T(8,128)S(1)} %collective-permute-done.8.refs_3_, ...), custom_call_target="tpu_custom_call" | custom-call | bytes 1048576 | tf_op jit(solution)/shard_map/combine/pallas_call | solution.py:476
  38.2 2.4 %collective-permute-start.12 = (f32[7,48,128]{2,1,0:T(8,128)S(1)}, f32[7,48,128]{2,1,0:T(8,128)S(1)}, u32[]{:S(2)}, u32[]{:S(2)}) collective-permute-start(f32[7,48,128]{2,1,0:T(8,128)S(1)} %combine.1.refs_4_.refs_9_), channel_id=1, source_target_pairs={{0,96},{8,104},{16,112},{24,120},{32,0},{40,8},{48,16},{56,24},{64... | collective-permute-start | bytes 516104 | tf_op jit(solution)/shard_map/ppermute | solution.py:515
  40.6 1.1 %collective-permute-start.11 = (f32[7,48,128]{2,1,0:T(8,128)S(1)}, f32[7,48,128]{2,1,0:T(8,128)S(1)}, u32[]{:S(2)}, u32[]{:S(2)}) collective-permute-start(f32[7,48,128]{2,1,0:T(8,128)S(1)} %combine.1.refs_4_.refs_9_), channel_id=1, source_target_pairs={{0,64},{8,72},{16,80},{24,88},{32,96},{40,104},{48,112},{56,120},{... | collective-permute-start | bytes 516104 | tf_op jit(solution)/shard_map/ppermute | solution.py:515
  41.7 0.7 %collective-permute-start.10 = (f32[7,48,128]{2,1,0:T(8,128)S(1)}, f32[7,48,128]{2,1,0:T(8,128)S(1)}, u32[]{:S(2)}, u32[]{:S(2)}) collective-permute-start(f32[7,48,128]{2,1,0:T(8,128)S(1)} %combine.1.refs_4_.refs_9_), channel_id=1, source_target_pairs={{0,32},{8,40},{16,48},{24,56},{32,64},{40,72},{48,80},{56,88},{64,... | collective-permute-start | bytes 516104 | tf_op jit(solution)/shard_map/ppermute | solution.py:515
  42.4 0.0 collective-permute-done.13.refs_6_
  42.4 0.0 copy-done.2
  42.4 2.2 %nest_steps.1 = (f32[4,128,128]{2,1,0:T(8,128)}, f32[8,128]{1,0:T(8,128)}) custom-call(s32[1,2]{1,0:T(1,128)S(1)} %copy-done.4, f32[7,48,128]{2,1,0:T(8,128)S(1)} %get-tuple-element.36.refs_5_.refs_1_, f32[7,48,128]{2,1,0:T(8,128)S(1)} %collective-permute-done.7.refs_2_, f32[7,48,128]{2,1,0:T(8,128)S(1)} %collective-permute-done.8.refs_3_, ...), custom_call_target="tpu_custom_call" | custom-call | flops 268435456 | bytes 6291456 | tf_op jit(solution)/shard_map/nest_steps/pallas_call | solution.py:476
  44.6 0.8 %collective-permute-done.12.refs_7_ = f32[7,48,128]{2,1,0:T(8,128)S(1)} collective-permute-done((f32[7,48,128]{2,1,0:T(8,128)S(1)}, f32[7,48,128]{2,1,0:T(8,128)S(1)}, u32[]{:S(2)}, u32[]{:S(2)}) %collective-permute-start.12) | collective-permute-done | bytes 172064 | tf_op jit(solution)/shard_map/ppermute | solution.py:515
  45.4 2.2 %collective-permute-done.11.refs_6_ = f32[7,48,128]{2,1,0:T(8,128)S(1)} collective-permute-done((f32[7,48,128]{2,1,0:T(8,128)S(1)}, f32[7,48,128]{2,1,0:T(8,128)S(1)}, u32[]{:S(2)}, u32[]{:S(2)}) %collective-permute-start.11) | collective-permute-done | bytes 172064 | tf_op jit(solution)/shard_map/ppermute | solution.py:515
  47.6 1.7 %collective-permute-done.10.refs_5_ = f32[7,48,128]{2,1,0:T(8,128)S(1)} collective-permute-done((f32[7,48,128]{2,1,0:T(8,128)S(1)}, f32[7,48,128]{2,1,0:T(8,128)S(1)}, u32[]{:S(2)}, u32[]{:S(2)}) %collective-permute-start.10) | collective-permute-done | bytes 172064 | tf_op jit(solution)/shard_map/ppermute | solution.py:515
  49.3 0.6 %patch.1 = f32[64,256,128]{2,1,0:T(8,128)} custom-call(s32[1,2]{1,0:T(1,128)S(1)} %copy-done.4, f32[64,256,128]{2,1,0:T(8,128)} %get-tuple-element.37.refs_1_, f32[22,48,128]{2,1,0:T(8,128)S(1)} %own_feed.1.refs_7_.refs_2_, f32[22,56,128]{2,1,0:T(8,128)S(1)} %get-tuple-element.38.refs_3_, ...), custom_call_target="tpu_custom_call", output_to_operand_aliasing={{}: (1, {})} | custom-call | bytes 2097152 | tf_op jit(solution)/shard_map/patch/pallas_call | solution.py:476
Async XLA Ops:
  0.6 26.9 %copy-start = (f32[64,256,128]{2,1,0:T(8,128)S(1)}, f32[64,256,128]{2,1,0:T(8,128)}, u32[]{:S(2)}) copy-start(f32[64,256,128]{2,1,0:T(8,128)} %refs_1_.5) | copy-start | bytes 25165828
  0.6 0.8 %copy-start.4 = (s32[1,2]{1,0:T(1,128)S(1)}, s32[1,2]{1,0:T(1,128)}, u32[]{:S(2)}) copy-start(s32[1,2]{1,0:T(1,128)} %refs_0_.15) | copy-start | bytes 28
  1.4 11.9 %copy-start.5 = (f32[2,128]{1,0:T(2,128)S(1)}, f32[2,128]{1,0:T(2,128)}, u32[]{:S(2)}) copy-start(f32[2,128]{1,0:T(2,128)} %refs_8_.1) | copy-start | bytes 3076
  3.9 14.6 %collective-permute-start.4 = (f32[8,48,128]{2,1,0:T(8,128)S(1)}, f32[8,48,128]{2,1,0:T(8,128)S(1)}, u32[]{:S(2)}, u32[]{:S(2)}) collective-permute-start(f32[8,48,128]{2,1,0:T(8,128)S(1)} %get-tuple-element.33), channel_id=1, source_target_pairs={{0,32},{8,40},{16,48},{24,56},{32,64},{40,72},{48,80},{56,88},{64,... | collective-permute-start | bytes 589832 | tf_op jit(solution)/shard_map/ppermute | solution.py:515
  5.6 15.9 %collective-permute-start.5 = (f32[8,48,128]{2,1,0:T(8,128)S(1)}, f32[8,48,128]{2,1,0:T(8,128)S(1)}, u32[]{:S(2)}, u32[]{:S(2)}) collective-permute-start(f32[8,48,128]{2,1,0:T(8,128)S(1)} %get-tuple-element.34), channel_id=1, source_target_pairs={{0,64},{8,72},{16,80},{24,88},{32,96},{40,104},{48,112},{56,120},{... | collective-permute-start | bytes 589832 | tf_op jit(solution)/shard_map/ppermute | solution.py:515
  8.5 13.0 %collective-permute-start.6 = (f32[8,48,128]{2,1,0:T(8,128)S(1)}, f32[8,48,128]{2,1,0:T(8,128)S(1)}, u32[]{:S(2)}, u32[]{:S(2)}) collective-permute-start(f32[8,48,128]{2,1,0:T(8,128)S(1)} %get-tuple-element.35), channel_id=1, source_target_pairs={{0,96},{8,104},{16,112},{24,120},{32,0},{40,8},{48,16},{56,24},{64... | collective-permute-start | bytes 589832 | tf_op jit(solution)/shard_map/ppermute | solution.py:515
  9.9 8.6 %collective-permute-start.1 = (f32[256,128]{1,0:T(8,128)S(1)}, f32[256,128]{1,0:T(8,128)S(1)}, u32[]{:S(2)}, u32[]{:S(2)}) collective-permute-start(f32[256,128]{1,0:T(8,128)S(1)} %get-tuple-element.25), channel_id=1, source_target_pairs={{0,120},{8,0},{16,8},{24,16},{32,24},{40,32},{48,40},{56,48},{64,5... | collective-permute-start | bytes 393224 | tf_op jit(solution)/shard_map/ppermute | solution.py:515
  13.3 14.1 %collective-permute-start = (f32[256,128]{1,0:T(8,128)S(1)}, f32[256,128]{1,0:T(8,128)S(1)}, u32[]{:S(2)}, u32[]{:S(2)}) collective-permute-start(f32[256,128]{1,0:T(8,128)S(1)} %get-tuple-element.24), channel_id=1, source_target_pairs={{0,8},{8,16},{16,24},{24,32},{32,40},{40,48},{48,56},{56,64},{64,7... | collective-permute-start | bytes 393224 | tf_op jit(solution)/shard_map/ppermute | solution.py:515
  13.4 1.0 %copy-start.1 = (f32[1,4,128,128]{3,2,1,0:T(8,128)S(1)}, f32[1,4,128,128]{3,2,1,0:T(8,128)}, u32[]{:S(2)}) copy-start(f32[1,4,128,128]{3,2,1,0:T(8,128)} %param.7) | copy-start | bytes 786436
  14.3 0.8 %copy-start.6 = (f32[128,128]{1,0:T(8,128)S(1)}, f32[128,128]{1,0:T(8,128)}, u32[]{:S(2)}) copy-start(f32[128,128]{1,0:T(8,128)} %refs_2_.1) | copy-start | bytes 196612
  15.1 15.0 %copy-start.3 = (f32[128,128]{1,0:T(8,128)S(1)}, f32[128,128]{1,0:T(8,128)}, u32[]{:S(2)}) copy-start(f32[128,128]{1,0:T(8,128)} %refs_6_.1) | copy-start | bytes 196612
  18.5 9.6 %collective-permute-start.2 = (f32[64,128]{1,0:T(8,128)S(1)}, f32[64,128]{1,0:T(8,128)S(1)}, u32[]{:S(2)}, u32[]{:S(2)}) collective-permute-start(f32[64,128]{1,0:T(8,128)S(1)} %get-tuple-element.29), channel_id=1, source_target_pairs={{0,1},{1,2},{2,3},{3,4},{4,5},{5,6},{6,7},{7,0},{8,9},{9,10},{10,1... | collective-permute-start | bytes 98312 | tf_op jit(solution)/shard_map/ppermute | solution.py:551
  18.5 11.7 %collective-permute-start.3 = (f32[64,128]{1,0:T(8,128)S(1)}, f32[64,128]{1,0:T(8,128)S(1)}, u32[]{:S(2)}, u32[]{:S(2)}) collective-permute-start(f32[64,128]{1,0:T(8,128)S(1)} %get-tuple-element.30.refs_4_), channel_id=1, source_target_pairs={{0,7},{1,0},{2,1},{3,2},{4,3},{5,4},{6,5},{7,6},{8,15},{9,8},{10,9... | collective-permute-start | bytes 98312 | tf_op jit(solution)/shard_map/ppermute | solution.py:552
  22.2 15.3 %collective-permute-start.7 = (f32[7,48,128]{2,1,0:T(8,128)S(1)}, f32[7,48,128]{2,1,0:T(8,128)S(1)}, u32[]{:S(2)}, u32[]{:S(2)}) collective-permute-start(f32[7,48,128]{2,1,0:T(8,128)S(1)} %get-tuple-element.39), channel_id=1, source_target_pairs={{0,8},{8,16},{16,24},{24,0},{32,40},{40,48},{48,56},{56,32},{64,72... | collective-permute-start | bytes 516104 | tf_op jit(solution)/shard_map/ppermute | solution.py:515
  22.3 15.2 %collective-permute-start.8 = (f32[7,48,128]{2,1,0:T(8,128)S(1)}, f32[7,48,128]{2,1,0:T(8,128)S(1)}, u32[]{:S(2)}, u32[]{:S(2)}) collective-permute-start(f32[7,48,128]{2,1,0:T(8,128)S(1)} %get-tuple-element.40), channel_id=1, source_target_pairs={{0,16},{8,24},{16,0},{24,8},{32,48},{40,56},{48,32},{56,40},{64,80... | collective-permute-start | bytes 516104 | tf_op jit(solution)/shard_map/ppermute | solution.py:515
  27.5 10.0 %collective-permute-start.9 = (f32[7,48,128]{2,1,0:T(8,128)S(1)}, f32[7,48,128]{2,1,0:T(8,128)S(1)}, u32[]{:S(2)}, u32[]{:S(2)}) collective-permute-start(f32[7,48,128]{2,1,0:T(8,128)S(1)} %get-tuple-element.41), channel_id=1, source_target_pairs={{0,24},{8,0},{16,8},{24,16},{32,56},{40,32},{48,40},{56,48},{64,88... | collective-permute-start | bytes 516104 | tf_op jit(solution)/shard_map/ppermute | solution.py:515
  27.5 14.9 %copy-start.2 = (f32[1,4,128,128]{3,2,1,0:T(8,128)S(1)}, f32[1,4,128,128]{3,2,1,0:T(8,128)}, u32[]{:S(2)}) copy-start(f32[1,4,128,128]{3,2,1,0:T(8,128)} %param.7) | copy-start | bytes 786436
  28.1 14.3 %collective-permute-start.13 = (f32[3,128,128]{2,1,0:T(8,128)S(1)}, f32[3,128,128]{2,1,0:T(8,128)S(1)}, u32[]{:S(2)}, u32[]{:S(2)}) collective-permute-start(f32[3,128,128]{2,1,0:T(8,128)S(1)} %get-tuple-element.44), channel_id=1, source_target_pairs={{0,8},{8,16},{16,24},{24,32},{32,40},{40,48},{48,56},{56,64},{64,7... | collective-permute-start | bytes 589832 | tf_op jit(solution)/shard_map/ppermute | solution.py:515
  38.2 7.2 %collective-permute-start.12 = (f32[7,48,128]{2,1,0:T(8,128)S(1)}, f32[7,48,128]{2,1,0:T(8,128)S(1)}, u32[]{:S(2)}, u32[]{:S(2)}) collective-permute-start(f32[7,48,128]{2,1,0:T(8,128)S(1)} %combine.1.refs_4_.refs_9_), channel_id=1, source_target_pairs={{0,96},{8,104},{16,112},{24,120},{32,0},{40,8},{48,16},{56,24},{64... | collective-permute-start | bytes 516104 | tf_op jit(solution)/shard_map/ppermute | solution.py:515
  40.6 7.0 %collective-permute-start.11 = (f32[7,48,128]{2,1,0:T(8,128)S(1)}, f32[7,48,128]{2,1,0:T(8,128)S(1)}, u32[]{:S(2)}, u32[]{:S(2)}) collective-permute-start(f32[7,48,128]{2,1,0:T(8,128)S(1)} %combine.1.refs_4_.refs_9_), channel_id=1, source_target_pairs={{0,64},{8,72},{16,80},{24,88},{32,96},{40,104},{48,112},{56,120},{... | collective-permute-start | bytes 516104 | tf_op jit(solution)/shard_map/ppermute | solution.py:515
  41.7 7.6 %collective-permute-start.10 = (f32[7,48,128]{2,1,0:T(8,128)S(1)}, f32[7,48,128]{2,1,0:T(8,128)S(1)}, u32[]{:S(2)}, u32[]{:S(2)}) collective-permute-start(f32[7,48,128]{2,1,0:T(8,128)S(1)} %combine.1.refs_4_.refs_9_), channel_id=1, source_target_pairs={{0,32},{8,40},{16,48},{24,56},{32,64},{40,72},{48,80},{56,88},{64,... | collective-permute-start | bytes 516104 | tf_op jit(solution)/shard_map/ppermute | solution.py:515
